TPU v7x, 128 devices: a whole 4x4x4 slice. The times are simulated.
128 devices in a mesh: seq: 8 (over y, core), vocab: 16 (over x, z).
Axes of the slice: x: 4, y: 4, z: 4, core: 2. Of those that a mesh axis runs over, the one named last changes fastest.
Arguments:
- queries: bfloat16 [8192, 2, 2048], P(('seq', 'vocab')), may hold values from -40 to 40
- key_vectors: bfloat16 [8192, 2, 2048], P(('seq', 'vocab')), may hold values from -40 to 40
- value_vectors: bfloat16 [8192, 2, 2048], P(('seq', 'vocab')), may hold values from -18 to 18
- residual: bfloat16 [8192, 2, 2048], P(('seq', 'vocab')), may hold values from -3 to 3
- norm_gain: float32 [2048], replicated, may hold values from 0.1 to 1.9
- head_weight: bfloat16 [2048, 16384], P(None, 'vocab'), may hold values from -0.125 to 0.125
- head_bias: float32 [16384], P('vocab'), may hold values from -6 to 6
- doc_lengths: int32 [2], replicated, may hold values from 1 to 8192, 12288 in all
Outputs:
- pooled: float32 [2, 16384], P(None, 'vocab')
- grad_hidden: bfloat16 [8192, 2, 2048], P(('seq', 'vocab'))
Inputs may be any that keep to these rules, and one draw needn't show every extreme that they name: `doc_lengths`: the lengths add up to 12288.
All inputs are finite; a program needn't handle non-finite values.
Results may differ from a plain program's by a relative error of at most 0.018.
Values may be sent and summed in bfloat16 or wider, within the bound.
No kernel may reach another device: no remote copies, remote signals or barrier semaphores. Data moves between devices by JAX's collectives and lax.ppermute only.
A program may use at most 128 MiB of HBM per device.

v0:
```python
import math

import jax
import jax.numpy as jnp
from jax import lax
from jax.experimental import pallas as pl
from jax.experimental.pallas import tpu as pltpu
from jax.sharding import Mesh
from jax.sharding import PartitionSpec as P


HEAD_DIM = 128
AXES = ("y", "c", "u", "w", "z")
PLANE = ("c", "u", "w", "z")
LOW = -1e30

sharpness = 8.0
flops_weight = 500.0
epsilon = 1e-05


def shift_perm(sizes, **by):
    steps = [by.get(axis, 0) for axis in AXES]
    pairs = []
    for source in range(math.prod(sizes)):
        rest, place = source, []
        for size in reversed(sizes):
            place.append(rest % size)
            rest //= size
        target = 0
        for size, at, step in zip(sizes, reversed(place), steps):
            target = target * size + (at + step) % size
        pairs.append((source, target))
    return pairs


def attention_kernel(first, last, turns, sub, lengths, q_ref, *refs):
    chunks = len(turns)
    keys = refs[: 2 * chunks : 2]
    values = refs[1 : 2 * chunks : 2]
    rest = list(refs[2 * chunks :])
    if not first:
        top_in, sum_in = rest.pop(0), rest.pop(0)
    if last:
        out_ref = rest.pop(0)
        top_ref, sum_ref = rest.pop(0), rest.pop(0)
    else:
        top_ref, sum_ref = rest.pop(0), rest.pop(0)
    wide = rest.pop(0)
    step = pl.program_id(0)
    rows = top_ref.shape[0]
    depth = wide.shape[1]
    scale = math.log2(math.e) / math.sqrt(HEAD_DIM)

    @pl.when(step == 0)
    def _():
        for n in range(chunks):
            wide[n, :, :HEAD_DIM] = values[n][...].reshape(depth, HEAD_DIM)
            wide[n, :, HEAD_DIM:] = jnp.ones((depth, HEAD_DIM), wide.dtype)

    if first:
        top_ref[...] = jnp.full_like(top_ref, LOW)
        sum_ref[...] = jnp.zeros_like(sum_ref)
    else:
        top_ref[...] = top_in[...]
        sum_ref[...] = sum_in[...]
    length = lengths[lax.axis_index("c")]
    y_at, y_size = lax.axis_index("y"), lax.axis_size("y")
    queries_real = length - y_at * depth > step * rows
    counts = [length - lax.rem(y_at + turn + y_size, y_size) * depth for turn in turns]

    def attend(n, masked):
        key = keys[n][...].reshape(depth, HEAD_DIM)

        def piece(index, _):
            at = pl.multiple_of(index * sub, sub)
            query = q_ref[pl.ds(index * (sub // 64), sub // 64)].reshape(sub, HEAD_DIM)
            scores = lax.dot_general(
                query, key, (((1,), (1,)), ((), ())), preferred_element_type=jnp.float32
            )
            if masked:
                place = lax.broadcasted_iota(jnp.int32, scores.shape, 1)
                scores = jnp.where(place < counts[n], scores, LOW)
            old_top = top_ref[pl.ds(at, sub), :]
            new_top = jnp.maximum(old_top, jnp.max(scores, axis=1, keepdims=True))
            weights = jnp.exp2((scores - new_top[:, :1]) * scale)
            shrink = jnp.exp2((old_top - new_top) * scale)
            added = jnp.dot(
                weights.astype(jnp.bfloat16), wide[n], preferred_element_type=jnp.float32
            )
            top_ref[pl.ds(at, sub), :] = new_top
            for part in range(0, 2 * HEAD_DIM, HEAD_DIM):
                cols = pl.ds(part, HEAD_DIM)
                sum_ref[pl.ds(at, sub), cols] = (
                    sum_ref[pl.ds(at, sub), cols] * shrink + added[:, part : part + HEAD_DIM]
                )
            return 0

        lax.fori_loop(0, rows // sub, piece, 0)

    for n in range(chunks):

        @pl.when(jnp.logical_and(queries_real, counts[n] >= depth))
        def _():
            attend(n, False)

        @pl.when(
            jnp.logical_and(
                queries_real, jnp.logical_and(counts[n] > 0, counts[n] < depth)
            )
        )
        def _():
            attend(n, True)

    if last:

        @pl.when(queries_real)
        def _():
            done = sum_ref[:, :HEAD_DIM] / sum_ref[:, HEAD_DIM:]
            out_ref[...] = done.astype(out_ref.dtype).reshape(out_ref.shape)

        @pl.when(jnp.logical_not(queries_real))
        def _():
            out_ref[...] = jnp.zeros_like(out_ref)


def attend_chunks(lengths, qkv, pairs, turns, carry, last, block=512, sub=256):
    sources, tokens = qkv.shape[0], qkv.shape[2]
    total = sources * tokens
    first = carry is None
    chunks = len(pairs) // 2

    def whole(array, part):
        if array.ndim == 4:
            return pl.BlockSpec(
                (sources, None, tokens, HEAD_DIM), lambda i, counts: (0, part, 0, 0)
            )
        return pl.BlockSpec((sources, tokens, HEAD_DIM), lambda i, counts: (0, 0, 0))

    in_specs = [
        pl.BlockSpec((block // tokens, None, tokens, HEAD_DIM), lambda i, counts: (i, 0, 0, 0))
    ]
    operands = [qkv]
    for array, part in pairs:
        in_specs.append(whole(array, part))
        operands.append(array)
    top_spec = pl.BlockSpec((block, HEAD_DIM), lambda i, counts: (i, 0))
    sum_spec = pl.BlockSpec((block, 2 * HEAD_DIM), lambda i, counts: (i, 0))
    if not first:
        in_specs += [top_spec, sum_spec]
        operands += list(carry)
    scratch = [pltpu.VMEM((chunks, total, 2 * HEAD_DIM), jnp.bfloat16)]
    if last:
        out_specs = pl.BlockSpec((block // tokens, tokens, HEAD_DIM), lambda i, counts: (i, 0, 0))
        out_shape = jax.ShapeDtypeStruct((sources, tokens, HEAD_DIM), jnp.bfloat16)
        scratch = [
            pltpu.VMEM((block, HEAD_DIM), jnp.float32),
            pltpu.VMEM((block, 2 * HEAD_DIM), jnp.float32),
        ] + scratch
    else:
        out_specs = [top_spec, sum_spec]
        out_shape = [
            jax.ShapeDtypeStruct((total, HEAD_DIM), jnp.float32),
            jax.ShapeDtypeStruct((total, 2 * HEAD_DIM), jnp.float32),
        ]

    def body(*refs):
        attention_kernel(first, last, turns, sub, *refs)

    return pl.pallas_call(
        body,
        grid_spec=pltpu.PrefetchScalarGridSpec(
            num_scalar_prefetch=1,
            grid=(total // block,),
            in_specs=in_specs,
            out_specs=out_specs,
            scratch_shapes=scratch,
        ),
        out_shape=out_shape,
        cost_estimate=pl.CostEstimate(
            flops=8 * total * total * HEAD_DIM * chunks,
            bytes_accessed=4 << 20,
            transcendentals=total * total * chunks,
        ),
        compiler_params=pltpu.CompilerParams(vmem_limit_bytes=24 << 20),
        name="attend_last" if last else ("attend_first" if first else "attend_next"),
    )(lengths, *operands)


def logits_kernel(blocks, tiles, places, lengths, own_hbm, near_hbm, far_hbm, bias_ref, *refs):
    rows_in = refs[:blocks]
    slope_ref, total_ref, rows_ref, held, sems = refs[blocks:]
    step = pl.program_id(0)
    steps = pl.num_programs(0)
    cols = held.shape[2]

    def fetch(at, slot):
        def start(source, first):
            where = pl.ds(pl.multiple_of((at - first) * cols, cols), cols)
            pltpu.make_async_copy(source.at[:, where], held.at[slot], sems.at[slot]).start()

        @pl.when(at < tiles[0])
        def _():
            start(own_hbm, 0)

        @pl.when(jnp.logical_and(at >= tiles[0], at < tiles[1]))
        def _():
            start(near_hbm, tiles[0])

        @pl.when(at >= tiles[1])
        def _():
            start(far_hbm, tiles[1])

    slot = lax.rem(step, 2)

    @pl.when(step == 0)
    def _():
        fetch(step, slot)

    @pl.when(step + 1 < steps)
    def _():
        fetch(step + 1, 1 - slot)

    @pl.when(step == 0)
    def _():
        at = 0
        for ref in rows_in:
            rows_ref[pl.ds(at, ref.shape[0]), :] = ref[...]
            at += ref.shape[0]

    pltpu.make_async_copy(own_hbm.at[:, pl.ds(0, cols)], held.at[slot], sems.at[slot]).wait()
    logits = jnp.dot(rows_ref[...], held[slot], preferred_element_type=jnp.float32) + bias_ref[...]
    tokens = 64
    y_at, c_at, u_at, w_at, z_at = [lax.axis_index(axis) for axis in AXES]
    _, c_size, u_size, w_size, z_size = [lax.axis_size(axis) for axis in AXES]
    sums = [jnp.zeros((1, cols), jnp.float32), jnp.zeros((1, cols), jnp.float32)]
    for part in range(rows_ref.shape[0] // tokens):
        piece = logits[part * tokens : (part + 1) * tokens]
        base = 1.0 + jnp.maximum(piece, 0.0)
        power2 = base * base
        power4 = power2 * power2
        place = lax.broadcasted_iota(jnp.int32, piece.shape, 0)
        w_by, z_by = places[part // 2]
        shard = (y_at * c_size + c_at) * u_size + u_at
        shard = shard * w_size + lax.rem(w_at + w_by, w_size)
        shard = shard * z_size + lax.rem(z_at + z_by + z_size, z_size)
        allowed = place < lengths[part % 2] - shard * tokens
        boosted = jnp.where(allowed, power4 * power4, 0.0)
        slope = jnp.where(
            jnp.logical_and(allowed, piece > 0.0), power4 * (power2 * base), 0.0
        )
        slope_ref[pl.ds(part * tokens, tokens), :] = slope
        sums[part % 2] = sums[part % 2] + jnp.sum(boosted, axis=0, keepdims=True)
    total_ref[0:1, :] = sums[0]
    total_ref[1:2, :] = sums[1]


def boost(lengths, weights, bias, blocks, places, cols=256):
    width = weights[0].shape[0]
    sizes = [w.shape[1] for w in weights]
    entries = sum(sizes)
    rows = sum(b.shape[0] for b in blocks)
    tiles = (sizes[0] // cols, (sizes[0] + sizes[1]) // cols)

    def body(*refs):
        logits_kernel(len(blocks), tiles, places, *refs)

    return pl.pallas_call(
        body,
        grid_spec=pltpu.PrefetchScalarGridSpec(
            num_scalar_prefetch=1,
            grid=(entries // cols,),
            in_specs=[pl.BlockSpec(memory_space=pltpu.HBM)] * 3
            + [pl.BlockSpec((1, cols), lambda j, counts: (0, j))]
            + [pl.BlockSpec(b.shape, lambda j, counts: (0, 0)) for b in blocks],
            out_specs=[
                pl.BlockSpec((rows, cols), lambda j, counts: (0, j)),
                pl.BlockSpec((2, cols), lambda j, counts: (0, j)),
            ],
            scratch_shapes=[
                pltpu.VMEM((rows, width), jnp.bfloat16),
                pltpu.VMEM((2, width, cols), jnp.bfloat16),
                pltpu.SemaphoreType.DMA((2,)),
            ],
        ),
        out_shape=[
            pltpu.HBM((rows, entries), jnp.float32),
            jax.ShapeDtypeStruct((2, entries), jnp.float32),
        ],
        cost_estimate=pl.CostEstimate(
            flops=4 * max(rows, 256) * width * entries,
            bytes_accessed=width * entries * 2 + rows * entries * 4,
            transcendentals=0,
        ),
        compiler_params=pltpu.CompilerParams(vmem_limit_bytes=20 << 20),
        name="boost",
    )(lengths, *weights, bias, *blocks)


def gradient_kernel(outs, slope_ref, coef_ref, own_ref, near_ref, far_ref, *refs):
    out_refs, slopes = refs[:outs], refs[outs]
    tokens = 64

    @pl.when(pl.program_id(0) == 0)
    def _():
        for part in range(slopes.shape[0] // tokens):
            where = pl.ds(part * tokens, tokens)
            doc = part % 2
            slopes[where, :] = (coef_ref[doc : doc + 1, :] * slope_ref[where, :]).astype(
                slopes.dtype
            )

    result = None
    at = 0
    for ref in (own_ref, near_ref, far_ref):
        term = lax.dot_general(
            slopes[:, at : at + ref.shape[1]],
            ref[...],
            (((1,), (1,)), ((), ())),
            preferred_element_type=jnp.float32,
        )
        result = term if result is None else result + term
        at += ref.shape[1]
    at = 0
    for ref in out_refs:
        ref[...] = result[at : at + ref.shape[0]].astype(ref.dtype)
        at += ref.shape[0]


def gradient(slope, coefficient, weights, split, cols=256):
    rows, entries = slope.shape
    width = weights[0].shape[0]

    def body(*refs):
        gradient_kernel(len(split), *refs)

    return pl.pallas_call(
        body,
        grid=(width // cols,),
        in_specs=[
            pl.BlockSpec((rows, entries), lambda j: (0, 0)),
            pl.BlockSpec((2, entries), lambda j: (0, 0)),
        ]
        + [pl.BlockSpec((cols, w.shape[1]), lambda j: (j, 0)) for w in weights],
        out_specs=[pl.BlockSpec((n, cols), lambda j: (0, j)) for n in split],
        out_shape=[jax.ShapeDtypeStruct((n, width), jnp.bfloat16) for n in split],
        scratch_shapes=[pltpu.VMEM((rows, entries), jnp.bfloat16)],
        cost_estimate=pl.CostEstimate(
            flops=4 * max(rows, 256) * width * entries,
            bytes_accessed=width * entries * 2 + rows * entries * 4,
            transcendentals=0,
        ),
        compiler_params=pltpu.CompilerParams(vmem_limit_bytes=20 << 20),
        name="gradient",
    )(
        slope, coefficient, *[pltpu.with_memory_space_constraint(w, pltpu.HBM) for w in weights]
    )


def norm_kernel(docs, heads, back_ref, residual_ref, gain_ref, out_ref):
    tokens = residual_ref.shape[1]
    for d in range(docs):
        pieces = []
        squares = jnp.zeros((tokens, 1), jnp.float32)
        for h in range(heads):
            cols = slice(h * HEAD_DIM, (h + 1) * HEAD_DIM)
            piece = residual_ref[d, :, cols].astype(jnp.float32) + back_ref[d * heads + h].astype(
                jnp.float32
            )
            pieces.append(piece)
            squares = squares + jnp.sum(piece * piece, axis=1, keepdims=True)
        inv_rms = lax.rsqrt(squares / (heads * HEAD_DIM) + epsilon)
        for h in range(heads):
            cols = slice(h * HEAD_DIM, (h + 1) * HEAD_DIM)
            out_ref[d * tokens : (d + 1) * tokens, cols] = (
                pieces[h] * inv_rms * gain_ref[:, cols]
            ).astype(out_ref.dtype)


def normalized(back, residual, gain):
    docs, tokens, width = residual.shape
    return pl.pallas_call(
        lambda *refs: norm_kernel(docs, width // HEAD_DIM, *refs),
        out_shape=jax.ShapeDtypeStruct((docs * tokens, width), jnp.bfloat16),
        cost_estimate=pl.CostEstimate(
            flops=8 * docs * tokens * width, bytes_accessed=6 * docs * tokens * width, transcendentals=0
        ),
        compiler_params=pltpu.CompilerParams(vmem_limit_bytes=16 << 20),
        name="normalized",
    )(back, residual, gain.reshape(1, width))


def add(*terms):
    return sum(t.astype(jnp.float32) for t in terms).astype(jnp.bfloat16)


def local(
    queries, key_vectors, value_vectors, residual, norm_gain, head_weight, head_bias, doc_lengths
):
    tokens, docs, width = queries.shape
    heads = width // HEAD_DIM
    sizes = [lax.axis_size(axis) for axis in AXES]
    y_size, c_size, u_size, _, _ = sizes
    _, c_at, u_at, _, _ = [lax.axis_index(axis) for axis in AXES]

    def by_head(array):
        return jnp.transpose(array.reshape(tokens, docs, heads, HEAD_DIM), (1, 2, 0, 3)).reshape(
            docs * heads, tokens, HEAD_DIM
        )

    def move(array, **by):
        return lax.ppermute(array, AXES, shift_perm(sizes, **by))

    stacked = jnp.stack([by_head(a) for a in (queries, key_vectors, value_vectors)], axis=1)
    qkv = lax.all_to_all(stacked, PLANE, split_axis=0, concat_axis=0, tiled=True)
    key_own, value_own = qkv[:, 1], qkv[:, 2]
    key_left = move(key_own, y=1)
    value_right = move(value_own, y=-1)
    value_left = move(value_own, y=1)
    key_right = move(key_own, y=-1)
    key_far = move(key_left, y=1)
    value_far = move(value_right, y=-1)

    entries = head_weight.shape[1]
    half = entries // 2
    near = move(lax.dynamic_slice_in_dim(head_weight, c_at * half, half, 1), u=1)
    far = move(near, c=1)
    weights = (head_weight, near, far)
    other_bias = move(head_bias.reshape(1, entries), u=1)

    def in_halves(array):
        swapped = jnp.concatenate([array[:, half:], array[:, :half]], axis=1)
        return jnp.where(c_at == 0, array, swapped)

    bias = jnp.concatenate([head_bias.reshape(1, entries), in_halves(other_bias)], axis=1)

    carry = attend_chunks(doc_lengths, qkv, [(qkv, 1), (qkv, 2)], [0], None, False)
    carry = attend_chunks(
        doc_lengths,
        qkv,
        [(key_left, 0), (value_left, 0), (key_right, 0), (value_right, 0)],
        [-1, 1],
        carry,
        False,
    )
    attended = attend_chunks(
        doc_lengths, qkv, [(key_far, 0), (value_far, 0)], [2], carry, True
    )
    back = lax.all_to_all(attended, PLANE, split_axis=0, concat_axis=0, tiled=True)
    inward = jnp.transpose(residual, (1, 0, 2))
    hidden = normalized(back, inward, norm_gain)

    rows = {(0, 0): hidden}
    rows[1, 0] = move(hidden, w=1)
    rows[0, -1] = move(hidden, z=1)
    rows[0, 1] = move(hidden, z=-1)
    rows[1, -1] = move(rows[0, -1], w=1)
    rows[0, 2] = move(rows[0, -1], z=1)
    rows[1, 1] = move(rows[1, 0], z=-1)
    far_first = move(rows[1, -1][:tokens], z=1)
    far_second = move(rows[1, 1][tokens:], z=-1)

    waves = [[(0, 0)], [(1, 0), (0, -1), (0, 1)], [(1, -1), (0, 2), (1, 1)], [(1, 2)]]
    slopes, sums = [], 0.0
    for wave in waves:
        blocks = [far_first, far_second] if wave == [(1, 2)] else [rows[at] for at in wave]
        slope, part = boost(doc_lengths, weights, bias, blocks, wave)
        slopes.append(slope)
        sums = sums + part

    own_sums, other_sums = sums[:, :entries], in_halves(sums[:, entries:])
    ordered = jnp.where(
        u_at == 0, jnp.stack([own_sums, other_sums]), jnp.stack([other_sums, own_sums])
    )
    peers = y_size * c_size * u_size
    spread = jnp.broadcast_to(ordered[None], (peers,) + ordered.shape)
    gathered = lax.all_to_all(spread, ("y", "c", "u"), split_axis=0, concat_axis=0, tiled=True)
    totals = jnp.sum(gathered, axis=0)
    pooled = jnp.log(totals / doc_lengths[None, :, None].astype(jnp.float32)) / sharpness
    coefficient = 2.0 * flops_weight / docs * jnp.mean(pooled, axis=1)[:, None, :] / totals
    own_pooled = jnp.where(u_at == 0, pooled[0], pooled[1])
    own_coef = jnp.where(u_at == 0, coefficient[0], coefficient[1])
    other_coef = in_halves(jnp.where(u_at == 0, coefficient[1], coefficient[0]))
    coef = jnp.concatenate([own_coef, other_coef], axis=1)

    block = docs * tokens

    def terms(number, split):
        return gradient(slopes[number], coef, weights, split)

    first, second = terms(3, [tokens, tokens])
    first = move(first, z=-1)
    second = move(second, z=1)
    left, across, right = terms(2, [block] * 3)
    across = move(across, z=-1)
    left = jnp.concatenate([add(left[:tokens], first), left[tokens:]])
    right = jnp.concatenate([right[:tokens], add(right[tokens:], second)])
    left = move(left, w=1)
    right = move(right, z=1)
    pair, before, after = terms(1, [block] * 3)
    after = move(after, z=1)
    pair = move(add(pair, right), w=1)
    before = move(add(before, left, across), z=-1)
    (own,) = terms(0, [block])
    result = add(own, pair, before, after)
    return (own_pooled, jnp.transpose(result.reshape(docs, tokens, width), (1, 0, 2)))


def solution(mesh):
    grid = Mesh(mesh.devices.reshape(4, 2, 2, 2, 4), AXES)
    rows = P(AXES, None, None)
    vocab = ("u", "w", "z")
    in_specs = (rows, rows, rows, rows, P(), P(None, vocab), P(vocab), P())
    out_specs = (P(None, vocab), rows)

    return jax.shard_map(local, mesh=grid, in_specs=in_specs, out_specs=out_specs, check_vma=False)
```

profile of v0, /device:TPU:0, one launch (start us, length us, event | category | flops | bytes accessed | tf_op | source)
XLA Modules:
  0.0 258.5 jit_solution(1019041603257839102)
XLA Ops:
  0.6 1.5 reshape.69
  2.1 0.2 copy.34
  2.3 0.3 reshape.70
  2.7 0.2 copy.35
  2.9 0.3 reshape.71
  3.2 0.2 copy.36
  3.5 1.3 pad_maximum_fusion
  4.8 8.3 %all-to-all-start = ((bf16[32,3,64,128]{3,2,1,0:T(8,128)(2,1)}), bf16[32,3,64,128]{3,2,1,0:T(8,128)(2,1)S(1)}, u32[]{:S(2)}, u32[]{:S(2)}) async-start(bf16[32,3,64,128]{3,2,1,0:T(8,128)(2,1)} %pad_maximum_fusion), calls=%async_computation | async-start | bytes 3145728 | tf_op jit(solution)/shard_map/all_to_all | solution.py:415
  13.1 3.1 %constant_dynamic-slice_fusion = bf16[2048,512]{1,0:T(8,128)(2,1)} fusion(bf16[2048,1024]{1,0:T(8,128)(2,1)} %refs_2_.7, s32[]{:T(128)S(6)} %select_n.60), kind=kLoop, calls=%fused_computation.28 | loop fusion | bytes 4194308 | tf_op jit(solution)/shard_map/dynamic_slice | solution.py:426
  16.1 3.3 %collective-permute-start = (bf16[2048,512]{1,0:T(8,128)(2,1)}, bf16[2048,512]{1,0:T(8,128)(2,1)}, u32[]{:S(2)}, u32[]{:S(2)}) collective-permute-start(bf16[2048,512]{1,0:T(8,128)(2,1)} %constant_dynamic-slice_fusion), channel_id=1, source_target_pairs={{0,8},{1,9},{2,10},{3,11},{4,12},{5,13},{6,14},{7,15},{8,0},{9,1},... | collective-permute-start | bytes 6291464 | tf_op jit(solution)/shard_map/ppermute | solution.py:412
  19.4 16.8 %all-to-all-done.refs_1_.refs_2_.refs_3_ = bf16[32,3,64,128]{3,2,1,0:T(8,128)(2,1)S(1)} async-done(((bf16[32,3,64,128]{3,2,1,0:T(8,128)(2,1)}), bf16[32,3,64,128]{3,2,1,0:T(8,128)(2,1)S(1)}, u32[]{:S(2)}, u32[]{:S(2)}) %all-to-all-start) | async-done | bytes 1572896 | tf_op jit(solution)/shard_map/all_to_all | solution.py:415
  36.4 1.6 collective-permute-start.3
  38.0 1.7 collective-permute-start.5
  39.7 0.4 collective-permute-start.7
  40.0 2.9 %collective-permute-start.8 = (bf16[32,64,128]{2,1,0:T(8,128)(2,1)S(1)}, bf16[32,64,128]{2,1,0:T(8,128)(2,1)S(1)}, u32[]{:S(2)}, u32[]{:S(2)}) collective-permute-start(bf16[32,64,128]{2,1,0:T(8,128)(2,1)S(1)} %get-tuple-element.45), channel_id=1, source_target_pairs={{0,96},{1,97},{2,98},{3,99},{4,100},{5,101},{6,102},{7,103},{8,104... | collective-permute-start | bytes 1572872 | tf_op jit(solution)/shard_map/ppermute | solution.py:412
  42.9 13.7 %attend_first.1 = (f32[2048,128]{1,0:T(8,128)S(1)}, f32[2048,256]{1,0:T(8,128)S(1)}) custom-call(s32[2]{0:T(128)S(1)} %copy-done.2, bf16[32,3,64,128]{3,2,1,0:T(8,128)(2,1)S(1)} %all-to-all-done.refs_1_.refs_2_.refs_3_, bf16[32,3,64,128]{3,2,1,0:T(8,128)(2,1)S(1)} %all-to-all-done.refs_1_.refs_2_.refs_3_, ...), custom_call_target="tpu_custom_call" | custom-call | flops 4294967296 | bytes 4194304 | tf_op jit(solution)/shard_map/attend_first/pallas_call | solution.py:170
  56.7 3.2 %collective-permute-start.6 = (bf16[32,64,128]{2,1,0:T(8,128)(2,1)S(1)}, bf16[32,64,128]{2,1,0:T(8,128)(2,1)S(1)}, u32[]{:S(2)}, u32[]{:S(2)}) collective-permute-start(bf16[32,64,128]{2,1,0:T(8,128)(2,1)S(1)} %collective-permute-done.5.refs_5_), channel_id=1, source_target_pairs={{0,96},{1,97},{2,98},{3,99},{4,100},{5,101},{6,102},{7,103},{8,104... | collective-permute-start | bytes 1572872 | tf_op jit(solution)/shard_map/ppermute | solution.py:412
  59.9 3.8 %collective-permute-done.7.refs_3_ = bf16[32,64,128]{2,1,0:T(8,128)(2,1)S(1)} collective-permute-done((bf16[32,64,128]{2,1,0:T(8,128)(2,1)S(1)}, bf16[32,64,128]{2,1,0:T(8,128)(2,1)S(1)}, u32[]{:S(2)}, u32[]{:S(2)}) %collective-permute-start.7) | collective-permute-done | bytes 524320 | tf_op jit(solution)/shard_map/ppermute | solution.py:412
  63.7 0.4 collective-permute-done.8.refs_4_
  64.0 26.5 %attend_next.1 = (f32[2048,128]{1,0:T(8,128)S(1)}, f32[2048,256]{1,0:T(8,128)S(1)}) custom-call(s32[2]{0:T(128)S(1)} %copy-done.2, bf16[32,3,64,128]{3,2,1,0:T(8,128)(2,1)S(1)} %all-to-all-done.refs_1_.refs_2_.refs_3_, bf16[32,64,128]{2,1,0:T(8,128)(2,1)S(1)} %collective-permute-done.3.refs_2_, bf16[32,64,128]{2,1,0:T(8,128)(2,1)S(1)} %collective-permute-done.7.refs_3_, ...), custom_call_target="tpu_custom_call" | custom-call | flops 8589934592 | bytes 4194304 | tf_op jit(solution)/shard_map/attend_next/pallas_call | solution.py:170
  90.7 14.4 %attend_last.1 = bf16[32,64,128]{2,1,0:T(8,128)(2,1)} custom-call(s32[2]{0:T(128)S(1)} %copy-done.2, bf16[32,3,64,128]{3,2,1,0:T(8,128)(2,1)S(1)} %all-to-all-done.refs_1_.refs_2_.refs_3_, bf16[32,64,128]{2,1,0:T(8,128)(2,1)S(1)} %collective-permute-done.4.refs_2_, bf16[32,64,128]{2,1,0:T(8,128)(2,1)S(1)} %collective-permute-done.6.refs_3_, ...), custom_call_target="tpu_custom_call" | custom-call | flops 4294967296 | bytes 4194304 | tf_op jit(solution)/shard_map/attend_last/pallas_call | solution.py:170
  105.2 4.9 %all-to-all-start.1 = ((bf16[32,64,128]{2,1,0:T(8,128)(2,1)}), bf16[32,64,128]{2,1,0:T(8,128)(2,1)S(1)}, u32[]{:S(2)}, u32[]{:S(2)}) async-start(bf16[32,64,128]{2,1,0:T(8,128)(2,1)} %attend_last.1), calls=%async_computation.1 | async-start | bytes 1048576 | tf_op jit(solution)/shard_map/all_to_all | solution.py:449
  110.1 0.2 copy.48
  110.2 11.8 %all-to-all-done.1.refs_0_ = bf16[32,64,128]{2,1,0:T(8,128)(2,1)S(1)} async-done(((bf16[32,64,128]{2,1,0:T(8,128)(2,1)}), bf16[32,64,128]{2,1,0:T(8,128)(2,1)S(1)}, u32[]{:S(2)}, u32[]{:S(2)}) %all-to-all-start.1) | async-done | bytes 524320 | tf_op jit(solution)/shard_map/all_to_all | solution.py:449
  122.0 0.4 normalized.1.refs_5_
  122.5 0.3 collective-permute-start.10
  122.8 0.6 collective-permute-start.9
  123.4 1.8 collective-permute-start.2
  125.2 3.1 %collective-permute-start.11 = (bf16[128,2048]{1,0:T(8,128)(2,1)S(1)}, bf16[128,2048]{1,0:T(8,128)(2,1)S(1)}, u32[]{:S(2)}, u32[]{:S(2)}) collective-permute-start(bf16[128,2048]{1,0:T(8,128)(2,1)S(1)} %normalized.1.refs_5_), channel_id=1, source_target_pairs={{0,3},{1,0},{2,1},{3,2},{4,7},{5,4},{6,5},{7,6},{8,11},{9,8},{10,9... | collective-permute-start | bytes 1572872 | tf_op jit(solution)/shard_map/ppermute | solution.py:412
  128.2 8.5 %collective-permute-done.10.refs_6_ = bf16[128,2048]{1,0:T(8,128)(2,1)S(1)} collective-permute-done((bf16[128,2048]{1,0:T(8,128)(2,1)S(1)}, bf16[128,2048]{1,0:T(8,128)(2,1)S(1)}, u32[]{:S(2)}, u32[]{:S(2)}) %collective-permute-start.10) | collective-permute-done | bytes 524320 | tf_op jit(solution)/shard_map/ppermute | solution.py:412
  136.8 1.0 collective-permute-start.12
  137.8 1.3 collective-permute-start.14
  139.1 0.8 collective-permute-start.13
  139.9 9.0 %collective-permute-done.12.refs_5_ = bf16[128,2048]{1,0:T(8,128)(2,1)S(1)} collective-permute-done((bf16[128,2048]{1,0:T(8,128)(2,1)S(1)}, bf16[128,2048]{1,0:T(8,128)(2,1)S(1)}, u32[]{:S(2)}, u32[]{:S(2)}) %collective-permute-start.12) | collective-permute-done | bytes 524320 | tf_op jit(solution)/shard_map/ppermute | solution.py:412
  149.0 0.8 collective-permute-start.15
  149.7 0.4 collective-permute-done.14.refs_7_
  150.1 3.8 %collective-permute-start.16 = (bf16[64,2048]{1,0:T(8,128)(2,1)S(1)}, bf16[64,2048]{1,0:T(8,128)(2,1)S(1)}, u32[]{:S(2)}, u32[]{:S(2)}) collective-permute-start(bf16[64,2048]{1,0:T(8,128)(2,1)S(1)} %slice.89), channel_id=1, source_target_pairs={{0,3},{1,0},{2,1},{3,2},{4,7},{5,4},{6,5},{7,6},{8,11},{9,8},{10,9... | collective-permute-start | bytes 786440 | tf_op jit(solution)/shard_map/ppermute | solution.py:412
  153.9 2.2 copy-done
  156.1 9.2 %boost.5 = (f32[384,2048]{1,0:T(8,128)}, f32[2,2048]{1,0:T(2,128)S(1)}) custom-call(s32[2]{0:T(128)S(1)} %copy-done.2, bf16[2048,1024]{1,0:T(8,128)(2,1)S(1)} %copy-done, bf16[2048,512]{1,0:T(8,128)(2,1)} %collective-permute-done.refs_2_.refs_3_, bf16[2048,512]{1,0:T(8,128)(2,1)} %collective-permute-done.1.refs_3_.refs_4_, ...), custom_call_target="tpu_custom_call" | custom-call | flops 6442450944 | bytes 11534336 | tf_op jit(solution)/shard_map/boost/pallas_call | solution.py:268
  165.3 9.2 %boost.6 = (f32[384,2048]{1,0:T(8,128)}, f32[2,2048]{1,0:T(2,128)S(1)}) custom-call(s32[2]{0:T(128)S(1)} %copy-done.2, bf16[2048,1024]{1,0:T(8,128)(2,1)S(1)} %copy-done, bf16[2048,512]{1,0:T(8,128)(2,1)} %collective-permute-done.refs_2_.refs_3_, bf16[2048,512]{1,0:T(8,128)(2,1)} %collective-permute-done.1.refs_3_.refs_4_, ...), custom_call_target="tpu_custom_call" | custom-call | flops 6442450944 | bytes 11534336 | tf_op jit(solution)/shard_map/boost/pallas_call | solution.py:268
  174.5 7.1 %boost.4 = (f32[128,2048]{1,0:T(8,128)}, f32[2,2048]{1,0:T(2,128)S(1)}) custom-call(s32[2]{0:T(128)S(1)} %copy-done.2, bf16[2048,1024]{1,0:T(8,128)(2,1)S(1)} %copy-done, bf16[2048,512]{1,0:T(8,128)(2,1)} %collective-permute-done.refs_2_.refs_3_, bf16[2048,512]{1,0:T(8,128)(2,1)} %collective-permute-done.1.refs_3_.refs_4_, ...), custom_call_target="tpu_custom_call" | custom-call | flops 4294967296 | bytes 9437184 | tf_op jit(solution)/shard_map/boost/pallas_call | solution.py:268
  181.7 7.1 %boost.7 = (f32[128,2048]{1,0:T(8,128)}, f32[2,2048]{1,0:T(2,128)S(1)}) custom-call(s32[2]{0:T(128)S(1)} %copy-done.2, bf16[2048,1024]{1,0:T(8,128)(2,1)S(1)} %copy-done, bf16[2048,512]{1,0:T(8,128)(2,1)} %collective-permute-done.refs_2_.refs_3_, bf16[2048,512]{1,0:T(8,128)(2,1)} %collective-permute-done.1.refs_3_.refs_4_, ...), custom_call_target="tpu_custom_call" | custom-call | flops 4294967296 | bytes 9437184 | tf_op jit(solution)/shard_map/boost/pallas_call | solution.py:268
  188.9 0.8 broadcast_in_dim.2
  189.7 4.5 %all-to-all-start.2 = ((f32[16,2,2,1024]{3,2,1,0:T(2,128)}), f32[16,2,2,1024]{3,2,1,0:T(2,128)S(1)}, u32[]{:S(2)}, u32[]{:S(2)}) async-start(f32[16,2,2,1024]{3,2,1,0:T(2,128)} %broadcast_in_dim.2), calls=%async_computation.2 | async-start | bytes 524288 | tf_op jit(solution)/shard_map/all_to_all | solution.py:477
  194.2 9.0 %all-to-all-done.2 = f32[16,2,2,1024]{3,2,1,0:T(2,128)S(1)} async-done(((f32[16,2,2,1024]{3,2,1,0:T(2,128)}), f32[16,2,2,1024]{3,2,1,0:T(2,128)S(1)}, u32[]{:S(2)}, u32[]{:S(2)}) %all-to-all-start.2) | async-done | bytes 262176 | tf_op jit(solution)/shard_map/all_to_all | solution.py:477
  203.3 0.1 fusion.2
  203.5 1.2 copy-done.4
  204.7 7.7 %gradient.7 = (bf16[64,2048]{1,0:T(8,128)(2,1)S(1)}, bf16[64,2048]{1,0:T(8,128)(2,1)S(1)}) custom-call(f32[128,2048]{1,0:T(8,128)S(1)} %copy-done.4, f32[2,2048]{1,0:T(2,128)S(1)} %pad_maximum_fusion.3.refs_1_, bf16[2048,1024]{1,0:T(8,128)(2,1)} %refs_2_.7, bf16[2048,512]{1,0:T(8,128)(2,1)} %collective-permute-done.refs_2_.refs_3_, ...), custom_call_target="tpu_custom_call" | custom-call | flops 4294967296 | bytes 9437184 | tf_op jit(solution)/shard_map/gradient/pallas_call | solution.py:337
  212.5 0.1 collective-permute-start.17
  212.6 8.4 %gradient.6 = (bf16[128,2048]{1,0:T(8,128)(2,1)S(1)}, bf16[128,2048]{1,0:T(8,128)(2,1)S(1)}, bf16[128,2048]{1,0:T(8,128)(2,1)S(1)}) custom-call(f32[384,2048]{1,0:T(8,128)S(1)} %copy-done.6, f32[2,2048]{1,0:T(2,128)S(1)} %pad_maximum_fusion.3.refs_1_, bf16[2048,1024]{1,0:T(8,128)(2,1)} %refs_2_.7, bf16[2048,512]{1,0:T(8,128)(2,1)} %collective-permute-done.refs_2_.refs_3_, ...), custom_call_target="tpu_custom_call" | custom-call | flops 6442450944 | bytes 11534336 | tf_op jit(solution)/shard_map/gradient/pallas_call | solution.py:337
  221.1 3.2 %collective-permute-start.20 = (bf16[64,2048]{1,0:T(8,128)(2,1)S(1)}, bf16[64,2048]{1,0:T(8,128)(2,1)S(1)}, u32[]{:S(2)}, u32[]{:S(2)}) collective-permute-start(bf16[64,2048]{1,0:T(8,128)(2,1)S(1)} %get-tuple-element.39), channel_id=1, source_target_pairs={{0,3},{1,0},{2,1},{3,2},{4,7},{5,4},{6,5},{7,6},{8,11},{9,8},{10,9... | collective-permute-start | bytes 786440 | tf_op jit(solution)/shard_map/ppermute | solution.py:412
  224.5 2.1 collective-permute-start.18
  226.6 4.4 %collective-permute-done.20 = bf16[64,2048]{1,0:T(8,128)(2,1)S(1)} collective-permute-done((bf16[64,2048]{1,0:T(8,128)(2,1)S(1)}, bf16[64,2048]{1,0:T(8,128)(2,1)S(1)}, u32[]{:S(2)}, u32[]{:S(2)}) %collective-permute-start.20) | collective-permute-done | bytes 262176 | tf_op jit(solution)/shard_map/ppermute | solution.py:412
  231.1 1.1 collective-permute-start.21
  232.2 8.4 %gradient.5 = (bf16[128,2048]{1,0:T(8,128)(2,1)S(1)}, bf16[128,2048]{1,0:T(8,128)(2,1)S(1)}, bf16[128,2048]{1,0:T(8,128)(2,1)S(1)}) custom-call(f32[384,2048]{1,0:T(8,128)S(1)} %copy-done.5, f32[2,2048]{1,0:T(2,128)S(1)} %pad_maximum_fusion.3.refs_1_, bf16[2048,1024]{1,0:T(8,128)(2,1)} %refs_2_.7, bf16[2048,512]{1,0:T(8,128)(2,1)} %collective-permute-done.refs_2_.refs_3_, ...), custom_call_target="tpu_custom_call" | custom-call | flops 6442450944 | bytes 11534336 | tf_op jit(solution)/shard_map/gradient/pallas_call | solution.py:337
  240.8 0.1 add_convert_fusion.2
  240.9 1.1 collective-permute-start.19
  242.0 2.6 %collective-permute-done.21 = bf16[128,2048]{1,0:T(8,128)(2,1)S(1)} collective-permute-done((bf16[128,2048]{1,0:T(8,128)(2,1)S(1)}, bf16[128,2048]{1,0:T(8,128)(2,1)S(1)}, u32[]{:S(2)}, u32[]{:S(2)}) %collective-permute-start.21) | collective-permute-done | bytes 524320 | tf_op jit(solution)/shard_map/ppermute | solution.py:412
  244.6 0.2 add_convert_fusion.1
  244.9 3.8 %collective-permute-start.23 = (bf16[128,2048]{1,0:T(8,128)(2,1)S(1)}, bf16[128,2048]{1,0:T(8,128)(2,1)S(1)}, u32[]{:S(2)}, u32[]{:S(2)}) collective-permute-start(bf16[128,2048]{1,0:T(8,128)(2,1)S(1)} %add_convert_fusion.1), channel_id=1, source_target_pairs={{0,3},{1,0},{2,1},{3,2},{4,7},{5,4},{6,5},{7,6},{8,11},{9,8},{10,9... | collective-permute-start | bytes 1572872 | tf_op jit(solution)/shard_map/ppermute | solution.py:412
  248.6 0.6 fusion
  249.2 7.6 %gradient.4 = bf16[128,2048]{1,0:T(8,128)(2,1)S(1)} custom-call(f32[128,2048]{1,0:T(8,128)S(1)} %copy-done.3, f32[2,2048]{1,0:T(2,128)S(1)} %pad_maximum_fusion.3.refs_1_, bf16[2048,1024]{1,0:T(8,128)(2,1)} %refs_2_.7, bf16[2048,512]{1,0:T(8,128)(2,1)} %collective-permute-done.refs_2_.refs_3_, bf16[2048,512]{1,0:T(8,128)(2,1)} %collective-permute-done.1.refs_3_.refs_4_), custom_call_target="tpu_custom_call" | custom-call | flops 4294967296 | bytes 9437184 | tf_op jit(solution)/shard_map/gradient/pallas_call | solution.py:337
  256.8 0.3 add_convert_fusion
  257.2 1.3 copy.47
  (66 shorter events, 1.0 us)
Async XLA Ops:
  0.6 1.7 copy-start.7
  0.6 2.3 copy-start.8
  4.8 31.5 %all-to-all-start = ((bf16[32,3,64,128]{3,2,1,0:T(8,128)(2,1)}), bf16[32,3,64,128]{3,2,1,0:T(8,128)(2,1)S(1)}, u32[]{:S(2)}, u32[]{:S(2)}) async-start(bf16[32,3,64,128]{3,2,1,0:T(8,128)(2,1)} %pad_maximum_fusion), calls=%async_computation | async-start | bytes 3145728 | tf_op jit(solution)/shard_map/all_to_all | solution.py:415
  16.1 26.8 %copy-start.2 = (s32[2]{0:T(128)S(1)}, s32[2]{0:T(128)}, u32[]{:S(2)}) copy-start(s32[2]{0:T(128)} %refs_0_.13) | copy-start | bytes 28
  16.1 74.4 %collective-permute-start = (bf16[2048,512]{1,0:T(8,128)(2,1)}, bf16[2048,512]{1,0:T(8,128)(2,1)}, u32[]{:S(2)}, u32[]{:S(2)}) collective-permute-start(bf16[2048,512]{1,0:T(8,128)(2,1)} %constant_dynamic-slice_fusion), channel_id=1, source_target_pairs={{0,8},{1,9},{2,10},{3,11},{4,12},{5,13},{6,14},{7,15},{8,0},{9,1},... | collective-permute-start | bytes 6291464 | tf_op jit(solution)/shard_map/ppermute | solution.py:412
  36.4 20.2 %collective-permute-start.3 = (bf16[32,64,128]{2,1,0:T(8,128)(2,1)S(1)}, bf16[32,64,128]{2,1,0:T(8,128)(2,1)S(1)}, u32[]{:S(2)}, u32[]{:S(2)}) collective-permute-start(bf16[32,64,128]{2,1,0:T(8,128)(2,1)S(1)} %get-tuple-element.45), channel_id=1, source_target_pairs={{0,32},{1,33},{2,34},{3,35},{4,36},{5,37},{6,38},{7,39},{8,40},{9,... | collective-permute-start | bytes 1572872 | tf_op jit(solution)/shard_map/ppermute | solution.py:412
  38.0 18.7 %collective-permute-start.5 = (bf16[32,64,128]{2,1,0:T(8,128)(2,1)S(1)}, bf16[32,64,128]{2,1,0:T(8,128)(2,1)S(1)}, u32[]{:S(2)}, u32[]{:S(2)}) collective-permute-start(bf16[32,64,128]{2,1,0:T(8,128)(2,1)S(1)} %get-tuple-element.44), channel_id=1, source_target_pairs={{0,96},{1,97},{2,98},{3,99},{4,100},{5,101},{6,102},{7,103},{8,104... | collective-permute-start | bytes 1572872 | tf_op jit(solution)/shard_map/ppermute | solution.py:412
  39.7 24.0 %collective-permute-start.7 = (bf16[32,64,128]{2,1,0:T(8,128)(2,1)S(1)}, bf16[32,64,128]{2,1,0:T(8,128)(2,1)S(1)}, u32[]{:S(2)}, u32[]{:S(2)}) collective-permute-start(bf16[32,64,128]{2,1,0:T(8,128)(2,1)S(1)} %get-tuple-element.44), channel_id=1, source_target_pairs={{0,32},{1,33},{2,34},{3,35},{4,36},{5,37},{6,38},{7,39},{8,40},{9,... | collective-permute-start | bytes 1572872 | tf_op jit(solution)/shard_map/ppermute | solution.py:412
  40.0 24.0 %collective-permute-start.8 = (bf16[32,64,128]{2,1,0:T(8,128)(2,1)S(1)}, bf16[32,64,128]{2,1,0:T(8,128)(2,1)S(1)}, u32[]{:S(2)}, u32[]{:S(2)}) collective-permute-start(bf16[32,64,128]{2,1,0:T(8,128)(2,1)S(1)} %get-tuple-element.45), channel_id=1, source_target_pairs={{0,96},{1,97},{2,98},{3,99},{4,100},{5,101},{6,102},{7,103},{8,104... | collective-permute-start | bytes 1572872 | tf_op jit(solution)/shard_map/ppermute | solution.py:412
  56.6 34.1 %collective-permute-start.4 = (bf16[32,64,128]{2,1,0:T(8,128)(2,1)S(1)}, bf16[32,64,128]{2,1,0:T(8,128)(2,1)S(1)}, u32[]{:S(2)}, u32[]{:S(2)}) collective-permute-start(bf16[32,64,128]{2,1,0:T(8,128)(2,1)S(1)} %collective-permute-done.3.refs_2_), channel_id=1, source_target_pairs={{0,32},{1,33},{2,34},{3,35},{4,36},{5,37},{6,38},{7,39},{8,40},{9,... | collective-permute-start | bytes 1572872 | tf_op jit(solution)/shard_map/ppermute | solution.py:412
  56.7 34.0 %collective-permute-start.6 = (bf16[32,64,128]{2,1,0:T(8,128)(2,1)S(1)}, bf16[32,64,128]{2,1,0:T(8,128)(2,1)S(1)}, u32[]{:S(2)}, u32[]{:S(2)}) collective-permute-start(bf16[32,64,128]{2,1,0:T(8,128)(2,1)S(1)} %collective-permute-done.5.refs_5_), channel_id=1, source_target_pairs={{0,96},{1,97},{2,98},{3,99},{4,100},{5,101},{6,102},{7,103},{8,104... | collective-permute-start | bytes 1572872 | tf_op jit(solution)/shard_map/ppermute | solution.py:412
  90.6 63.3 %collective-permute-start.1 = (bf16[2048,512]{1,0:T(8,128)(2,1)}, bf16[2048,512]{1,0:T(8,128)(2,1)}, u32[]{:S(2)}, u32[]{:S(2)}) collective-permute-start(bf16[2048,512]{1,0:T(8,128)(2,1)} %collective-permute-done.refs_2_.refs_3_), channel_id=1, source_target_pairs={{0,16},{1,17},{2,18},{3,19},{4,20},{5,21},{6,22},{7,23},{8,24},{9,... | collective-permute-start | bytes 6291464 | tf_op jit(solution)/shard_map/ppermute | solution.py:412
  90.7 19.3 %copy-start.9 = (bf16[64,2,2048]{2,1,0:T(2,128)(2,1)S(1)}, bf16[64,2,2048]{2,1,0:T(2,128)(2,1)}, u32[]{:S(2)}) copy-start(bf16[64,2,2048]{2,1,0:T(2,128)(2,1)} %param.11) | copy-start | bytes 1572868
  105.2 16.9 %copy-start.1 = (f32[2048]{0:T(1024)S(1)}, f32[2048]{0:T(1024)}, u32[]{:S(2)}) copy-start(f32[2048]{0:T(1024)} %param.12) | copy-start | bytes 24580
  105.2 18.2 %copy-start.10 = (f32[1024]{0:T(1024)S(1)}, f32[1024]{0:T(1024)}, u32[]{:S(2)}) copy-start(f32[1024]{0:T(1024)} %param.14) | copy-start | bytes 12292
  105.2 16.9 %all-to-all-start.1 = ((bf16[32,64,128]{2,1,0:T(8,128)(2,1)}), bf16[32,64,128]{2,1,0:T(8,128)(2,1)S(1)}, u32[]{:S(2)}, u32[]{:S(2)}) async-start(bf16[32,64,128]{2,1,0:T(8,128)(2,1)} %attend_last.1), calls=%async_computation.1 | async-start | bytes 1048576 | tf_op jit(solution)/shard_map/all_to_all | solution.py:449
  122.5 14.3 %collective-permute-start.10 = (bf16[128,2048]{1,0:T(8,128)(2,1)S(1)}, bf16[128,2048]{1,0:T(8,128)(2,1)S(1)}, u32[]{:S(2)}, u32[]{:S(2)}) collective-permute-start(bf16[128,2048]{1,0:T(8,128)(2,1)S(1)} %normalized.1.refs_5_), channel_id=1, source_target_pairs={{0,1},{1,2},{2,3},{3,0},{4,5},{5,6},{6,7},{7,4},{8,9},{9,10},{10,1... | collective-permute-start | bytes 1572872 | tf_op jit(solution)/shard_map/ppermute | solution.py:412
  122.8 15.0 %collective-permute-start.9 = (bf16[128,2048]{1,0:T(8,128)(2,1)S(1)}, bf16[128,2048]{1,0:T(8,128)(2,1)S(1)}, u32[]{:S(2)}, u32[]{:S(2)}) collective-permute-start(bf16[128,2048]{1,0:T(8,128)(2,1)S(1)} %normalized.1.refs_5_), channel_id=1, source_target_pairs={{0,4},{1,5},{2,6},{3,7},{4,0},{5,1},{6,2},{7,3},{8,12},{9,13},{10,... | collective-permute-start | bytes 1572872 | tf_op jit(solution)/shard_map/ppermute | solution.py:412
  123.4 15.7 %collective-permute-start.2 = (f32[1,1024]{1,0:T(1,128)S(1)}, f32[1,1024]{1,0:T(1,128)S(1)}, u32[]{:S(2)}, u32[]{:S(2)}) collective-permute-start(f32[1,1024]{1,0:T(1,128)S(1)} %bitcast.43), channel_id=1, source_target_pairs={{0,8},{1,9},{2,10},{3,11},{4,12},{5,13},{6,14},{7,15},{8,0},{9,1},... | collective-permute-start | bytes 12296 | tf_op jit(solution)/shard_map/ppermute | solution.py:412
  125.2 28.7 %collective-permute-start.11 = (bf16[128,2048]{1,0:T(8,128)(2,1)S(1)}, bf16[128,2048]{1,0:T(8,128)(2,1)S(1)}, u32[]{:S(2)}, u32[]{:S(2)}) collective-permute-start(bf16[128,2048]{1,0:T(8,128)(2,1)S(1)} %normalized.1.refs_5_), channel_id=1, source_target_pairs={{0,3},{1,0},{2,1},{3,2},{4,7},{5,4},{6,5},{7,6},{8,11},{9,8},{10,9... | collective-permute-start | bytes 1572872 | tf_op jit(solution)/shard_map/ppermute | solution.py:412
  136.8 12.2 %collective-permute-start.12 = (bf16[128,2048]{1,0:T(8,128)(2,1)S(1)}, bf16[128,2048]{1,0:T(8,128)(2,1)S(1)}, u32[]{:S(2)}, u32[]{:S(2)}) collective-permute-start(bf16[128,2048]{1,0:T(8,128)(2,1)S(1)} %collective-permute-done.10.refs_6_), channel_id=1, source_target_pairs={{0,4},{1,5},{2,6},{3,7},{4,0},{5,1},{6,2},{7,3},{8,12},{9,13},{10,... | collective-permute-start | bytes 1572872 | tf_op jit(solution)/shard_map/ppermute | solution.py:412
  137.8 12.3 %collective-permute-start.14 = (bf16[128,2048]{1,0:T(8,128)(2,1)S(1)}, bf16[128,2048]{1,0:T(8,128)(2,1)S(1)}, u32[]{:S(2)}, u32[]{:S(2)}) collective-permute-start(bf16[128,2048]{1,0:T(8,128)(2,1)S(1)} %collective-permute-done.9.refs_5_), channel_id=1, source_target_pairs={{0,3},{1,0},{2,1},{3,2},{4,7},{5,4},{6,5},{7,6},{8,11},{9,8},{10,9... | collective-permute-start | bytes 1572872 | tf_op jit(solution)/shard_map/ppermute | solution.py:412
  139.1 26.2 %collective-permute-start.13 = (bf16[128,2048]{1,0:T(8,128)(2,1)S(1)}, bf16[128,2048]{1,0:T(8,128)(2,1)S(1)}, u32[]{:S(2)}, u32[]{:S(2)}) collective-permute-start(bf16[128,2048]{1,0:T(8,128)(2,1)S(1)} %collective-permute-done.10.refs_6_), channel_id=1, source_target_pairs={{0,1},{1,2},{2,3},{3,0},{4,5},{5,6},{6,7},{7,4},{8,9},{9,10},{10,1... | collective-permute-start | bytes 1572872 | tf_op jit(solution)/shard_map/ppermute | solution.py:412
  149.0 32.7 %collective-permute-start.15 = (bf16[64,2048]{1,0:T(8,128)(2,1)S(1)}, bf16[64,2048]{1,0:T(8,128)(2,1)S(1)}, u32[]{:S(2)}, u32[]{:S(2)}) collective-permute-start(bf16[64,2048]{1,0:T(8,128)(2,1)S(1)} %slice.88), channel_id=1, source_target_pairs={{0,1},{1,2},{2,3},{3,0},{4,5},{5,6},{6,7},{7,4},{8,9},{9,10},{10,1... | collective-permute-start | bytes 786440 | tf_op jit(solution)/shard_map/ppermute | solution.py:412
  150.1 31.5 %collective-permute-start.16 = (bf16[64,2048]{1,0:T(8,128)(2,1)S(1)}, bf16[64,2048]{1,0:T(8,128)(2,1)S(1)}, u32[]{:S(2)}, u32[]{:S(2)}) collective-permute-start(bf16[64,2048]{1,0:T(8,128)(2,1)S(1)} %slice.89), channel_id=1, source_target_pairs={{0,3},{1,0},{2,1},{3,2},{4,7},{5,4},{6,5},{7,6},{8,11},{9,8},{10,9... | collective-permute-start | bytes 786440 | tf_op jit(solution)/shard_map/ppermute | solution.py:412
  153.9 2.2 copy-start
  189.7 13.5 %all-to-all-start.2 = ((f32[16,2,2,1024]{3,2,1,0:T(2,128)}), f32[16,2,2,1024]{3,2,1,0:T(2,128)S(1)}, u32[]{:S(2)}, u32[]{:S(2)}) async-start(f32[16,2,2,1024]{3,2,1,0:T(2,128)} %broadcast_in_dim.2), calls=%async_computation.2 | async-start | bytes 524288 | tf_op jit(solution)/shard_map/all_to_all | solution.py:477
  203.5 1.2 copy-start.4
  204.7 7.9 %copy-start.6 = (f32[384,2048]{1,0:T(8,128)S(1)}, f32[384,2048]{1,0:T(8,128)}, u32[]{:S(2)}) copy-start(f32[384,2048]{1,0:T(8,128)} %get-tuple-element.33.refs_0_) | copy-start | bytes 9437188
  212.5 11.9 %collective-permute-start.17 = (bf16[64,2048]{1,0:T(8,128)(2,1)S(1)}, bf16[64,2048]{1,0:T(8,128)(2,1)S(1)}, u32[]{:S(2)}, u32[]{:S(2)}) collective-permute-start(bf16[64,2048]{1,0:T(8,128)(2,1)S(1)} %get-tuple-element.36), channel_id=1, source_target_pairs={{0,1},{1,2},{2,3},{3,0},{4,5},{5,6},{6,7},{7,4},{8,9},{9,10},{10,1... | collective-permute-start | bytes 786440 | tf_op jit(solution)/shard_map/ppermute | solution.py:412
  221.1 9.9 %collective-permute-start.20 = (bf16[64,2048]{1,0:T(8,128)(2,1)S(1)}, bf16[64,2048]{1,0:T(8,128)(2,1)S(1)}, u32[]{:S(2)}, u32[]{:S(2)}) collective-permute-start(bf16[64,2048]{1,0:T(8,128)(2,1)S(1)} %get-tuple-element.39), channel_id=1, source_target_pairs={{0,3},{1,0},{2,1},{3,2},{4,7},{5,4},{6,5},{7,6},{8,11},{9,8},{10,9... | collective-permute-start | bytes 786440 | tf_op jit(solution)/shard_map/ppermute | solution.py:412
  224.3 7.9 %copy-start.5 = (f32[384,2048]{1,0:T(8,128)S(1)}, f32[384,2048]{1,0:T(8,128)}, u32[]{:S(2)}) copy-start(f32[384,2048]{1,0:T(8,128)} %get-tuple-element.31.refs_0_) | copy-start | bytes 9437188
  224.3 17.6 %collective-permute-start.22 = (bf16[128,2048]{1,0:T(8,128)(2,1)S(1)}, bf16[128,2048]{1,0:T(8,128)(2,1)S(1)}, u32[]{:S(2)}, u32[]{:S(2)}) collective-permute-start(bf16[128,2048]{1,0:T(8,128)(2,1)S(1)} %get-tuple-element.40), channel_id=1, source_target_pairs={{0,3},{1,0},{2,1},{3,2},{4,7},{5,4},{6,5},{7,6},{8,11},{9,8},{10,9... | collective-permute-start | bytes 1572872 | tf_op jit(solution)/shard_map/ppermute | solution.py:412
  224.5 16.2 %collective-permute-start.18 = (bf16[128,2048]{1,0:T(8,128)(2,1)S(1)}, bf16[128,2048]{1,0:T(8,128)(2,1)S(1)}, u32[]{:S(2)}, u32[]{:S(2)}) collective-permute-start(bf16[128,2048]{1,0:T(8,128)(2,1)S(1)} %pad_maximum_fusion.1), channel_id=1, source_target_pairs={{0,1},{1,2},{2,3},{3,0},{4,5},{5,6},{6,7},{7,4},{8,9},{9,10},{10,1... | collective-permute-start | bytes 1572872 | tf_op jit(solution)/shard_map/ppermute | solution.py:412
  231.1 13.5 %collective-permute-start.21 = (bf16[128,2048]{1,0:T(8,128)(2,1)S(1)}, bf16[128,2048]{1,0:T(8,128)(2,1)S(1)}, u32[]{:S(2)}, u32[]{:S(2)}) collective-permute-start(bf16[128,2048]{1,0:T(8,128)(2,1)S(1)} %pad_maximum_fusion.2), channel_id=1, source_target_pairs={{0,4},{1,5},{2,6},{3,7},{4,0},{5,1},{6,2},{7,3},{8,12},{9,13},{10,... | collective-permute-start | bytes 1572872 | tf_op jit(solution)/shard_map/ppermute | solution.py:412
  240.7 8.6 %copy-start.3 = (f32[128,2048]{1,0:T(8,128)S(1)}, f32[128,2048]{1,0:T(8,128)}, u32[]{:S(2)}) copy-start(f32[128,2048]{1,0:T(8,128)} %get-tuple-element.30.refs_0_) | copy-start | bytes 3145732
  240.7 16.1 %collective-permute-start.24 = (bf16[128,2048]{1,0:T(8,128)(2,1)S(1)}, bf16[128,2048]{1,0:T(8,128)(2,1)S(1)}, u32[]{:S(2)}, u32[]{:S(2)}) collective-permute-start(bf16[128,2048]{1,0:T(8,128)(2,1)S(1)} %get-tuple-element.41), channel_id=1, source_target_pairs={{0,1},{1,2},{2,3},{3,0},{4,5},{5,6},{6,7},{7,4},{8,9},{9,10},{10,1... | collective-permute-start | bytes 1572872 | tf_op jit(solution)/shard_map/ppermute | solution.py:412
  240.9 15.9 %collective-permute-start.19 = (bf16[128,2048]{1,0:T(8,128)(2,1)S(1)}, bf16[128,2048]{1,0:T(8,128)(2,1)S(1)}, u32[]{:S(2)}, u32[]{:S(2)}) collective-permute-start(bf16[128,2048]{1,0:T(8,128)(2,1)S(1)} %add_convert_fusion.2), channel_id=1, source_target_pairs={{0,4},{1,5},{2,6},{3,7},{4,0},{5,1},{6,2},{7,3},{8,12},{9,13},{10,... | collective-permute-start | bytes 1572872 | tf_op jit(solution)/shard_map/ppermute | solution.py:412
  244.9 12.0 %collective-permute-start.23 = (bf16[128,2048]{1,0:T(8,128)(2,1)S(1)}, bf16[128,2048]{1,0:T(8,128)(2,1)S(1)}, u32[]{:S(2)}, u32[]{:S(2)}) collective-permute-start(bf16[128,2048]{1,0:T(8,128)(2,1)S(1)} %add_convert_fusion.1), channel_id=1, source_target_pairs={{0,3},{1,0},{2,1},{3,2},{4,7},{5,4},{6,5},{7,6},{8,11},{9,8},{10,9... | collective-permute-start | bytes 1572872 | tf_op jit(solution)/shard_map/ppermute | solution.py:412
where the time goes:
time: 260 us; the launch traced here: 258 us
  Pallas kernels  120 us (46%)
  waiting for transfers between devices  66.7 us (26%)
  starting transfers between devices  55.9 us (22%)
  local copies, waits for them, and re-layouts  11.7 us (4%)
  other arithmetic  3.16 us (1%)
    pallas_call x3, Pallas kernels, attend_chunks(): pl.pallas_call(body, grid_spec=pltpu.PrefetchScalarGridSpec(num_scalar_pr...  54.6 us
    ppermute x25, starting transfers between devices, move(): return lax.ppermute(array, AXES, shift_perm(sizes, **by))  38.2 us
    pallas_call x4, Pallas kernels, boost(): pl.pallas_call(body, grid_spec=pltpu.PrefetchScalarGridSpec(num_scalar_pr...  32.7 us
    pallas_call x4, Pallas kernels, gradient(): pl.pallas_call(body, grid=(width // cols,), in_specs=[pl.BlockSpec((rows,...  32.1 us
    ppermute x25, waiting for transfers between devices, move(): return lax.ppermute(array, AXES, shift_perm(sizes, **by))  29.1 us
    all_to_all x1, waiting for transfers between devices, local(): lax.all_to_all(stacked, PLANE, split_axis=0, concat_axis=0, tiled=True)  16.8 us
    all_to_all x1, waiting for transfers between devices, local(): lax.all_to_all(attended, PLANE, split_axis=0, concat_axis=0, tiled=True)  11.8 us
    all_to_all x1, waiting for transfers between devices, local(): lax.all_to_all(spread, ('y', 'c', 'u'), split_axis=0, concat_axis=0, tile...  8.97 us
  transfers between devices with their start and end apart: 28, of which 10 were waited for; matrix products, arithmetic and copies ran while one was open for 2% of the time, Pallas kernels for 41%

commit v1 on v0

--- a/solution.py
+++ b/solution.py
@@ -34,7 +34,7 @@
     return pairs
 
 
-def attention_kernel(first, last, turns, sub, lengths, q_ref, *refs):
+def attention_kernel(first, last, turns, sub, part, lengths, q_ref, *refs):
     chunks = len(turns)
     keys = refs[: 2 * chunks : 2]
     values = refs[1 : 2 * chunks : 2]
@@ -46,7 +46,7 @@
         top_ref, sum_ref = rest.pop(0), rest.pop(0)
     else:
         top_ref, sum_ref = rest.pop(0), rest.pop(0)
-    wide = rest.pop(0)
+    wide, held = rest.pop(0), rest.pop(0)
     step = pl.program_id(0)
     rows = top_ref.shape[0]
     depth = wide.shape[1]
@@ -57,6 +57,7 @@
         for n in range(chunks):
             wide[n, :, :HEAD_DIM] = values[n][...].reshape(depth, HEAD_DIM)
             wide[n, :, HEAD_DIM:] = jnp.ones((depth, HEAD_DIM), wide.dtype)
+            held[n] = keys[n][...].reshape(depth, HEAD_DIM)
 
     if first:
         top_ref[...] = jnp.full_like(top_ref, LOW)
@@ -67,50 +68,62 @@
     length = lengths[lax.axis_index("c")]
     y_at, y_size = lax.axis_index("y"), lax.axis_size("y")
     queries_real = length - y_at * depth > step * rows
-    counts = [length - lax.rem(y_at + turn + y_size, y_size) * depth for turn in turns]
-
-    def attend(n, masked):
-        key = keys[n][...].reshape(depth, HEAD_DIM)
-
-        def piece(index, _):
-            at = pl.multiple_of(index * sub, sub)
-            query = q_ref[pl.ds(index * (sub // 64), sub // 64)].reshape(sub, HEAD_DIM)
+
+    def piece(n, at, count, masked):
+        query = q_ref[pl.ds(at // 64, sub // 64)].reshape(sub, HEAD_DIM)
+        where = pl.ds(at, sub)
+        top = top_ref[where, :1]
+        summed = sum_ref[where, :]
+        for start in range(0, depth, part):
+            key = held[n, start : start + part]
             scores = lax.dot_general(
                 query, key, (((1,), (1,)), ((), ())), preferred_element_type=jnp.float32
             )
             if masked:
-                place = lax.broadcasted_iota(jnp.int32, scores.shape, 1)
-                scores = jnp.where(place < counts[n], scores, LOW)
-            old_top = top_ref[pl.ds(at, sub), :]
-            new_top = jnp.maximum(old_top, jnp.max(scores, axis=1, keepdims=True))
-            weights = jnp.exp2((scores - new_top[:, :1]) * scale)
-            shrink = jnp.exp2((old_top - new_top) * scale)
+                place = lax.broadcasted_iota(jnp.int32, scores.shape, 1) + start
+                scores = jnp.where(place < count, scores, LOW)
+            new_top = jnp.maximum(top, jnp.max(scores, axis=1, keepdims=True))
+            weights = jnp.exp2((scores - new_top) * scale)
             added = jnp.dot(
-                weights.astype(jnp.bfloat16), wide[n], preferred_element_type=jnp.float32
+                weights.astype(jnp.bfloat16),
+                wide[n, start : start + part],
+                preferred_element_type=jnp.float32,
             )
-            top_ref[pl.ds(at, sub), :] = new_top
-            for part in range(0, 2 * HEAD_DIM, HEAD_DIM):
-                cols = pl.ds(part, HEAD_DIM)
-                sum_ref[pl.ds(at, sub), cols] = (
-                    sum_ref[pl.ds(at, sub), cols] * shrink + added[:, part : part + HEAD_DIM]
-                )
-            return 0
-
-        lax.fori_loop(0, rows // sub, piece, 0)
-
-    for n in range(chunks):
-
-        @pl.when(jnp.logical_and(queries_real, counts[n] >= depth))
+            summed = summed * jnp.exp2((top - new_top) * scale) + added
+            top = new_top
+        top_ref[where, :] = jnp.broadcast_to(top, (sub, HEAD_DIM))
+        sum_ref[where, :] = summed
+
+    def attend(n, count, masked):
+        if masked:
+
+            def one(index, carry):
+                piece(n, pl.multiple_of(index * sub, sub), count, True)
+                return carry
+
+            lax.fori_loop(0, rows // sub, one, 0)
+        else:
+            for at in range(0, rows, sub):
+                piece(n, at, count, False)
+
+    def chunk(n, carry):
+        turn = turns[0] + n * (turns[-1] - turns[0])
+        count = length - lax.rem(y_at + turn + y_size, y_size) * depth
+
+        @pl.when(jnp.logical_and(queries_real, count >= depth))
         def _():
-            attend(n, False)
-
-        @pl.when(
-            jnp.logical_and(
-                queries_real, jnp.logical_and(counts[n] > 0, counts[n] < depth)
-            )
-        )
+            attend(n, count, False)
+
+        @pl.when(jnp.logical_and(queries_real, jnp.logical_and(count > 0, count < depth)))
         def _():
-            attend(n, True)
+            attend(n, count, True)
+
+        return carry
+
+    if chunks == 1:
+        chunk(0, 0)
+    else:
+        lax.fori_loop(0, chunks, chunk, 0)
 
     if last:
 
@@ -124,16 +137,16 @@
             out_ref[...] = jnp.zeros_like(out_ref)
 
 
-def attend_chunks(lengths, qkv, pairs, turns, carry, last, block=512, sub=256):
+def attend_chunks(lengths, qkv, pairs, turns, carry, last, block=512, sub=256, part=512):
     sources, tokens = qkv.shape[0], qkv.shape[2]
     total = sources * tokens
     first = carry is None
     chunks = len(pairs) // 2
 
-    def whole(array, part):
+    def whole(array, which):
         if array.ndim == 4:
             return pl.BlockSpec(
-                (sources, None, tokens, HEAD_DIM), lambda i, counts: (0, part, 0, 0)
+                (sources, None, tokens, HEAD_DIM), lambda i, counts: (0, which, 0, 0)
             )
         return pl.BlockSpec((sources, tokens, HEAD_DIM), lambda i, counts: (0, 0, 0))
 
@@ -141,15 +154,18 @@
         pl.BlockSpec((block // tokens, None, tokens, HEAD_DIM), lambda i, counts: (i, 0, 0, 0))
     ]
     operands = [qkv]
-    for array, part in pairs:
-        in_specs.append(whole(array, part))
+    for array, which in pairs:
+        in_specs.append(whole(array, which))
         operands.append(array)
     top_spec = pl.BlockSpec((block, HEAD_DIM), lambda i, counts: (i, 0))
     sum_spec = pl.BlockSpec((block, 2 * HEAD_DIM), lambda i, counts: (i, 0))
     if not first:
         in_specs += [top_spec, sum_spec]
         operands += list(carry)
-    scratch = [pltpu.VMEM((chunks, total, 2 * HEAD_DIM), jnp.bfloat16)]
+    scratch = [
+        pltpu.VMEM((chunks, total, 2 * HEAD_DIM), jnp.bfloat16),
+        pltpu.VMEM((chunks, total, HEAD_DIM), jnp.bfloat16),
+    ]
     if last:
         out_specs = pl.BlockSpec((block // tokens, tokens, HEAD_DIM), lambda i, counts: (i, 0, 0))
         out_shape = jax.ShapeDtypeStruct((sources, tokens, HEAD_DIM), jnp.bfloat16)
@@ -165,7 +181,7 @@
         ]
 
     def body(*refs):
-        attention_kernel(first, last, turns, sub, *refs)
+        attention_kernel(first, last, turns, sub, part, *refs)
 
     return pl.pallas_call(
         body,
@@ -187,39 +203,22 @@
     )(lengths, *operands)
 
 
-def logits_kernel(blocks, tiles, places, lengths, own_hbm, near_hbm, far_hbm, bias_ref, *refs):
+def logits_kernel(blocks, places, lengths, own_hbm, near_hbm, far_hbm, bias_ref, *refs):
     rows_in = refs[:blocks]
     slope_ref, total_ref, rows_ref, held, sems = refs[blocks:]
     step = pl.program_id(0)
-    steps = pl.num_programs(0)
     cols = held.shape[2]
 
-    def fetch(at, slot):
-        def start(source, first):
-            where = pl.ds(pl.multiple_of((at - first) * cols, cols), cols)
-            pltpu.make_async_copy(source.at[:, where], held.at[slot], sems.at[slot]).start()
-
-        @pl.when(at < tiles[0])
-        def _():
-            start(own_hbm, 0)
-
-        @pl.when(jnp.logical_and(at >= tiles[0], at < tiles[1]))
-        def _():
-            start(near_hbm, tiles[0])
-
-        @pl.when(at >= tiles[1])
-        def _():
-            start(far_hbm, tiles[1])
-
-    slot = lax.rem(step, 2)
+    tile_sources = []
+    for source in (own_hbm, near_hbm, far_hbm):
+        tile_sources += [(source, at) for at in range(0, source.shape[1], cols)]
 
     @pl.when(step == 0)
     def _():
-        fetch(step, slot)
-
-    @pl.when(step + 1 < steps)
-    def _():
-        fetch(step + 1, 1 - slot)
+        for n, (source, at) in enumerate(tile_sources):
+            pltpu.make_async_copy(
+                source.at[:, at : at + cols], held.at[n], sems.at[n]
+            ).start()
 
     @pl.when(step == 0)
     def _():
@@ -228,8 +227,8 @@
             rows_ref[pl.ds(at, ref.shape[0]), :] = ref[...]
             at += ref.shape[0]
 
-    pltpu.make_async_copy(own_hbm.at[:, pl.ds(0, cols)], held.at[slot], sems.at[slot]).wait()
-    logits = jnp.dot(rows_ref[...], held[slot], preferred_element_type=jnp.float32) + bias_ref[...]
+    pltpu.make_async_copy(own_hbm.at[:, pl.ds(0, cols)], held.at[step], sems.at[step]).wait()
+    logits = jnp.dot(rows_ref[...], held[step], preferred_element_type=jnp.float32) + bias_ref[...]
     tokens = 64
     y_at, c_at, u_at, w_at, z_at = [lax.axis_index(axis) for axis in AXES]
     _, c_size, u_size, w_size, z_size = [lax.axis_size(axis) for axis in AXES]
@@ -260,16 +259,16 @@
     sizes = [w.shape[1] for w in weights]
     entries = sum(sizes)
     rows = sum(b.shape[0] for b in blocks)
-    tiles = (sizes[0] // cols, (sizes[0] + sizes[1]) // cols)
+    tiles = entries // cols
 
     def body(*refs):
-        logits_kernel(len(blocks), tiles, places, *refs)
+        logits_kernel(len(blocks), places, *refs)
 
     return pl.pallas_call(
         body,
         grid_spec=pltpu.PrefetchScalarGridSpec(
             num_scalar_prefetch=1,
-            grid=(entries // cols,),
+            grid=(tiles,),
             in_specs=[pl.BlockSpec(memory_space=pltpu.HBM)] * 3
             + [pl.BlockSpec((1, cols), lambda j, counts: (0, j))]
             + [pl.BlockSpec(b.shape, lambda j, counts: (0, 0)) for b in blocks],
@@ -279,8 +278,8 @@
             ],
             scratch_shapes=[
                 pltpu.VMEM((rows, width), jnp.bfloat16),
-                pltpu.VMEM((2, width, cols), jnp.bfloat16),
-                pltpu.SemaphoreType.DMA((2,)),
+                pltpu.VMEM((tiles, width, cols), jnp.bfloat16),
+                pltpu.SemaphoreType.DMA((tiles,)),
             ],
         ),
         out_shape=[
@@ -292,17 +291,33 @@
             bytes_accessed=width * entries * 2 + rows * entries * 4,
             transcendentals=0,
         ),
-        compiler_params=pltpu.CompilerParams(vmem_limit_bytes=20 << 20),
+        compiler_params=pltpu.CompilerParams(vmem_limit_bytes=28 << 20),
         name="boost",
     )(lengths, *weights, bias, *blocks)
 
 
-def gradient_kernel(outs, slope_ref, coef_ref, own_ref, near_ref, far_ref, *refs):
-    out_refs, slopes = refs[:outs], refs[outs]
+def gradient_kernel(outs, slope_ref, coef_ref, own_hbm, near_hbm, far_hbm, *refs):
+    out_refs, slopes, held, sems = refs[:outs], *refs[outs:]
     tokens = 64
-
-    @pl.when(pl.program_id(0) == 0)
+    step = pl.program_id(0)
+    tiles, cols = held.shape[0], held.shape[1]
+    sources = (own_hbm, near_hbm, far_hbm)
+
+    def copies(tile, feature):
+        at = 0
+        for n, source in enumerate(sources):
+            yield pltpu.make_async_copy(
+                source.at[pl.ds(feature, cols), :],
+                held.at[tile, :, at : at + source.shape[1]],
+                sems.at[tile, n],
+            )
+            at += source.shape[1]
+
+    @pl.when(step == 0)
     def _():
+        for tile in range(tiles):
+            for copy in copies(tile, tile * cols):
+                copy.start()
         for part in range(slopes.shape[0] // tokens):
             where = pl.ds(part * tokens, tokens)
             doc = part % 2
@@ -310,17 +325,11 @@
                 slopes.dtype
             )
 
-    result = None
-    at = 0
-    for ref in (own_ref, near_ref, far_ref):
-        term = lax.dot_general(
-            slopes[:, at : at + ref.shape[1]],
-            ref[...],
-            (((1,), (1,)), ((), ())),
-            preferred_element_type=jnp.float32,
-        )
-        result = term if result is None else result + term
-        at += ref.shape[1]
+    for copy in copies(step, 0):
+        copy.wait()
+    result = lax.dot_general(
+        slopes[...], held[step], (((1,), (1,)), ((), ())), preferred_element_type=jnp.float32
+    )
     at = 0
     for ref in out_refs:
         ref[...] = result[at : at + ref.shape[0]].astype(ref.dtype)
@@ -341,20 +350,22 @@
             pl.BlockSpec((rows, entries), lambda j: (0, 0)),
             pl.BlockSpec((2, entries), lambda j: (0, 0)),
         ]
-        + [pl.BlockSpec((cols, w.shape[1]), lambda j: (j, 0)) for w in weights],
+        + [pl.BlockSpec(memory_space=pltpu.HBM)] * 3,
         out_specs=[pl.BlockSpec((n, cols), lambda j: (0, j)) for n in split],
         out_shape=[jax.ShapeDtypeStruct((n, width), jnp.bfloat16) for n in split],
-        scratch_shapes=[pltpu.VMEM((rows, entries), jnp.bfloat16)],
+        scratch_shapes=[
+            pltpu.VMEM((rows, entries), jnp.bfloat16),
+            pltpu.VMEM((width // cols, cols, entries), jnp.bfloat16),
+            pltpu.SemaphoreType.DMA((width // cols, 3)),
+        ],
         cost_estimate=pl.CostEstimate(
             flops=4 * max(rows, 256) * width * entries,
             bytes_accessed=width * entries * 2 + rows * entries * 4,
             transcendentals=0,
         ),
-        compiler_params=pltpu.CompilerParams(vmem_limit_bytes=20 << 20),
+        compiler_params=pltpu.CompilerParams(vmem_limit_bytes=28 << 20),
         name="gradient",
-    )(
-        slope, coefficient, *[pltpu.with_memory_space_constraint(w, pltpu.HBM) for w in weights]
-    )
+    )(slope, coefficient, *weights)
 
 
 def norm_kernel(docs, heads, back_ref, residual_ref, gain_ref, out_ref):

time: 260 us -> 244 us (0.938)
  Pallas kernels: 120 us -> 94.9 us
  waiting for transfers between devices: 66.7 us -> 73.6 us
    pallas_call x3, Pallas kernels: 54.6 us -> 43.5 us  [attend_chunks(): pl.pallas_call(body, grid_spec=pltpu.PrefetchScalarGridSpec(num_scalar_pr...]
    pallas_call x4, Pallas kernels: 32.1 us -> 23.7 us  [gradient(): pl.pallas_call(body, grid=(width // cols,), in_specs=[pl.BlockSpec((rows,...]
    ppermute x25, waiting for transfers between devices: 29.1 us -> 36.1 us  [move(): return lax.ppermute(array, AXES, shift_perm(sizes, **by))]
    pallas_call x4, Pallas kernels: 32.7 us -> 27.2 us  [boost(): pl.pallas_call(body, grid_spec=pltpu.PrefetchScalarGridSpec(num_scalar_pr...]
    unnamed x23 -> x25, local copies, waits for them, and re-layouts: 3.6 us -> 5.79 us
  transfers between devices with their start and end apart: 28 -> 28, of which waited for: 10 -> 13; matrix products, arithmetic and copies ran while one was open for 2% -> 2% of each run, Pallas kernels for 41% -> 34%
where the time goes in v1:
time: 244 us; the launch traced here: 243 us
  Pallas kernels  94.9 us (39%)
  waiting for transfers between devices  73.6 us (30%)
  starting transfers between devices  56.8 us (23%)
  local copies, waits for them, and re-layouts  13.9 us (6%)
  other arithmetic  3.15 us (1%)
    pallas_call x3, Pallas kernels, attend_chunks(): pl.pallas_call(body, grid_spec=pltpu.PrefetchScalarGridSpec(num_scalar_pr...  43.5 us
    ppermute x25, starting transfers between devices, move(): return lax.ppermute(array, AXES, shift_perm(sizes, **by))  38.7 us
    ppermute x25, waiting for transfers between devices, move(): return lax.ppermute(array, AXES, shift_perm(sizes, **by))  36.1 us
    pallas_call x4, Pallas kernels, boost(): pl.pallas_call(body, grid_spec=pltpu.PrefetchScalarGridSpec(num_scalar_pr...  27.2 us
    pallas_call x4, Pallas kernels, gradient(): pl.pallas_call(body, grid=(width // cols,), in_specs=[pl.BlockSpec((rows,...  23.7 us
    all_to_all x1, waiting for transfers between devices, local(): lax.all_to_all(stacked, PLANE, split_axis=0, concat_axis=0, tiled=True)  16.8 us
    all_to_all x1, waiting for transfers between devices, local(): lax.all_to_all(attended, PLANE, split_axis=0, concat_axis=0, tiled=True)  11.8 us
    all_to_all x1, waiting for transfers between devices, local(): lax.all_to_all(spread, ('y', 'c', 'u'), split_axis=0, concat_axis=0, tile...  8.9 us
  transfers between devices with their start and end apart: 28, of which 13 were waited for; matrix products, arithmetic and copies ran while one was open for 2% of the time, Pallas kernels for 34%

profile of v1, /device:TPU:0, one launch (start us, length us, event | category | flops | bytes accessed | tf_op | source)
XLA Modules:
  0.0 243.5 jit_solution(14174921442191363628)
XLA Ops:
  0.6 1.5 reshape.69
  2.1 0.2 copy.34
  2.3 0.3 reshape.70
  2.7 0.2 copy.35
  2.9 0.3 reshape.71
  3.2 0.2 copy.36
  3.5 1.3 pad_maximum_fusion
  4.8 8.3 %all-to-all-start = ((bf16[32,3,64,128]{3,2,1,0:T(8,128)(2,1)}), bf16[32,3,64,128]{3,2,1,0:T(8,128)(2,1)S(1)}, u32[]{:S(2)}, u32[]{:S(2)}) async-start(bf16[32,3,64,128]{3,2,1,0:T(8,128)(2,1)} %pad_maximum_fusion), calls=%async_computation | async-start | bytes 3145728 | tf_op jit(solution)/shard_map/all_to_all | solution.py:426
  13.1 3.1 %constant_dynamic-slice_fusion = bf16[2048,512]{1,0:T(8,128)(2,1)} fusion(bf16[2048,1024]{1,0:T(8,128)(2,1)} %refs_2_.7, s32[]{:T(128)S(6)} %select_n.60), kind=kLoop, calls=%fused_computation.28 | loop fusion | bytes 4194308 | tf_op jit(solution)/shard_map/dynamic_slice | solution.py:437
  16.1 3.3 %collective-permute-start = (bf16[2048,512]{1,0:T(8,128)(2,1)}, bf16[2048,512]{1,0:T(8,128)(2,1)}, u32[]{:S(2)}, u32[]{:S(2)}) collective-permute-start(bf16[2048,512]{1,0:T(8,128)(2,1)} %constant_dynamic-slice_fusion), channel_id=1, source_target_pairs={{0,8},{1,9},{2,10},{3,11},{4,12},{5,13},{6,14},{7,15},{8,0},{9,1},... | collective-permute-start | bytes 6291464 | tf_op jit(solution)/shard_map/ppermute | solution.py:423
  19.4 16.8 %all-to-all-done.refs_1_.refs_2_.refs_3_ = bf16[32,3,64,128]{3,2,1,0:T(8,128)(2,1)S(1)} async-done(((bf16[32,3,64,128]{3,2,1,0:T(8,128)(2,1)}), bf16[32,3,64,128]{3,2,1,0:T(8,128)(2,1)S(1)}, u32[]{:S(2)}, u32[]{:S(2)}) %all-to-all-start) | async-done | bytes 1572896 | tf_op jit(solution)/shard_map/all_to_all | solution.py:426
  36.3 1.6 collective-permute-start.3
  38.0 1.7 collective-permute-start.5
  39.7 0.4 collective-permute-start.7
  40.0 2.9 %collective-permute-start.8 = (bf16[32,64,128]{2,1,0:T(8,128)(2,1)S(1)}, bf16[32,64,128]{2,1,0:T(8,128)(2,1)S(1)}, u32[]{:S(2)}, u32[]{:S(2)}) collective-permute-start(bf16[32,64,128]{2,1,0:T(8,128)(2,1)S(1)} %get-tuple-element.45), channel_id=1, source_target_pairs={{0,96},{1,97},{2,98},{3,99},{4,100},{5,101},{6,102},{7,103},{8,104... | collective-permute-start | bytes 1572872 | tf_op jit(solution)/shard_map/ppermute | solution.py:423
  42.9 10.5 %attend_first.1 = (f32[2048,128]{1,0:T(8,128)S(1)}, f32[2048,256]{1,0:T(8,128)S(1)}) custom-call(s32[2]{0:T(128)S(1)} %copy-done.3, bf16[32,3,64,128]{3,2,1,0:T(8,128)(2,1)S(1)} %all-to-all-done.refs_1_.refs_2_.refs_3_, bf16[32,3,64,128]{3,2,1,0:T(8,128)(2,1)S(1)} %all-to-all-done.refs_1_.refs_2_.refs_3_, ...), custom_call_target="tpu_custom_call" | custom-call | flops 4294967296 | bytes 4194304 | tf_op jit(solution)/shard_map/attend_first/pallas_call | solution.py:186
  53.5 3.2 %collective-permute-start.6 = (bf16[32,64,128]{2,1,0:T(8,128)(2,1)S(1)}, bf16[32,64,128]{2,1,0:T(8,128)(2,1)S(1)}, u32[]{:S(2)}, u32[]{:S(2)}) collective-permute-start(bf16[32,64,128]{2,1,0:T(8,128)(2,1)S(1)} %collective-permute-done.5.refs_5_), channel_id=1, source_target_pairs={{0,96},{1,97},{2,98},{3,99},{4,100},{5,101},{6,102},{7,103},{8,104... | collective-permute-start | bytes 1572872 | tf_op jit(solution)/shard_map/ppermute | solution.py:423
  56.7 6.9 %collective-permute-done.7.refs_3_ = bf16[32,64,128]{2,1,0:T(8,128)(2,1)S(1)} collective-permute-done((bf16[32,64,128]{2,1,0:T(8,128)(2,1)S(1)}, bf16[32,64,128]{2,1,0:T(8,128)(2,1)S(1)}, u32[]{:S(2)}, u32[]{:S(2)}) %collective-permute-start.7) | collective-permute-done | bytes 524320 | tf_op jit(solution)/shard_map/ppermute | solution.py:423
  63.7 0.4 collective-permute-done.8.refs_4_
  64.0 21.8 %attend_next.1 = (f32[2048,128]{1,0:T(8,128)S(1)}, f32[2048,256]{1,0:T(8,128)S(1)}) custom-call(s32[2]{0:T(128)S(1)} %copy-done.3, bf16[32,3,64,128]{3,2,1,0:T(8,128)(2,1)S(1)} %all-to-all-done.refs_1_.refs_2_.refs_3_, bf16[32,64,128]{2,1,0:T(8,128)(2,1)S(1)} %collective-permute-done.3.refs_2_, bf16[32,64,128]{2,1,0:T(8,128)(2,1)S(1)} %collective-permute-done.7.refs_3_, ...), custom_call_target="tpu_custom_call" | custom-call | flops 8589934592 | bytes 4194304 | tf_op jit(solution)/shard_map/attend_next/pallas_call | solution.py:186
  86.0 11.2 %attend_last.1 = bf16[32,64,128]{2,1,0:T(8,128)(2,1)} custom-call(s32[2]{0:T(128)S(1)} %copy-done.3, bf16[32,3,64,128]{3,2,1,0:T(8,128)(2,1)S(1)} %all-to-all-done.refs_1_.refs_2_.refs_3_, bf16[32,64,128]{2,1,0:T(8,128)(2,1)S(1)} %collective-permute-done.4.refs_2_, bf16[32,64,128]{2,1,0:T(8,128)(2,1)S(1)} %collective-permute-done.6.refs_3_, ...), custom_call_target="tpu_custom_call" | custom-call | flops 4294967296 | bytes 4194304 | tf_op jit(solution)/shard_map/attend_last/pallas_call | solution.py:186
  97.2 6.2 %all-to-all-start.1 = ((bf16[32,64,128]{2,1,0:T(8,128)(2,1)}), bf16[32,64,128]{2,1,0:T(8,128)(2,1)S(1)}, u32[]{:S(2)}, u32[]{:S(2)}) async-start(bf16[32,64,128]{2,1,0:T(8,128)(2,1)} %attend_last.1), calls=%async_computation.1 | async-start | bytes 1048576 | tf_op jit(solution)/shard_map/all_to_all | solution.py:460
  103.7 11.8 %all-to-all-done.1.refs_0_ = bf16[32,64,128]{2,1,0:T(8,128)(2,1)S(1)} async-done(((bf16[32,64,128]{2,1,0:T(8,128)(2,1)}), bf16[32,64,128]{2,1,0:T(8,128)(2,1)S(1)}, u32[]{:S(2)}, u32[]{:S(2)}) %all-to-all-start.1) | async-done | bytes 524320 | tf_op jit(solution)/shard_map/all_to_all | solution.py:460
  115.5 0.4 normalized.1.refs_5_
  115.9 0.3 collective-permute-start.10
  116.2 0.6 collective-permute-start.9
  116.8 1.8 collective-permute-start.2
  118.6 3.1 %collective-permute-start.11 = (bf16[128,2048]{1,0:T(8,128)(2,1)S(1)}, bf16[128,2048]{1,0:T(8,128)(2,1)S(1)}, u32[]{:S(2)}, u32[]{:S(2)}) collective-permute-start(bf16[128,2048]{1,0:T(8,128)(2,1)S(1)} %normalized.1.refs_5_), channel_id=1, source_target_pairs={{0,3},{1,0},{2,1},{3,2},{4,7},{5,4},{6,5},{7,6},{8,11},{9,8},{10,9... | collective-permute-start | bytes 1572872 | tf_op jit(solution)/shard_map/ppermute | solution.py:423
  121.7 8.5 %collective-permute-done.10.refs_6_ = bf16[128,2048]{1,0:T(8,128)(2,1)S(1)} collective-permute-done((bf16[128,2048]{1,0:T(8,128)(2,1)S(1)}, bf16[128,2048]{1,0:T(8,128)(2,1)S(1)}, u32[]{:S(2)}, u32[]{:S(2)}) %collective-permute-start.10) | collective-permute-done | bytes 524320 | tf_op jit(solution)/shard_map/ppermute | solution.py:423
  130.2 1.0 collective-permute-start.12
  131.3 1.3 collective-permute-start.14
  132.6 0.8 collective-permute-start.13
  133.4 9.0 %collective-permute-done.12.refs_5_ = bf16[128,2048]{1,0:T(8,128)(2,1)S(1)} collective-permute-done((bf16[128,2048]{1,0:T(8,128)(2,1)S(1)}, bf16[128,2048]{1,0:T(8,128)(2,1)S(1)}, u32[]{:S(2)}, u32[]{:S(2)}) %collective-permute-start.12) | collective-permute-done | bytes 524320 | tf_op jit(solution)/shard_map/ppermute | solution.py:423
  142.4 0.8 collective-permute-start.15
  143.2 0.4 collective-permute-done.14.refs_7_
  143.6 4.0 %collective-permute-start.16 = (bf16[64,2048]{1,0:T(8,128)(2,1)S(1)}, bf16[64,2048]{1,0:T(8,128)(2,1)S(1)}, u32[]{:S(2)}, u32[]{:S(2)}) collective-permute-start(bf16[64,2048]{1,0:T(8,128)(2,1)S(1)} %slice.89), channel_id=1, source_target_pairs={{0,3},{1,0},{2,1},{3,2},{4,7},{5,4},{6,5},{7,6},{8,11},{9,8},{10,9... | collective-permute-start | bytes 786440 | tf_op jit(solution)/shard_map/ppermute | solution.py:423
  147.6 2.2 copy-done
  149.8 7.9 %boost.5 = (f32[384,2048]{1,0:T(8,128)}, f32[2,2048]{1,0:T(2,128)S(1)}) custom-call(s32[2]{0:T(128)S(1)} %copy-done.3, bf16[2048,1024]{1,0:T(8,128)(2,1)S(1)} %copy-done, bf16[2048,512]{1,0:T(8,128)(2,1)} %collective-permute-done.refs_2_.refs_3_, bf16[2048,512]{1,0:T(8,128)(2,1)} %collective-permute-done.1.refs_3_.refs_4_, ...), custom_call_target="tpu_custom_call" | custom-call | flops 6442450944 | bytes 11534336 | tf_op jit(solution)/shard_map/boost/pallas_call | solution.py:267
  157.6 8.0 %boost.6 = (f32[384,2048]{1,0:T(8,128)}, f32[2,2048]{1,0:T(2,128)S(1)}) custom-call(s32[2]{0:T(128)S(1)} %copy-done.3, bf16[2048,1024]{1,0:T(8,128)(2,1)S(1)} %copy-done, bf16[2048,512]{1,0:T(8,128)(2,1)} %collective-permute-done.refs_2_.refs_3_, bf16[2048,512]{1,0:T(8,128)(2,1)} %collective-permute-done.1.refs_3_.refs_4_, ...), custom_call_target="tpu_custom_call" | custom-call | flops 6442450944 | bytes 11534336 | tf_op jit(solution)/shard_map/boost/pallas_call | solution.py:267
  165.6 5.7 %boost.4 = (f32[128,2048]{1,0:T(8,128)}, f32[2,2048]{1,0:T(2,128)S(1)}) custom-call(s32[2]{0:T(128)S(1)} %copy-done.3, bf16[2048,1024]{1,0:T(8,128)(2,1)S(1)} %copy-done, bf16[2048,512]{1,0:T(8,128)(2,1)} %collective-permute-done.refs_2_.refs_3_, bf16[2048,512]{1,0:T(8,128)(2,1)} %collective-permute-done.1.refs_3_.refs_4_, ...), custom_call_target="tpu_custom_call" | custom-call | flops 4294967296 | bytes 9437184 | tf_op jit(solution)/shard_map/boost/pallas_call | solution.py:267
  171.3 5.7 %boost.7 = (f32[128,2048]{1,0:T(8,128)}, f32[2,2048]{1,0:T(2,128)S(1)}) custom-call(s32[2]{0:T(128)S(1)} %copy-done.3, bf16[2048,1024]{1,0:T(8,128)(2,1)S(1)} %copy-done, bf16[2048,512]{1,0:T(8,128)(2,1)} %collective-permute-done.refs_2_.refs_3_, bf16[2048,512]{1,0:T(8,128)(2,1)} %collective-permute-done.1.refs_3_.refs_4_, ...), custom_call_target="tpu_custom_call" | custom-call | flops 4294967296 | bytes 9437184 | tf_op jit(solution)/shard_map/boost/pallas_call | solution.py:267
  177.1 0.8 broadcast_in_dim.2
  177.9 3.5 %all-to-all-start.2 = ((f32[16,2,2,1024]{3,2,1,0:T(2,128)}), f32[16,2,2,1024]{3,2,1,0:T(2,128)S(1)}, u32[]{:S(2)}, u32[]{:S(2)}) async-start(f32[16,2,2,1024]{3,2,1,0:T(2,128)} %broadcast_in_dim.2), calls=%async_computation.2 | async-start | bytes 524288 | tf_op jit(solution)/shard_map/all_to_all | solution.py:488
  181.4 8.9 %all-to-all-done.2 = f32[16,2,2,1024]{3,2,1,0:T(2,128)S(1)} async-done(((f32[16,2,2,1024]{3,2,1,0:T(2,128)}), f32[16,2,2,1024]{3,2,1,0:T(2,128)S(1)}, u32[]{:S(2)}, u32[]{:S(2)}) %all-to-all-start.2) | async-done | bytes 262176 | tf_op jit(solution)/shard_map/all_to_all | solution.py:488
  190.7 2.2 copy-done.1
  192.9 1.2 copy-done.5
  194.1 5.5 %gradient.7 = (bf16[64,2048]{1,0:T(8,128)(2,1)S(1)}, bf16[64,2048]{1,0:T(8,128)(2,1)S(1)}) custom-call(f32[128,2048]{1,0:T(8,128)S(1)} %copy-done.5, f32[2,2048]{1,0:T(2,128)S(1)} %pad_maximum_fusion.3.refs_1_, bf16[2048,1024]{1,0:T(8,128)(2,1)S(1)} %copy-done.1, bf16[2048,512]{1,0:T(8,128)(2,1)} %collective-permute-done.refs_2_.refs_3_, ...), custom_call_target="tpu_custom_call" | custom-call | flops 4294967296 | bytes 9437184 | tf_op jit(solution)/shard_map/gradient/pallas_call | solution.py:346
  199.7 6.5 %gradient.6 = (bf16[128,2048]{1,0:T(8,128)(2,1)S(1)}, bf16[128,2048]{1,0:T(8,128)(2,1)S(1)}, bf16[128,2048]{1,0:T(8,128)(2,1)S(1)}) custom-call(f32[384,2048]{1,0:T(8,128)S(1)} %copy-done.7, f32[2,2048]{1,0:T(2,128)S(1)} %pad_maximum_fusion.3.refs_1_, bf16[2048,1024]{1,0:T(8,128)(2,1)S(1)} %copy-done.1, ...), custom_call_target="tpu_custom_call" | custom-call | flops 6442450944 | bytes 11534336 | tf_op jit(solution)/shard_map/gradient/pallas_call | solution.py:346
  206.1 3.3 %collective-permute-start.20 = (bf16[64,2048]{1,0:T(8,128)(2,1)S(1)}, bf16[64,2048]{1,0:T(8,128)(2,1)S(1)}, u32[]{:S(2)}, u32[]{:S(2)}) collective-permute-start(bf16[64,2048]{1,0:T(8,128)(2,1)S(1)} %get-tuple-element.39), channel_id=1, source_target_pairs={{0,3},{1,0},{2,1},{3,2},{4,7},{5,4},{6,5},{7,6},{8,11},{9,8},{10,9... | collective-permute-start | bytes 786440 | tf_op jit(solution)/shard_map/ppermute | solution.py:423
  209.6 2.1 collective-permute-start.18
  211.7 4.4 %collective-permute-done.20 = bf16[64,2048]{1,0:T(8,128)(2,1)S(1)} collective-permute-done((bf16[64,2048]{1,0:T(8,128)(2,1)S(1)}, bf16[64,2048]{1,0:T(8,128)(2,1)S(1)}, u32[]{:S(2)}, u32[]{:S(2)}) %collective-permute-start.20) | collective-permute-done | bytes 262176 | tf_op jit(solution)/shard_map/ppermute | solution.py:423
  216.2 0.8 collective-permute-start.21
  217.0 6.4 %gradient.5 = (bf16[128,2048]{1,0:T(8,128)(2,1)S(1)}, bf16[128,2048]{1,0:T(8,128)(2,1)S(1)}, bf16[128,2048]{1,0:T(8,128)(2,1)S(1)}) custom-call(f32[384,2048]{1,0:T(8,128)S(1)} %copy-done.6, f32[2,2048]{1,0:T(2,128)S(1)} %pad_maximum_fusion.3.refs_1_, bf16[2048,1024]{1,0:T(8,128)(2,1)S(1)} %copy-done.1, ...), custom_call_target="tpu_custom_call" | custom-call | flops 6442450944 | bytes 11534336 | tf_op jit(solution)/shard_map/gradient/pallas_call | solution.py:346
  223.5 0.8 collective-permute-done.18
  224.5 0.8 collective-permute-start.19
  225.3 1.0 collective-permute-done.22
  226.2 4.0 %collective-permute-done.21 = bf16[128,2048]{1,0:T(8,128)(2,1)S(1)} collective-permute-done((bf16[128,2048]{1,0:T(8,128)(2,1)S(1)}, bf16[128,2048]{1,0:T(8,128)(2,1)S(1)}, u32[]{:S(2)}, u32[]{:S(2)}) %collective-permute-start.21) | collective-permute-done | bytes 524320 | tf_op jit(solution)/shard_map/ppermute | solution.py:423
  230.2 0.2 add_convert_fusion.1
  230.4 4.7 %collective-permute-start.23 = (bf16[128,2048]{1,0:T(8,128)(2,1)S(1)}, bf16[128,2048]{1,0:T(8,128)(2,1)S(1)}, u32[]{:S(2)}, u32[]{:S(2)}) collective-permute-start(bf16[128,2048]{1,0:T(8,128)(2,1)S(1)} %add_convert_fusion.1), channel_id=1, source_target_pairs={{0,3},{1,0},{2,1},{3,2},{4,7},{5,4},{6,5},{7,6},{8,11},{9,8},{10,9... | collective-permute-start | bytes 1572872 | tf_op jit(solution)/shard_map/ppermute | solution.py:423
  235.1 0.6 fusion
  235.7 5.3 %gradient.4 = bf16[128,2048]{1,0:T(8,128)(2,1)S(1)} custom-call(f32[128,2048]{1,0:T(8,128)S(1)} %copy-done.4, f32[2,2048]{1,0:T(2,128)S(1)} %pad_maximum_fusion.3.refs_1_, bf16[2048,1024]{1,0:T(8,128)(2,1)S(1)} %copy-done.1, bf16[2048,512]{1,0:T(8,128)(2,1)} %collective-permute-done.refs_2_.refs_3_, bf16[2048,512]{1,0:T(8,128)(2,1)} %collective-permute-done.1.refs_3_.refs_4_), custom_call_target="tpu_custom_call" | custom-call | flops 4294967296 | bytes 9437184 | tf_op jit(solution)/shard_map/gradient/pallas_call | solution.py:346
  241.1 0.7 collective-permute-done.23
  241.8 0.3 add_convert_fusion
  242.1 1.3 copy.47
  (68 shorter events, 1.4 us)
Async XLA Ops:
  0.6 1.7 copy-start.8
  0.6 2.3 copy-start.9
  4.8 31.5 %all-to-all-start = ((bf16[32,3,64,128]{3,2,1,0:T(8,128)(2,1)}), bf16[32,3,64,128]{3,2,1,0:T(8,128)(2,1)S(1)}, u32[]{:S(2)}, u32[]{:S(2)}) async-start(bf16[32,3,64,128]{3,2,1,0:T(8,128)(2,1)} %pad_maximum_fusion), calls=%async_computation | async-start | bytes 3145728 | tf_op jit(solution)/shard_map/all_to_all | solution.py:426
  16.1 26.8 %copy-start.3 = (s32[2]{0:T(128)S(1)}, s32[2]{0:T(128)}, u32[]{:S(2)}) copy-start(s32[2]{0:T(128)} %refs_0_.13) | copy-start | bytes 28
  16.1 69.7 %collective-permute-start = (bf16[2048,512]{1,0:T(8,128)(2,1)}, bf16[2048,512]{1,0:T(8,128)(2,1)}, u32[]{:S(2)}, u32[]{:S(2)}) collective-permute-start(bf16[2048,512]{1,0:T(8,128)(2,1)} %constant_dynamic-slice_fusion), channel_id=1, source_target_pairs={{0,8},{1,9},{2,10},{3,11},{4,12},{5,13},{6,14},{7,15},{8,0},{9,1},... | collective-permute-start | bytes 6291464 | tf_op jit(solution)/shard_map/ppermute | solution.py:423
  36.3 17.1 %collective-permute-start.3 = (bf16[32,64,128]{2,1,0:T(8,128)(2,1)S(1)}, bf16[32,64,128]{2,1,0:T(8,128)(2,1)S(1)}, u32[]{:S(2)}, u32[]{:S(2)}) collective-permute-start(bf16[32,64,128]{2,1,0:T(8,128)(2,1)S(1)} %get-tuple-element.45), channel_id=1, source_target_pairs={{0,32},{1,33},{2,34},{3,35},{4,36},{5,37},{6,38},{7,39},{8,40},{9,... | collective-permute-start | bytes 1572872 | tf_op jit(solution)/shard_map/ppermute | solution.py:423
  38.0 15.5 %collective-permute-start.5 = (bf16[32,64,128]{2,1,0:T(8,128)(2,1)S(1)}, bf16[32,64,128]{2,1,0:T(8,128)(2,1)S(1)}, u32[]{:S(2)}, u32[]{:S(2)}) collective-permute-start(bf16[32,64,128]{2,1,0:T(8,128)(2,1)S(1)} %get-tuple-element.44), channel_id=1, source_target_pairs={{0,96},{1,97},{2,98},{3,99},{4,100},{5,101},{6,102},{7,103},{8,104... | collective-permute-start | bytes 1572872 | tf_op jit(solution)/shard_map/ppermute | solution.py:423
  39.7 24.0 %collective-permute-start.7 = (bf16[32,64,128]{2,1,0:T(8,128)(2,1)S(1)}, bf16[32,64,128]{2,1,0:T(8,128)(2,1)S(1)}, u32[]{:S(2)}, u32[]{:S(2)}) collective-permute-start(bf16[32,64,128]{2,1,0:T(8,128)(2,1)S(1)} %get-tuple-element.44), channel_id=1, source_target_pairs={{0,32},{1,33},{2,34},{3,35},{4,36},{5,37},{6,38},{7,39},{8,40},{9,... | collective-permute-start | bytes 1572872 | tf_op jit(solution)/shard_map/ppermute | solution.py:423
  40.0 24.0 %collective-permute-start.8 = (bf16[32,64,128]{2,1,0:T(8,128)(2,1)S(1)}, bf16[32,64,128]{2,1,0:T(8,128)(2,1)S(1)}, u32[]{:S(2)}, u32[]{:S(2)}) collective-permute-start(bf16[32,64,128]{2,1,0:T(8,128)(2,1)S(1)} %get-tuple-element.45), channel_id=1, source_target_pairs={{0,96},{1,97},{2,98},{3,99},{4,100},{5,101},{6,102},{7,103},{8,104... | collective-permute-start | bytes 1572872 | tf_op jit(solution)/shard_map/ppermute | solution.py:423
  53.4 32.5 %collective-permute-start.4 = (bf16[32,64,128]{2,1,0:T(8,128)(2,1)S(1)}, bf16[32,64,128]{2,1,0:T(8,128)(2,1)S(1)}, u32[]{:S(2)}, u32[]{:S(2)}) collective-permute-start(bf16[32,64,128]{2,1,0:T(8,128)(2,1)S(1)} %collective-permute-done.3.refs_2_), channel_id=1, source_target_pairs={{0,32},{1,33},{2,34},{3,35},{4,36},{5,37},{6,38},{7,39},{8,40},{9,... | collective-permute-start | bytes 1572872 | tf_op jit(solution)/shard_map/ppermute | solution.py:423
  53.5 32.4 %collective-permute-start.6 = (bf16[32,64,128]{2,1,0:T(8,128)(2,1)S(1)}, bf16[32,64,128]{2,1,0:T(8,128)(2,1)S(1)}, u32[]{:S(2)}, u32[]{:S(2)}) collective-permute-start(bf16[32,64,128]{2,1,0:T(8,128)(2,1)S(1)} %collective-permute-done.5.refs_5_), channel_id=1, source_target_pairs={{0,96},{1,97},{2,98},{3,99},{4,100},{5,101},{6,102},{7,103},{8,104... | collective-permute-start | bytes 1572872 | tf_op jit(solution)/shard_map/ppermute | solution.py:423
  85.8 61.7 %collective-permute-start.1 = (bf16[2048,512]{1,0:T(8,128)(2,1)}, bf16[2048,512]{1,0:T(8,128)(2,1)}, u32[]{:S(2)}, u32[]{:S(2)}) collective-permute-start(bf16[2048,512]{1,0:T(8,128)(2,1)} %collective-permute-done.refs_2_.refs_3_), channel_id=1, source_target_pairs={{0,16},{1,17},{2,18},{3,19},{4,20},{5,21},{6,22},{7,23},{8,24},{9,... | collective-permute-start | bytes 6291464 | tf_op jit(solution)/shard_map/ppermute | solution.py:423
  86.0 17.5 %copy-start.10 = (bf16[64,2,2048]{2,1,0:T(2,128)(2,1)S(1)}, bf16[64,2,2048]{2,1,0:T(2,128)(2,1)}, u32[]{:S(2)}) copy-start(bf16[64,2,2048]{2,1,0:T(2,128)(2,1)} %param.11) | copy-start | bytes 1572868
  97.2 18.2 %copy-start.2 = (f32[2048]{0:T(1024)S(1)}, f32[2048]{0:T(1024)}, u32[]{:S(2)}) copy-start(f32[2048]{0:T(1024)} %param.12) | copy-start | bytes 24580
  97.2 19.6 %copy-start.11 = (f32[1024]{0:T(1024)S(1)}, f32[1024]{0:T(1024)}, u32[]{:S(2)}) copy-start(f32[1024]{0:T(1024)} %param.14) | copy-start | bytes 12292
  97.2 18.2 %all-to-all-start.1 = ((bf16[32,64,128]{2,1,0:T(8,128)(2,1)}), bf16[32,64,128]{2,1,0:T(8,128)(2,1)S(1)}, u32[]{:S(2)}, u32[]{:S(2)}) async-start(bf16[32,64,128]{2,1,0:T(8,128)(2,1)} %attend_last.1), calls=%async_computation.1 | async-start | bytes 1048576 | tf_op jit(solution)/shard_map/all_to_all | solution.py:460
  115.9 14.3 %collective-permute-start.10 = (bf16[128,2048]{1,0:T(8,128)(2,1)S(1)}, bf16[128,2048]{1,0:T(8,128)(2,1)S(1)}, u32[]{:S(2)}, u32[]{:S(2)}) collective-permute-start(bf16[128,2048]{1,0:T(8,128)(2,1)S(1)} %normalized.1.refs_5_), channel_id=1, source_target_pairs={{0,1},{1,2},{2,3},{3,0},{4,5},{5,6},{6,7},{7,4},{8,9},{9,10},{10,1... | collective-permute-start | bytes 1572872 | tf_op jit(solution)/shard_map/ppermute | solution.py:423
  116.2 15.0 %collective-permute-start.9 = (bf16[128,2048]{1,0:T(8,128)(2,1)S(1)}, bf16[128,2048]{1,0:T(8,128)(2,1)S(1)}, u32[]{:S(2)}, u32[]{:S(2)}) collective-permute-start(bf16[128,2048]{1,0:T(8,128)(2,1)S(1)} %normalized.1.refs_5_), channel_id=1, source_target_pairs={{0,4},{1,5},{2,6},{3,7},{4,0},{5,1},{6,2},{7,3},{8,12},{9,13},{10,... | collective-permute-start | bytes 1572872 | tf_op jit(solution)/shard_map/ppermute | solution.py:423
  116.8 15.7 %collective-permute-start.2 = (f32[1,1024]{1,0:T(1,128)S(1)}, f32[1,1024]{1,0:T(1,128)S(1)}, u32[]{:S(2)}, u32[]{:S(2)}) collective-permute-start(f32[1,1024]{1,0:T(1,128)S(1)} %bitcast.43), channel_id=1, source_target_pairs={{0,8},{1,9},{2,10},{3,11},{4,12},{5,13},{6,14},{7,15},{8,0},{9,1},... | collective-permute-start | bytes 12296 | tf_op jit(solution)/shard_map/ppermute | solution.py:423
  118.6 29.0 %collective-permute-start.11 = (bf16[128,2048]{1,0:T(8,128)(2,1)S(1)}, bf16[128,2048]{1,0:T(8,128)(2,1)S(1)}, u32[]{:S(2)}, u32[]{:S(2)}) collective-permute-start(bf16[128,2048]{1,0:T(8,128)(2,1)S(1)} %normalized.1.refs_5_), channel_id=1, source_target_pairs={{0,3},{1,0},{2,1},{3,2},{4,7},{5,4},{6,5},{7,6},{8,11},{9,8},{10,9... | collective-permute-start | bytes 1572872 | tf_op jit(solution)/shard_map/ppermute | solution.py:423
  130.2 12.2 %collective-permute-start.12 = (bf16[128,2048]{1,0:T(8,128)(2,1)S(1)}, bf16[128,2048]{1,0:T(8,128)(2,1)S(1)}, u32[]{:S(2)}, u32[]{:S(2)}) collective-permute-start(bf16[128,2048]{1,0:T(8,128)(2,1)S(1)} %collective-permute-done.10.refs_6_), channel_id=1, source_target_pairs={{0,4},{1,5},{2,6},{3,7},{4,0},{5,1},{6,2},{7,3},{8,12},{9,13},{10,... | collective-permute-start | bytes 1572872 | tf_op jit(solution)/shard_map/ppermute | solution.py:423
  131.3 12.3 %collective-permute-start.14 = (bf16[128,2048]{1,0:T(8,128)(2,1)S(1)}, bf16[128,2048]{1,0:T(8,128)(2,1)S(1)}, u32[]{:S(2)}, u32[]{:S(2)}) collective-permute-start(bf16[128,2048]{1,0:T(8,128)(2,1)S(1)} %collective-permute-done.9.refs_5_), channel_id=1, source_target_pairs={{0,3},{1,0},{2,1},{3,2},{4,7},{5,4},{6,5},{7,6},{8,11},{9,8},{10,9... | collective-permute-start | bytes 1572872 | tf_op jit(solution)/shard_map/ppermute | solution.py:423
  132.6 25.1 %collective-permute-start.13 = (bf16[128,2048]{1,0:T(8,128)(2,1)S(1)}, bf16[128,2048]{1,0:T(8,128)(2,1)S(1)}, u32[]{:S(2)}, u32[]{:S(2)}) collective-permute-start(bf16[128,2048]{1,0:T(8,128)(2,1)S(1)} %collective-permute-done.10.refs_6_), channel_id=1, source_target_pairs={{0,1},{1,2},{2,3},{3,0},{4,5},{5,6},{6,7},{7,4},{8,9},{9,10},{10,1... | collective-permute-start | bytes 1572872 | tf_op jit(solution)/shard_map/ppermute | solution.py:423
  142.4 28.9 %collective-permute-start.15 = (bf16[64,2048]{1,0:T(8,128)(2,1)S(1)}, bf16[64,2048]{1,0:T(8,128)(2,1)S(1)}, u32[]{:S(2)}, u32[]{:S(2)}) collective-permute-start(bf16[64,2048]{1,0:T(8,128)(2,1)S(1)} %slice.88), channel_id=1, source_target_pairs={{0,1},{1,2},{2,3},{3,0},{4,5},{5,6},{6,7},{7,4},{8,9},{9,10},{10,1... | collective-permute-start | bytes 786440 | tf_op jit(solution)/shard_map/ppermute | solution.py:423
  143.6 27.8 %collective-permute-start.16 = (bf16[64,2048]{1,0:T(8,128)(2,1)S(1)}, bf16[64,2048]{1,0:T(8,128)(2,1)S(1)}, u32[]{:S(2)}, u32[]{:S(2)}) collective-permute-start(bf16[64,2048]{1,0:T(8,128)(2,1)S(1)} %slice.89), channel_id=1, source_target_pairs={{0,3},{1,0},{2,1},{3,2},{4,7},{5,4},{6,5},{7,6},{8,11},{9,8},{10,9... | collective-permute-start | bytes 786440 | tf_op jit(solution)/shard_map/ppermute | solution.py:423
  147.6 2.2 copy-start
  177.9 12.5 %all-to-all-start.2 = ((f32[16,2,2,1024]{3,2,1,0:T(2,128)}), f32[16,2,2,1024]{3,2,1,0:T(2,128)S(1)}, u32[]{:S(2)}, u32[]{:S(2)}) async-start(f32[16,2,2,1024]{3,2,1,0:T(2,128)} %broadcast_in_dim.2), calls=%async_computation.2 | async-start | bytes 524288 | tf_op jit(solution)/shard_map/all_to_all | solution.py:488
  190.7 2.2 copy-start.1
  192.8 1.2 copy-start.5
  194.1 5.6 %copy-start.7 = (f32[384,2048]{1,0:T(8,128)S(1)}, f32[384,2048]{1,0:T(8,128)}, u32[]{:S(2)}) copy-start(f32[384,2048]{1,0:T(8,128)} %get-tuple-element.33.refs_0_) | copy-start | bytes 9437188
  199.6 10.0 %collective-permute-start.17 = (bf16[64,2048]{1,0:T(8,128)(2,1)S(1)}, bf16[64,2048]{1,0:T(8,128)(2,1)S(1)}, u32[]{:S(2)}, u32[]{:S(2)}) collective-permute-start(bf16[64,2048]{1,0:T(8,128)(2,1)S(1)} %get-tuple-element.36), channel_id=1, source_target_pairs={{0,1},{1,2},{2,3},{3,0},{4,5},{5,6},{6,7},{7,4},{8,9},{9,10},{10,1... | collective-permute-start | bytes 786440 | tf_op jit(solution)/shard_map/ppermute | solution.py:423
  206.1 10.0 %collective-permute-start.20 = (bf16[64,2048]{1,0:T(8,128)(2,1)S(1)}, bf16[64,2048]{1,0:T(8,128)(2,1)S(1)}, u32[]{:S(2)}, u32[]{:S(2)}) collective-permute-start(bf16[64,2048]{1,0:T(8,128)(2,1)S(1)} %get-tuple-element.39), channel_id=1, source_target_pairs={{0,3},{1,0},{2,1},{3,2},{4,7},{5,4},{6,5},{7,6},{8,11},{9,8},{10,9... | collective-permute-start | bytes 786440 | tf_op jit(solution)/shard_map/ppermute | solution.py:423
  209.4 7.6 %copy-start.6 = (f32[384,2048]{1,0:T(8,128)S(1)}, f32[384,2048]{1,0:T(8,128)}, u32[]{:S(2)}) copy-start(f32[384,2048]{1,0:T(8,128)} %get-tuple-element.31.refs_0_) | copy-start | bytes 9437188
  209.4 16.8 %collective-permute-start.22 = (bf16[128,2048]{1,0:T(8,128)(2,1)S(1)}, bf16[128,2048]{1,0:T(8,128)(2,1)S(1)}, u32[]{:S(2)}, u32[]{:S(2)}) collective-permute-start(bf16[128,2048]{1,0:T(8,128)(2,1)S(1)} %get-tuple-element.40), channel_id=1, source_target_pairs={{0,3},{1,0},{2,1},{3,2},{4,7},{5,4},{6,5},{7,6},{8,11},{9,8},{10,9... | collective-permute-start | bytes 1572872 | tf_op jit(solution)/shard_map/ppermute | solution.py:423
  209.6 14.7 %collective-permute-start.18 = (bf16[128,2048]{1,0:T(8,128)(2,1)S(1)}, bf16[128,2048]{1,0:T(8,128)(2,1)S(1)}, u32[]{:S(2)}, u32[]{:S(2)}) collective-permute-start(bf16[128,2048]{1,0:T(8,128)(2,1)S(1)} %pad_maximum_fusion.1), channel_id=1, source_target_pairs={{0,1},{1,2},{2,3},{3,0},{4,5},{5,6},{6,7},{7,4},{8,9},{9,10},{10,1... | collective-permute-start | bytes 1572872 | tf_op jit(solution)/shard_map/ppermute | solution.py:423
  216.2 14.0 %collective-permute-start.21 = (bf16[128,2048]{1,0:T(8,128)(2,1)S(1)}, bf16[128,2048]{1,0:T(8,128)(2,1)S(1)}, u32[]{:S(2)}, u32[]{:S(2)}) collective-permute-start(bf16[128,2048]{1,0:T(8,128)(2,1)S(1)} %pad_maximum_fusion.2), channel_id=1, source_target_pairs={{0,4},{1,5},{2,6},{3,7},{4,0},{5,1},{6,2},{7,3},{8,12},{9,13},{10,... | collective-permute-start | bytes 1572872 | tf_op jit(solution)/shard_map/ppermute | solution.py:423
  223.5 12.2 %copy-start.4 = (f32[128,2048]{1,0:T(8,128)S(1)}, f32[128,2048]{1,0:T(8,128)}, u32[]{:S(2)}) copy-start(f32[128,2048]{1,0:T(8,128)} %get-tuple-element.30.refs_0_) | copy-start | bytes 3145732
  223.5 17.6 %collective-permute-start.24 = (bf16[128,2048]{1,0:T(8,128)(2,1)S(1)}, bf16[128,2048]{1,0:T(8,128)(2,1)S(1)}, u32[]{:S(2)}, u32[]{:S(2)}) collective-permute-start(bf16[128,2048]{1,0:T(8,128)(2,1)S(1)} %get-tuple-element.41), channel_id=1, source_target_pairs={{0,1},{1,2},{2,3},{3,0},{4,5},{5,6},{6,7},{7,4},{8,9},{9,10},{10,1... | collective-permute-start | bytes 1572872 | tf_op jit(solution)/shard_map/ppermute | solution.py:423
  224.5 16.6 %collective-permute-start.19 = (bf16[128,2048]{1,0:T(8,128)(2,1)S(1)}, bf16[128,2048]{1,0:T(8,128)(2,1)S(1)}, u32[]{:S(2)}, u32[]{:S(2)}) collective-permute-start(bf16[128,2048]{1,0:T(8,128)(2,1)S(1)} %add_convert_fusion.2), channel_id=1, source_target_pairs={{0,4},{1,5},{2,6},{3,7},{4,0},{5,1},{6,2},{7,3},{8,12},{9,13},{10,... | collective-permute-start | bytes 1572872 | tf_op jit(solution)/shard_map/ppermute | solution.py:423
  230.4 11.4 %collective-permute-start.23 = (bf16[128,2048]{1,0:T(8,128)(2,1)S(1)}, bf16[128,2048]{1,0:T(8,128)(2,1)S(1)}, u32[]{:S(2)}, u32[]{:S(2)}) collective-permute-start(bf16[128,2048]{1,0:T(8,128)(2,1)S(1)} %add_convert_fusion.1), channel_id=1, source_target_pairs={{0,3},{1,0},{2,1},{3,2},{4,7},{5,4},{6,5},{7,6},{8,11},{9,8},{10,9... | collective-permute-start | bytes 1572872 | tf_op jit(solution)/shard_map/ppermute | solution.py:423

commit v2 on v1

--- a/solution.py
+++ b/solution.py
@@ -69,11 +69,8 @@
     y_at, y_size = lax.axis_index("y"), lax.axis_size("y")
     queries_real = length - y_at * depth > step * rows
 
-    def piece(n, at, count, masked):
+    def piece(n, at, count, masked, top, summed):
         query = q_ref[pl.ds(at // 64, sub // 64)].reshape(sub, HEAD_DIM)
-        where = pl.ds(at, sub)
-        top = top_ref[where, :1]
-        summed = sum_ref[where, :]
         for start in range(0, depth, part):
             key = held[n, start : start + part]
             scores = lax.dot_general(
@@ -82,29 +79,42 @@
             if masked:
                 place = lax.broadcasted_iota(jnp.int32, scores.shape, 1) + start
                 scores = jnp.where(place < count, scores, LOW)
-            new_top = jnp.maximum(top, jnp.max(scores, axis=1, keepdims=True))
+            new_top = jnp.max(scores, axis=1, keepdims=True)
+            if top is not None:
+                new_top = jnp.maximum(top, new_top)
             weights = jnp.exp2((scores - new_top) * scale)
             added = jnp.dot(
                 weights.astype(jnp.bfloat16),
                 wide[n, start : start + part],
                 preferred_element_type=jnp.float32,
             )
-            summed = summed * jnp.exp2((top - new_top) * scale) + added
-            top = new_top
-        top_ref[where, :] = jnp.broadcast_to(top, (sub, HEAD_DIM))
-        sum_ref[where, :] = summed
+            if top is not None:
+                added = summed * jnp.exp2((top - new_top) * scale) + added
+            top, summed = new_top, added
+        return top, summed
+
+    def before(at):
+        return (None, None) if first else (top_ref[pl.ds(at, sub), :1], sum_ref[pl.ds(at, sub), :])
+
+    def after(at, top, summed):
+        top_ref[pl.ds(at, sub), :] = jnp.broadcast_to(top, (sub, HEAD_DIM))
+        sum_ref[pl.ds(at, sub), :] = summed
 
     def attend(n, count, masked):
         if masked:
 
             def one(index, carry):
-                piece(n, pl.multiple_of(index * sub, sub), count, True)
+                at = pl.multiple_of(index * sub, sub)
+                after(at, *piece(n, at, count, True, *before(at)))
                 return carry
 
             lax.fori_loop(0, rows // sub, one, 0)
         else:
-            for at in range(0, rows, sub):
-                piece(n, at, count, False)
+            places = range(0, rows, sub)
+            running = [before(at) for at in places]
+            done = [piece(n, at, count, False, *run) for at, run in zip(places, running)]
+            for at, run in zip(places, done):
+                after(at, *run)
 
     def chunk(n, carry):
         turn = turns[0] + n * (turns[-1] - turns[0])
@@ -203,22 +213,10 @@
     )(lengths, *operands)
 
 
-def logits_kernel(blocks, places, lengths, own_hbm, near_hbm, far_hbm, bias_ref, *refs):
+def logits_kernel(blocks, places, cols, lengths, own_ref, near_ref, far_ref, bias_ref, *refs):
     rows_in = refs[:blocks]
-    slope_ref, total_ref, rows_ref, held, sems = refs[blocks:]
+    slope_ref, total_ref, rows_ref, logits_ref = refs[blocks:]
     step = pl.program_id(0)
-    cols = held.shape[2]
-
-    tile_sources = []
-    for source in (own_hbm, near_hbm, far_hbm):
-        tile_sources += [(source, at) for at in range(0, source.shape[1], cols)]
-
-    @pl.when(step == 0)
-    def _():
-        for n, (source, at) in enumerate(tile_sources):
-            pltpu.make_async_copy(
-                source.at[:, at : at + cols], held.at[n], sems.at[n]
-            ).start()
 
     @pl.when(step == 0)
     def _():
@@ -227,8 +225,19 @@
             rows_ref[pl.ds(at, ref.shape[0]), :] = ref[...]
             at += ref.shape[0]
 
-    pltpu.make_async_copy(own_hbm.at[:, pl.ds(0, cols)], held.at[step], sems.at[step]).wait()
-    logits = jnp.dot(rows_ref[...], held[step], preferred_element_type=jnp.float32) + bias_ref[...]
+    first = 0
+    for ref in (own_ref, near_ref, far_ref):
+        tiles = ref.shape[1] // cols
+
+        @pl.when(jnp.logical_and(step >= first, step < first + tiles))
+        def _():
+            where = pl.ds(pl.multiple_of((step - first) * cols, cols), cols)
+            logits_ref[...] = jnp.dot(
+                rows_ref[...], ref[:, where], preferred_element_type=jnp.float32
+            )
+
+        first += tiles
+    logits = logits_ref[...] + bias_ref[...]
     tokens = 64
     y_at, c_at, u_at, w_at, z_at = [lax.axis_index(axis) for axis in AXES]
     _, c_size, u_size, w_size, z_size = [lax.axis_size(axis) for axis in AXES]
@@ -262,14 +271,14 @@
     tiles = entries // cols
 
     def body(*refs):
-        logits_kernel(len(blocks), places, *refs)
+        logits_kernel(len(blocks), places, cols, *refs)
 
     return pl.pallas_call(
         body,
         grid_spec=pltpu.PrefetchScalarGridSpec(
             num_scalar_prefetch=1,
             grid=(tiles,),
-            in_specs=[pl.BlockSpec(memory_space=pltpu.HBM)] * 3
+            in_specs=[pl.BlockSpec(memory_space=pltpu.VMEM)] * 3
             + [pl.BlockSpec((1, cols), lambda j, counts: (0, j))]
             + [pl.BlockSpec(b.shape, lambda j, counts: (0, 0)) for b in blocks],
             out_specs=[
@@ -278,8 +287,7 @@
             ],
             scratch_shapes=[
                 pltpu.VMEM((rows, width), jnp.bfloat16),
-                pltpu.VMEM((tiles, width, cols), jnp.bfloat16),
-                pltpu.SemaphoreType.DMA((tiles,)),
+                pltpu.VMEM((rows, cols), jnp.float32),
             ],
         ),
         out_shape=[
@@ -365,7 +373,11 @@
         ),
         compiler_params=pltpu.CompilerParams(vmem_limit_bytes=28 << 20),
         name="gradient",
-    )(slope, coefficient, *weights)
+    )(
+        pltpu.with_memory_space_constraint(slope, pltpu.HBM),
+        coefficient,
+        *[pltpu.with_memory_space_constraint(w, pltpu.HBM) for w in weights],
+    )
 
 
 def norm_kernel(docs, heads, back_ref, residual_ref, gain_ref, out_ref):
@@ -411,8 +423,8 @@
     tokens, docs, width = queries.shape
     heads = width // HEAD_DIM
     sizes = [lax.axis_size(axis) for axis in AXES]
-    y_size, c_size, u_size, _, _ = sizes
-    _, c_at, u_at, _, _ = [lax.axis_index(axis) for axis in AXES]
+    y_size, c_size, _, _, _ = sizes
+    _, c_at, _, _, _ = [lax.axis_index(axis) for axis in AXES]
 
     def by_head(array):
         return jnp.transpose(array.reshape(tokens, docs, heads, HEAD_DIM), (1, 2, 0, 3)).reshape(
@@ -480,19 +492,17 @@
         sums = sums + part
 
     own_sums, other_sums = sums[:, :entries], in_halves(sums[:, entries:])
-    ordered = jnp.where(
-        u_at == 0, jnp.stack([own_sums, other_sums]), jnp.stack([other_sums, own_sums])
-    )
-    peers = y_size * c_size * u_size
+    ordered = jnp.concatenate([own_sums, other_sums], axis=0)
+    swapped = move(jnp.concatenate([other_sums, own_sums], axis=0), u=1)
+    ordered = ordered + swapped
+    peers = y_size * c_size
     spread = jnp.broadcast_to(ordered[None], (peers,) + ordered.shape)
-    gathered = lax.all_to_all(spread, ("y", "c", "u"), split_axis=0, concat_axis=0, tiled=True)
-    totals = jnp.sum(gathered, axis=0)
+    gathered = lax.all_to_all(spread, ("y", "c"), split_axis=0, concat_axis=0, tiled=True)
+    totals = jnp.sum(gathered, axis=0).reshape(2, docs, entries)
     pooled = jnp.log(totals / doc_lengths[None, :, None].astype(jnp.float32)) / sharpness
     coefficient = 2.0 * flops_weight / docs * jnp.mean(pooled, axis=1)[:, None, :] / totals
-    own_pooled = jnp.where(u_at == 0, pooled[0], pooled[1])
-    own_coef = jnp.where(u_at == 0, coefficient[0], coefficient[1])
-    other_coef = in_halves(jnp.where(u_at == 0, coefficient[1], coefficient[0]))
-    coef = jnp.concatenate([own_coef, other_coef], axis=1)
+    own_pooled = pooled[0]
+    coef = jnp.concatenate([coefficient[0], in_halves(coefficient[1])], axis=1)
 
     block = docs * tokens
 

time: 244 us -> 253 us (1.037)
  Pallas kernels: 94.9 us -> 106 us
  local copies, waits for them, and re-layouts: 13.9 us -> 11 us
    pallas_call x4, Pallas kernels: 27.2 us -> 35.4 us  [boost(): pl.pallas_call(body, grid_spec=pltpu.PrefetchScalarGridSpec(num_scalar_pr...]
    pallas_call x4, Pallas kernels: 23.7 us -> 30.2 us  [gradient(): pl.pallas_call(body, grid=(width // cols,), in_specs=[pl.BlockSpec((rows,...]
    unnamed x25 -> x15, local copies, waits for them, and re-layouts: 5.79 us -> 2.37 us
    pallas_call x3, Pallas kernels: 43.5 us -> 40.3 us  [attend_chunks(): pl.pallas_call(body, grid_spec=pltpu.PrefetchScalarGridSpec(num_scalar_pr...]
    all_to_all x1, waiting for transfers between devices: 8.9 us -> 6.02 us  [local(): lax.all_to_all(spread, ('y', 'c'), split_axis=0, concat_axis=0, tiled=True)]
    ppermute x25 -> x26, waiting for transfers between devices: 36.1 us -> 39 us  [move(): return lax.ppermute(array, AXES, shift_perm(sizes, **by))]
    ppermute x25 -> x26, starting transfers between devices: 38.7 us -> 40 us  [move(): return lax.ppermute(array, AXES, shift_perm(sizes, **by))]
  transfers between devices with their start and end apart: 28 -> 29, of which waited for: 13 -> 12; matrix products, arithmetic and copies ran while one was open for 2% -> 2% of each run, Pallas kernels for 34% -> 36%
where the time goes in v2:
time: 253 us
  Pallas kernels  106 us (42%)
  waiting for transfers between devices  73.6 us (29%)
  starting transfers between devices  58.1 us (23%)
  local copies, waits for them, and re-layouts  11 us (4%)
    pallas_call x3, Pallas kernels, attend_chunks(): pl.pallas_call(body, grid_spec=pltpu.PrefetchScalarGridSpec(num_scalar_pr...  40.3 us
    ppermute x26, starting transfers between devices, move(): return lax.ppermute(array, AXES, shift_perm(sizes, **by))  40 us
    ppermute x26, waiting for transfers between devices, move(): return lax.ppermute(array, AXES, shift_perm(sizes, **by))  39 us
    pallas_call x4, Pallas kernels, boost(): pl.pallas_call(body, grid_spec=pltpu.PrefetchScalarGridSpec(num_scalar_pr...  35.4 us
    pallas_call x4, Pallas kernels, gradient(): pl.pallas_call(body, grid=(width // cols,), in_specs=[pl.BlockSpec((rows,...  30.2 us
    all_to_all x1, waiting for transfers between devices, local(): lax.all_to_all(stacked, PLANE, split_axis=0, concat_axis=0, tiled=True)  16.8 us
    all_to_all x1, waiting for transfers between devices, local(): lax.all_to_all(attended, PLANE, split_axis=0, concat_axis=0, tiled=True)  11.8 us
    all_to_all x1, starting transfers between devices, local(): lax.all_to_all(stacked, PLANE, split_axis=0, concat_axis=0, tiled=True)  8.28 us
  transfers between devices with their start and end apart: 29, of which 12 were waited for; matrix products, arithmetic and copies ran while one was open for 2% of the time, Pallas kernels for 36%

profile of v2, /device:TPU:0, one launch (start us, length us, event | category | flops | bytes accessed | tf_op | source)
XLA Modules:
  0.0 252.6 jit_solution(8304612249077289993)
XLA Ops:
  0.6 1.5 reshape.34
  2.1 0.2 copy.34
  2.3 0.3 reshape.35
  2.7 0.2 copy.35
  2.9 0.3 reshape.36
  3.2 0.2 copy.36
  3.5 1.3 pad_maximum_fusion
  4.8 8.3 %all-to-all-start = ((bf16[32,3,64,128]{3,2,1,0:T(8,128)(2,1)}), bf16[32,3,64,128]{3,2,1,0:T(8,128)(2,1)S(1)}, u32[]{:S(2)}, u32[]{:S(2)}) async-start(bf16[32,3,64,128]{3,2,1,0:T(8,128)(2,1)} %pad_maximum_fusion), calls=%async_computation | async-start | bytes 3145728 | tf_op jit(solution)/shard_map/all_to_all | solution.py:438
  13.1 3.1 %constant_dynamic-slice_fusion = bf16[2048,512]{1,0:T(8,128)(2,1)} fusion(bf16[2048,1024]{1,0:T(8,128)(2,1)} %refs_2_.7, s32[]{:T(128)S(6)} %select_n.23), kind=kLoop, calls=%fused_computation.26 | loop fusion | bytes 4194308 | tf_op jit(solution)/shard_map/dynamic_slice | solution.py:449
  16.1 3.3 %collective-permute-start = (bf16[2048,512]{1,0:T(8,128)(2,1)}, bf16[2048,512]{1,0:T(8,128)(2,1)}, u32[]{:S(2)}, u32[]{:S(2)}) collective-permute-start(bf16[2048,512]{1,0:T(8,128)(2,1)} %constant_dynamic-slice_fusion), channel_id=1, source_target_pairs={{0,8},{1,9},{2,10},{3,11},{4,12},{5,13},{6,14},{7,15},{8,0},{9,1},... | collective-permute-start | bytes 6291464 | tf_op jit(solution)/shard_map/ppermute | solution.py:435
  19.4 16.8 %all-to-all-done.refs_1_.refs_2_.refs_3_ = bf16[32,3,64,128]{3,2,1,0:T(8,128)(2,1)S(1)} async-done(((bf16[32,3,64,128]{3,2,1,0:T(8,128)(2,1)}), bf16[32,3,64,128]{3,2,1,0:T(8,128)(2,1)S(1)}, u32[]{:S(2)}, u32[]{:S(2)}) %all-to-all-start) | async-done | bytes 1572896 | tf_op jit(solution)/shard_map/all_to_all | solution.py:438
  36.4 1.6 collective-permute-start.3
  38.0 1.7 collective-permute-start.5
  39.7 0.4 collective-permute-start.7
  40.0 2.9 %collective-permute-start.8 = (bf16[32,64,128]{2,1,0:T(8,128)(2,1)S(1)}, bf16[32,64,128]{2,1,0:T(8,128)(2,1)S(1)}, u32[]{:S(2)}, u32[]{:S(2)}) collective-permute-start(bf16[32,64,128]{2,1,0:T(8,128)(2,1)S(1)} %get-tuple-element.45), channel_id=1, source_target_pairs={{0,96},{1,97},{2,98},{3,99},{4,100},{5,101},{6,102},{7,103},{8,104... | collective-permute-start | bytes 1572872 | tf_op jit(solution)/shard_map/ppermute | solution.py:435
  42.9 7.5 %attend_first.1 = (f32[2048,128]{1,0:T(8,128)S(1)}, f32[2048,256]{1,0:T(8,128)S(1)}) custom-call(s32[2]{0:T(128)S(1)} %copy-done.2, bf16[32,3,64,128]{3,2,1,0:T(8,128)(2,1)S(1)} %all-to-all-done.refs_1_.refs_2_.refs_3_, bf16[32,3,64,128]{3,2,1,0:T(8,128)(2,1)S(1)} %all-to-all-done.refs_1_.refs_2_.refs_3_, ...), custom_call_target="tpu_custom_call" | custom-call | flops 4294967296 | bytes 4194304 | tf_op jit(solution)/shard_map/attend_first/pallas_call | solution.py:196
  50.4 2.0 collective-permute-done.3.refs_2_
  52.4 0.4 collective-permute-start.4
  52.8 2.9 %collective-permute-start.6 = (bf16[32,64,128]{2,1,0:T(8,128)(2,1)S(1)}, bf16[32,64,128]{2,1,0:T(8,128)(2,1)S(1)}, u32[]{:S(2)}, u32[]{:S(2)}) collective-permute-start(bf16[32,64,128]{2,1,0:T(8,128)(2,1)S(1)} %collective-permute-done.5.refs_5_), channel_id=1, source_target_pairs={{0,96},{1,97},{2,98},{3,99},{4,100},{5,101},{6,102},{7,103},{8,104... | collective-permute-start | bytes 1572872 | tf_op jit(solution)/shard_map/ppermute | solution.py:435
  55.7 8.0 %collective-permute-done.7.refs_3_ = bf16[32,64,128]{2,1,0:T(8,128)(2,1)S(1)} collective-permute-done((bf16[32,64,128]{2,1,0:T(8,128)(2,1)S(1)}, bf16[32,64,128]{2,1,0:T(8,128)(2,1)S(1)}, u32[]{:S(2)}, u32[]{:S(2)}) %collective-permute-start.7) | collective-permute-done | bytes 524320 | tf_op jit(solution)/shard_map/ppermute | solution.py:435
  63.7 0.4 collective-permute-done.8.refs_4_
  64.0 21.7 %attend_next.1 = (f32[2048,128]{1,0:T(8,128)S(1)}, f32[2048,256]{1,0:T(8,128)S(1)}) custom-call(s32[2]{0:T(128)S(1)} %copy-done.2, bf16[32,3,64,128]{3,2,1,0:T(8,128)(2,1)S(1)} %all-to-all-done.refs_1_.refs_2_.refs_3_, bf16[32,64,128]{2,1,0:T(8,128)(2,1)S(1)} %collective-permute-done.3.refs_2_, bf16[32,64,128]{2,1,0:T(8,128)(2,1)S(1)} %collective-permute-done.7.refs_3_, ...), custom_call_target="tpu_custom_call" | custom-call | flops 8589934592 | bytes 4194304 | tf_op jit(solution)/shard_map/attend_next/pallas_call | solution.py:196
  85.8 0.3 collective-permute-start.1
  86.1 11.1 %attend_last.1 = bf16[32,64,128]{2,1,0:T(8,128)(2,1)} custom-call(s32[2]{0:T(128)S(1)} %copy-done.2, bf16[32,3,64,128]{3,2,1,0:T(8,128)(2,1)S(1)} %all-to-all-done.refs_1_.refs_2_.refs_3_, bf16[32,64,128]{2,1,0:T(8,128)(2,1)S(1)} %collective-permute-done.4.refs_2_, bf16[32,64,128]{2,1,0:T(8,128)(2,1)S(1)} %collective-permute-done.6.refs_3_, ...), custom_call_target="tpu_custom_call" | custom-call | flops 4294967296 | bytes 4194304 | tf_op jit(solution)/shard_map/attend_last/pallas_call | solution.py:196
  97.1 6.4 %all-to-all-start.1 = ((bf16[32,64,128]{2,1,0:T(8,128)(2,1)}), bf16[32,64,128]{2,1,0:T(8,128)(2,1)S(1)}, u32[]{:S(2)}, u32[]{:S(2)}) async-start(bf16[32,64,128]{2,1,0:T(8,128)(2,1)} %attend_last.1), calls=%async_computation.1 | async-start | bytes 1048576 | tf_op jit(solution)/shard_map/all_to_all | solution.py:472
  103.6 0.2 copy.48
  103.7 11.8 %all-to-all-done.1.refs_0_ = bf16[32,64,128]{2,1,0:T(8,128)(2,1)S(1)} async-done(((bf16[32,64,128]{2,1,0:T(8,128)(2,1)}), bf16[32,64,128]{2,1,0:T(8,128)(2,1)S(1)}, u32[]{:S(2)}, u32[]{:S(2)}) %all-to-all-start.1) | async-done | bytes 524320 | tf_op jit(solution)/shard_map/all_to_all | solution.py:472
  115.5 0.4 normalized.1.refs_5_
  116.0 0.3 collective-permute-start.10
  116.3 0.6 collective-permute-start.9
  116.9 1.8 collective-permute-start.2
  118.7 3.1 %collective-permute-start.11 = (bf16[128,2048]{1,0:T(8,128)(2,1)S(1)}, bf16[128,2048]{1,0:T(8,128)(2,1)S(1)}, u32[]{:S(2)}, u32[]{:S(2)}) collective-permute-start(bf16[128,2048]{1,0:T(8,128)(2,1)S(1)} %normalized.1.refs_5_), channel_id=1, source_target_pairs={{0,3},{1,0},{2,1},{3,2},{4,7},{5,4},{6,5},{7,6},{8,11},{9,8},{10,9... | collective-permute-start | bytes 1572872 | tf_op jit(solution)/shard_map/ppermute | solution.py:435
  121.8 8.5 %collective-permute-done.10.refs_6_ = bf16[128,2048]{1,0:T(8,128)(2,1)S(1)} collective-permute-done((bf16[128,2048]{1,0:T(8,128)(2,1)S(1)}, bf16[128,2048]{1,0:T(8,128)(2,1)S(1)}, u32[]{:S(2)}, u32[]{:S(2)}) %collective-permute-start.10) | collective-permute-done | bytes 524320 | tf_op jit(solution)/shard_map/ppermute | solution.py:435
  130.3 1.0 collective-permute-start.12
  131.3 1.3 collective-permute-start.14
  132.7 0.8 collective-permute-start.13
  133.5 9.0 %collective-permute-done.12.refs_5_ = bf16[128,2048]{1,0:T(8,128)(2,1)S(1)} collective-permute-done((bf16[128,2048]{1,0:T(8,128)(2,1)S(1)}, bf16[128,2048]{1,0:T(8,128)(2,1)S(1)}, u32[]{:S(2)}, u32[]{:S(2)}) %collective-permute-start.12) | collective-permute-done | bytes 524320 | tf_op jit(solution)/shard_map/ppermute | solution.py:435
  142.5 0.8 collective-permute-start.15
  143.3 0.4 collective-permute-done.14.refs_7_
  143.7 4.0 %collective-permute-start.16 = (bf16[64,2048]{1,0:T(8,128)(2,1)S(1)}, bf16[64,2048]{1,0:T(8,128)(2,1)S(1)}, u32[]{:S(2)}, u32[]{:S(2)}) collective-permute-start(bf16[64,2048]{1,0:T(8,128)(2,1)S(1)} %slice.83), channel_id=1, source_target_pairs={{0,3},{1,0},{2,1},{3,2},{4,7},{5,4},{6,5},{7,6},{8,11},{9,8},{10,9... | collective-permute-start | bytes 786440 | tf_op jit(solution)/shard_map/ppermute | solution.py:435
  147.7 2.2 copy-done
  149.9 10.2 %boost.5 = (f32[384,2048]{1,0:T(8,128)}, f32[2,2048]{1,0:T(2,128)S(1)}) custom-call(s32[2]{0:T(128)S(1)} %copy-done.2, bf16[2048,1024]{1,0:T(8,128)(2,1)S(1)} %copy-done, bf16[2048,512]{1,0:T(8,128)(2,1)} %collective-permute-done.refs_2_.refs_3_, bf16[2048,512]{1,0:T(8,128)(2,1)} %collective-permute-done.1.refs_3_.refs_4_, ...), custom_call_target="tpu_custom_call" | custom-call | flops 6442450944 | bytes 11534336 | tf_op jit(solution)/shard_map/boost/pallas_call | solution.py:276
  160.0 10.2 %boost.6 = (f32[384,2048]{1,0:T(8,128)}, f32[2,2048]{1,0:T(2,128)S(1)}) custom-call(s32[2]{0:T(128)S(1)} %copy-done.2, bf16[2048,1024]{1,0:T(8,128)(2,1)S(1)} %copy-done, bf16[2048,512]{1,0:T(8,128)(2,1)} %collective-permute-done.refs_2_.refs_3_, bf16[2048,512]{1,0:T(8,128)(2,1)} %collective-permute-done.1.refs_3_.refs_4_, ...), custom_call_target="tpu_custom_call" | custom-call | flops 6442450944 | bytes 11534336 | tf_op jit(solution)/shard_map/boost/pallas_call | solution.py:276
  170.2 7.5 %boost.4 = (f32[128,2048]{1,0:T(8,128)}, f32[2,2048]{1,0:T(2,128)S(1)}) custom-call(s32[2]{0:T(128)S(1)} %copy-done.2, bf16[2048,1024]{1,0:T(8,128)(2,1)S(1)} %copy-done, bf16[2048,512]{1,0:T(8,128)(2,1)} %collective-permute-done.refs_2_.refs_3_, bf16[2048,512]{1,0:T(8,128)(2,1)} %collective-permute-done.1.refs_3_.refs_4_, ...), custom_call_target="tpu_custom_call" | custom-call | flops 4294967296 | bytes 9437184 | tf_op jit(solution)/shard_map/boost/pallas_call | solution.py:276
  177.7 7.5 %boost.7 = (f32[128,2048]{1,0:T(8,128)}, f32[2,2048]{1,0:T(2,128)S(1)}) custom-call(s32[2]{0:T(128)S(1)} %copy-done.2, bf16[2048,1024]{1,0:T(8,128)(2,1)S(1)} %copy-done, bf16[2048,512]{1,0:T(8,128)(2,1)} %collective-permute-done.refs_2_.refs_3_, bf16[2048,512]{1,0:T(8,128)(2,1)} %collective-permute-done.1.refs_3_.refs_4_, ...), custom_call_target="tpu_custom_call" | custom-call | flops 4294967296 | bytes 9437184 | tf_op jit(solution)/shard_map/boost/pallas_call | solution.py:276
  185.3 1.2 collective-permute-start.17
  186.6 4.1 %collective-permute-done.17 = f32[4,1024]{1,0:T(4,128)S(1)} collective-permute-done((f32[4,1024]{1,0:T(4,128)S(1)}, f32[4,1024]{1,0:T(4,128)S(1)}, u32[]{:S(2)}, u32[]{:S(2)}) %collective-permute-start.17) | collective-permute-done | bytes 16416 | tf_op jit(solution)/shard_map/ppermute | solution.py:435
  190.7 0.7 broadcast_in_dim.2
  191.3 3.4 %all-to-all-start.2 = ((f32[8,4,1024]{2,1,0:T(4,128)}), f32[8,4,1024]{2,1,0:T(4,128)S(1)}, u32[]{:S(2)}, u32[]{:S(2)}) async-start(f32[8,4,1024]{2,1,0:T(4,128)} %broadcast_in_dim.2), calls=%async_computation.2 | async-start | bytes 262144 | tf_op jit(solution)/shard_map/all_to_all | solution.py:500
  194.7 6.0 %all-to-all-done.2 = f32[8,4,1024]{2,1,0:T(4,128)S(1)} async-done(((f32[8,4,1024]{2,1,0:T(4,128)}), f32[8,4,1024]{2,1,0:T(4,128)S(1)}, u32[]{:S(2)}, u32[]{:S(2)}) %all-to-all-start.2) | async-done | bytes 131104 | tf_op jit(solution)/shard_map/all_to_all | solution.py:500
  201.0 6.7 %gradient.7 = (bf16[64,2048]{1,0:T(8,128)(2,1)S(1)}, bf16[64,2048]{1,0:T(8,128)(2,1)S(1)}) custom-call(f32[128,2048]{1,0:T(8,128)} %get-tuple-element.35.refs_0_, f32[2,2048]{1,0:T(2,128)S(1)} %pad_maximum_fusion.4.refs_1_, bf16[2048,1024]{1,0:T(8,128)(2,1)} %refs_2_.7, bf16[2048,512]{1,0:T(8,128)(2,1)} %collective-permute-done.refs_2_.refs_3_, ...), custom_call_target="tpu_custom_call" | custom-call | flops 4294967296 | bytes 9437184 | tf_op jit(solution)/shard_map/gradient/pallas_call | solution.py:354
  207.8 8.4 %gradient.6 = (bf16[128,2048]{1,0:T(8,128)(2,1)S(1)}, bf16[128,2048]{1,0:T(8,128)(2,1)S(1)}, bf16[128,2048]{1,0:T(8,128)(2,1)S(1)}) custom-call(f32[384,2048]{1,0:T(8,128)} %get-tuple-element.33.refs_0_, f32[2,2048]{1,0:T(2,128)S(1)} %pad_maximum_fusion.4.refs_1_, bf16[2048,1024]{1,0:T(8,128)(2,1)} %refs_2_.7, ...), custom_call_target="tpu_custom_call" | custom-call | flops 6442450944 | bytes 11534336 | tf_op jit(solution)/shard_map/gradient/pallas_call | solution.py:354
  216.3 3.3 %collective-permute-start.21 = (bf16[64,2048]{1,0:T(8,128)(2,1)S(1)}, bf16[64,2048]{1,0:T(8,128)(2,1)S(1)}, u32[]{:S(2)}, u32[]{:S(2)}) collective-permute-start(bf16[64,2048]{1,0:T(8,128)(2,1)S(1)} %get-tuple-element.39), channel_id=1, source_target_pairs={{0,3},{1,0},{2,1},{3,2},{4,7},{5,4},{6,5},{7,6},{8,11},{9,8},{10,9... | collective-permute-start | bytes 786440 | tf_op jit(solution)/shard_map/ppermute | solution.py:435
  219.8 2.1 collective-permute-start.19
  221.8 4.4 %collective-permute-done.21 = bf16[64,2048]{1,0:T(8,128)(2,1)S(1)} collective-permute-done((bf16[64,2048]{1,0:T(8,128)(2,1)S(1)}, bf16[64,2048]{1,0:T(8,128)(2,1)S(1)}, u32[]{:S(2)}, u32[]{:S(2)}) %collective-permute-start.21) | collective-permute-done | bytes 262176 | tf_op jit(solution)/shard_map/ppermute | solution.py:435
  226.4 8.4 %gradient.5 = (bf16[128,2048]{1,0:T(8,128)(2,1)S(1)}, bf16[128,2048]{1,0:T(8,128)(2,1)S(1)}, bf16[128,2048]{1,0:T(8,128)(2,1)S(1)}) custom-call(f32[384,2048]{1,0:T(8,128)} %get-tuple-element.31.refs_0_, f32[2,2048]{1,0:T(2,128)S(1)} %pad_maximum_fusion.4.refs_1_, bf16[2048,1024]{1,0:T(8,128)(2,1)} %refs_2_.7, ...), custom_call_target="tpu_custom_call" | custom-call | flops 6442450944 | bytes 11534336 | tf_op jit(solution)/shard_map/gradient/pallas_call | solution.py:354
  235.1 2.1 collective-permute-start.20
  237.2 2.1 collective-permute-done.22
  239.3 0.2 add_convert_fusion.1
  239.6 4.1 %collective-permute-start.24 = (bf16[128,2048]{1,0:T(8,128)(2,1)S(1)}, bf16[128,2048]{1,0:T(8,128)(2,1)S(1)}, u32[]{:S(2)}, u32[]{:S(2)}) collective-permute-start(bf16[128,2048]{1,0:T(8,128)(2,1)S(1)} %add_convert_fusion.1), channel_id=1, source_target_pairs={{0,3},{1,0},{2,1},{3,2},{4,7},{5,4},{6,5},{7,6},{8,11},{9,8},{10,9... | collective-permute-start | bytes 1572872 | tf_op jit(solution)/shard_map/ppermute | solution.py:435
  243.6 0.6 slice_bitcast_fusion.4
  244.2 6.7 %gradient.4 = bf16[128,2048]{1,0:T(8,128)(2,1)S(1)} custom-call(f32[128,2048]{1,0:T(8,128)} %get-tuple-element.30.refs_0_, f32[2,2048]{1,0:T(2,128)S(1)} %pad_maximum_fusion.4.refs_1_, bf16[2048,1024]{1,0:T(8,128)(2,1)} %refs_2_.7, bf16[2048,512]{1,0:T(8,128)(2,1)} %collective-permute-done.refs_2_.refs_3_, ...), custom_call_target="tpu_custom_call" | custom-call | flops 4294967296 | bytes 9437184 | tf_op jit(solution)/shard_map/gradient/pallas_call | solution.py:354
  250.9 0.3 add_convert_fusion
  251.3 1.3 copy.47
  (62 shorter events, 1.2 us)
Async XLA Ops:
  0.6 1.7 copy-start.3
  0.6 2.3 copy-start.4
  4.8 31.5 %all-to-all-start = ((bf16[32,3,64,128]{3,2,1,0:T(8,128)(2,1)}), bf16[32,3,64,128]{3,2,1,0:T(8,128)(2,1)S(1)}, u32[]{:S(2)}, u32[]{:S(2)}) async-start(bf16[32,3,64,128]{3,2,1,0:T(8,128)(2,1)} %pad_maximum_fusion), calls=%async_computation | async-start | bytes 3145728 | tf_op jit(solution)/shard_map/all_to_all | solution.py:438
  16.1 26.8 %copy-start.2 = (s32[2]{0:T(128)S(1)}, s32[2]{0:T(128)}, u32[]{:S(2)}) copy-start(s32[2]{0:T(128)} %refs_0_.13) | copy-start | bytes 28
  16.1 69.6 %collective-permute-start = (bf16[2048,512]{1,0:T(8,128)(2,1)}, bf16[2048,512]{1,0:T(8,128)(2,1)}, u32[]{:S(2)}, u32[]{:S(2)}) collective-permute-start(bf16[2048,512]{1,0:T(8,128)(2,1)} %constant_dynamic-slice_fusion), channel_id=1, source_target_pairs={{0,8},{1,9},{2,10},{3,11},{4,12},{5,13},{6,14},{7,15},{8,0},{9,1},... | collective-permute-start | bytes 6291464 | tf_op jit(solution)/shard_map/ppermute | solution.py:435
  36.4 16.1 %collective-permute-start.3 = (bf16[32,64,128]{2,1,0:T(8,128)(2,1)S(1)}, bf16[32,64,128]{2,1,0:T(8,128)(2,1)S(1)}, u32[]{:S(2)}, u32[]{:S(2)}) collective-permute-start(bf16[32,64,128]{2,1,0:T(8,128)(2,1)S(1)} %get-tuple-element.45), channel_id=1, source_target_pairs={{0,32},{1,33},{2,34},{3,35},{4,36},{5,37},{6,38},{7,39},{8,40},{9,... | collective-permute-start | bytes 1572872 | tf_op jit(solution)/shard_map/ppermute | solution.py:435
  38.0 14.8 %collective-permute-start.5 = (bf16[32,64,128]{2,1,0:T(8,128)(2,1)S(1)}, bf16[32,64,128]{2,1,0:T(8,128)(2,1)S(1)}, u32[]{:S(2)}, u32[]{:S(2)}) collective-permute-start(bf16[32,64,128]{2,1,0:T(8,128)(2,1)S(1)} %get-tuple-element.44), channel_id=1, source_target_pairs={{0,96},{1,97},{2,98},{3,99},{4,100},{5,101},{6,102},{7,103},{8,104... | collective-permute-start | bytes 1572872 | tf_op jit(solution)/shard_map/ppermute | solution.py:435
  39.7 24.0 %collective-permute-start.7 = (bf16[32,64,128]{2,1,0:T(8,128)(2,1)S(1)}, bf16[32,64,128]{2,1,0:T(8,128)(2,1)S(1)}, u32[]{:S(2)}, u32[]{:S(2)}) collective-permute-start(bf16[32,64,128]{2,1,0:T(8,128)(2,1)S(1)} %get-tuple-element.44), channel_id=1, source_target_pairs={{0,32},{1,33},{2,34},{3,35},{4,36},{5,37},{6,38},{7,39},{8,40},{9,... | collective-permute-start | bytes 1572872 | tf_op jit(solution)/shard_map/ppermute | solution.py:435
  40.0 24.0 %collective-permute-start.8 = (bf16[32,64,128]{2,1,0:T(8,128)(2,1)S(1)}, bf16[32,64,128]{2,1,0:T(8,128)(2,1)S(1)}, u32[]{:S(2)}, u32[]{:S(2)}) collective-permute-start(bf16[32,64,128]{2,1,0:T(8,128)(2,1)S(1)} %get-tuple-element.45), channel_id=1, source_target_pairs={{0,96},{1,97},{2,98},{3,99},{4,100},{5,101},{6,102},{7,103},{8,104... | collective-permute-start | bytes 1572872 | tf_op jit(solution)/shard_map/ppermute | solution.py:435
  52.4 33.6 %collective-permute-start.4 = (bf16[32,64,128]{2,1,0:T(8,128)(2,1)S(1)}, bf16[32,64,128]{2,1,0:T(8,128)(2,1)S(1)}, u32[]{:S(2)}, u32[]{:S(2)}) collective-permute-start(bf16[32,64,128]{2,1,0:T(8,128)(2,1)S(1)} %collective-permute-done.3.refs_2_), channel_id=1, source_target_pairs={{0,32},{1,33},{2,34},{3,35},{4,36},{5,37},{6,38},{7,39},{8,40},{9,... | collective-permute-start | bytes 1572872 | tf_op jit(solution)/shard_map/ppermute | solution.py:435
  52.8 33.2 %collective-permute-start.6 = (bf16[32,64,128]{2,1,0:T(8,128)(2,1)S(1)}, bf16[32,64,128]{2,1,0:T(8,128)(2,1)S(1)}, u32[]{:S(2)}, u32[]{:S(2)}) collective-permute-start(bf16[32,64,128]{2,1,0:T(8,128)(2,1)S(1)} %collective-permute-done.5.refs_5_), channel_id=1, source_target_pairs={{0,96},{1,97},{2,98},{3,99},{4,100},{5,101},{6,102},{7,103},{8,104... | collective-permute-start | bytes 1572872 | tf_op jit(solution)/shard_map/ppermute | solution.py:435
  85.8 61.9 %collective-permute-start.1 = (bf16[2048,512]{1,0:T(8,128)(2,1)}, bf16[2048,512]{1,0:T(8,128)(2,1)}, u32[]{:S(2)}, u32[]{:S(2)}) collective-permute-start(bf16[2048,512]{1,0:T(8,128)(2,1)} %collective-permute-done.refs_2_.refs_3_), channel_id=1, source_target_pairs={{0,16},{1,17},{2,18},{3,19},{4,20},{5,21},{6,22},{7,23},{8,24},{9,... | collective-permute-start | bytes 6291464 | tf_op jit(solution)/shard_map/ppermute | solution.py:435
  86.1 17.5 %copy-start.5 = (bf16[64,2,2048]{2,1,0:T(2,128)(2,1)S(1)}, bf16[64,2,2048]{2,1,0:T(2,128)(2,1)}, u32[]{:S(2)}) copy-start(bf16[64,2,2048]{2,1,0:T(2,128)(2,1)} %param.11) | copy-start | bytes 1572868
  97.1 18.4 %copy-start.1 = (f32[2048]{0:T(1024)S(1)}, f32[2048]{0:T(1024)}, u32[]{:S(2)}) copy-start(f32[2048]{0:T(1024)} %param.12) | copy-start | bytes 24580
  97.1 19.8 %copy-start.6 = (f32[1024]{0:T(1024)S(1)}, f32[1024]{0:T(1024)}, u32[]{:S(2)}) copy-start(f32[1024]{0:T(1024)} %param.14) | copy-start | bytes 12292
  97.1 18.4 %all-to-all-start.1 = ((bf16[32,64,128]{2,1,0:T(8,128)(2,1)}), bf16[32,64,128]{2,1,0:T(8,128)(2,1)S(1)}, u32[]{:S(2)}, u32[]{:S(2)}) async-start(bf16[32,64,128]{2,1,0:T(8,128)(2,1)} %attend_last.1), calls=%async_computation.1 | async-start | bytes 1048576 | tf_op jit(solution)/shard_map/all_to_all | solution.py:472
  116.0 14.3 %collective-permute-start.10 = (bf16[128,2048]{1,0:T(8,128)(2,1)S(1)}, bf16[128,2048]{1,0:T(8,128)(2,1)S(1)}, u32[]{:S(2)}, u32[]{:S(2)}) collective-permute-start(bf16[128,2048]{1,0:T(8,128)(2,1)S(1)} %normalized.1.refs_5_), channel_id=1, source_target_pairs={{0,1},{1,2},{2,3},{3,0},{4,5},{5,6},{6,7},{7,4},{8,9},{9,10},{10,1... | collective-permute-start | bytes 1572872 | tf_op jit(solution)/shard_map/ppermute | solution.py:435
  116.3 15.0 %collective-permute-start.9 = (bf16[128,2048]{1,0:T(8,128)(2,1)S(1)}, bf16[128,2048]{1,0:T(8,128)(2,1)S(1)}, u32[]{:S(2)}, u32[]{:S(2)}) collective-permute-start(bf16[128,2048]{1,0:T(8,128)(2,1)S(1)} %normalized.1.refs_5_), channel_id=1, source_target_pairs={{0,4},{1,5},{2,6},{3,7},{4,0},{5,1},{6,2},{7,3},{8,12},{9,13},{10,... | collective-permute-start | bytes 1572872 | tf_op jit(solution)/shard_map/ppermute | solution.py:435
  116.9 15.7 %collective-permute-start.2 = (f32[1,1024]{1,0:T(1,128)S(1)}, f32[1,1024]{1,0:T(1,128)S(1)}, u32[]{:S(2)}, u32[]{:S(2)}) collective-permute-start(f32[1,1024]{1,0:T(1,128)S(1)} %bitcast.41), channel_id=1, source_target_pairs={{0,8},{1,9},{2,10},{3,11},{4,12},{5,13},{6,14},{7,15},{8,0},{9,1},... | collective-permute-start | bytes 12296 | tf_op jit(solution)/shard_map/ppermute | solution.py:435
  118.7 29.0 %collective-permute-start.11 = (bf16[128,2048]{1,0:T(8,128)(2,1)S(1)}, bf16[128,2048]{1,0:T(8,128)(2,1)S(1)}, u32[]{:S(2)}, u32[]{:S(2)}) collective-permute-start(bf16[128,2048]{1,0:T(8,128)(2,1)S(1)} %normalized.1.refs_5_), channel_id=1, source_target_pairs={{0,3},{1,0},{2,1},{3,2},{4,7},{5,4},{6,5},{7,6},{8,11},{9,8},{10,9... | collective-permute-start | bytes 1572872 | tf_op jit(solution)/shard_map/ppermute | solution.py:435
  130.3 12.2 %collective-permute-start.12 = (bf16[128,2048]{1,0:T(8,128)(2,1)S(1)}, bf16[128,2048]{1,0:T(8,128)(2,1)S(1)}, u32[]{:S(2)}, u32[]{:S(2)}) collective-permute-start(bf16[128,2048]{1,0:T(8,128)(2,1)S(1)} %collective-permute-done.10.refs_6_), channel_id=1, source_target_pairs={{0,4},{1,5},{2,6},{3,7},{4,0},{5,1},{6,2},{7,3},{8,12},{9,13},{10,... | collective-permute-start | bytes 1572872 | tf_op jit(solution)/shard_map/ppermute | solution.py:435
  131.3 12.3 %collective-permute-start.14 = (bf16[128,2048]{1,0:T(8,128)(2,1)S(1)}, bf16[128,2048]{1,0:T(8,128)(2,1)S(1)}, u32[]{:S(2)}, u32[]{:S(2)}) collective-permute-start(bf16[128,2048]{1,0:T(8,128)(2,1)S(1)} %collective-permute-done.9.refs_5_), channel_id=1, source_target_pairs={{0,3},{1,0},{2,1},{3,2},{4,7},{5,4},{6,5},{7,6},{8,11},{9,8},{10,9... | collective-permute-start | bytes 1572872 | tf_op jit(solution)/shard_map/ppermute | solution.py:435
  132.7 27.4 %collective-permute-start.13 = (bf16[128,2048]{1,0:T(8,128)(2,1)S(1)}, bf16[128,2048]{1,0:T(8,128)(2,1)S(1)}, u32[]{:S(2)}, u32[]{:S(2)}) collective-permute-start(bf16[128,2048]{1,0:T(8,128)(2,1)S(1)} %collective-permute-done.10.refs_6_), channel_id=1, source_target_pairs={{0,1},{1,2},{2,3},{3,0},{4,5},{5,6},{6,7},{7,4},{8,9},{9,10},{10,1... | collective-permute-start | bytes 1572872 | tf_op jit(solution)/shard_map/ppermute | solution.py:435
  142.5 35.2 %collective-permute-start.15 = (bf16[64,2048]{1,0:T(8,128)(2,1)S(1)}, bf16[64,2048]{1,0:T(8,128)(2,1)S(1)}, u32[]{:S(2)}, u32[]{:S(2)}) collective-permute-start(bf16[64,2048]{1,0:T(8,128)(2,1)S(1)} %slice.82), channel_id=1, source_target_pairs={{0,1},{1,2},{2,3},{3,0},{4,5},{5,6},{6,7},{7,4},{8,9},{9,10},{10,1... | collective-permute-start | bytes 786440 | tf_op jit(solution)/shard_map/ppermute | solution.py:435
  143.7 34.0 %collective-permute-start.16 = (bf16[64,2048]{1,0:T(8,128)(2,1)S(1)}, bf16[64,2048]{1,0:T(8,128)(2,1)S(1)}, u32[]{:S(2)}, u32[]{:S(2)}) collective-permute-start(bf16[64,2048]{1,0:T(8,128)(2,1)S(1)} %slice.83), channel_id=1, source_target_pairs={{0,3},{1,0},{2,1},{3,2},{4,7},{5,4},{6,5},{7,6},{8,11},{9,8},{10,9... | collective-permute-start | bytes 786440 | tf_op jit(solution)/shard_map/ppermute | solution.py:435
  147.7 2.2 copy-start
  185.3 5.3 %collective-permute-start.17 = (f32[4,1024]{1,0:T(4,128)S(1)}, f32[4,1024]{1,0:T(4,128)S(1)}, u32[]{:S(2)}, u32[]{:S(2)}) collective-permute-start(f32[4,1024]{1,0:T(4,128)S(1)} %pad_maximum_fusion.3), channel_id=1, source_target_pairs={{0,8},{1,9},{2,10},{3,11},{4,12},{5,13},{6,14},{7,15},{8,0},{9,1},... | collective-permute-start | bytes 49160 | tf_op jit(solution)/shard_map/ppermute | solution.py:435
  191.3 9.4 %all-to-all-start.2 = ((f32[8,4,1024]{2,1,0:T(4,128)}), f32[8,4,1024]{2,1,0:T(4,128)S(1)}, u32[]{:S(2)}, u32[]{:S(2)}) async-start(f32[8,4,1024]{2,1,0:T(4,128)} %broadcast_in_dim.2), calls=%async_computation.2 | async-start | bytes 262144 | tf_op jit(solution)/shard_map/all_to_all | solution.py:500
  207.7 11.9 %collective-permute-start.18 = (bf16[64,2048]{1,0:T(8,128)(2,1)S(1)}, bf16[64,2048]{1,0:T(8,128)(2,1)S(1)}, u32[]{:S(2)}, u32[]{:S(2)}) collective-permute-start(bf16[64,2048]{1,0:T(8,128)(2,1)S(1)} %get-tuple-element.36), channel_id=1, source_target_pairs={{0,1},{1,2},{2,3},{3,0},{4,5},{5,6},{6,7},{7,4},{8,9},{9,10},{10,1... | collective-permute-start | bytes 786440 | tf_op jit(solution)/shard_map/ppermute | solution.py:435
  216.3 10.0 %collective-permute-start.21 = (bf16[64,2048]{1,0:T(8,128)(2,1)S(1)}, bf16[64,2048]{1,0:T(8,128)(2,1)S(1)}, u32[]{:S(2)}, u32[]{:S(2)}) collective-permute-start(bf16[64,2048]{1,0:T(8,128)(2,1)S(1)} %get-tuple-element.39), channel_id=1, source_target_pairs={{0,3},{1,0},{2,1},{3,2},{4,7},{5,4},{6,5},{7,6},{8,11},{9,8},{10,9... | collective-permute-start | bytes 786440 | tf_op jit(solution)/shard_map/ppermute | solution.py:435
  219.5 17.6 %collective-permute-start.23 = (bf16[128,2048]{1,0:T(8,128)(2,1)S(1)}, bf16[128,2048]{1,0:T(8,128)(2,1)S(1)}, u32[]{:S(2)}, u32[]{:S(2)}) collective-permute-start(bf16[128,2048]{1,0:T(8,128)(2,1)S(1)} %get-tuple-element.40), channel_id=1, source_target_pairs={{0,3},{1,0},{2,1},{3,2},{4,7},{5,4},{6,5},{7,6},{8,11},{9,8},{10,9... | collective-permute-start | bytes 1572872 | tf_op jit(solution)/shard_map/ppermute | solution.py:435
  219.8 15.2 %collective-permute-start.19 = (bf16[128,2048]{1,0:T(8,128)(2,1)S(1)}, bf16[128,2048]{1,0:T(8,128)(2,1)S(1)}, u32[]{:S(2)}, u32[]{:S(2)}) collective-permute-start(bf16[128,2048]{1,0:T(8,128)(2,1)S(1)} %pad_maximum_fusion.1), channel_id=1, source_target_pairs={{0,1},{1,2},{2,3},{3,0},{4,5},{5,6},{6,7},{7,4},{8,9},{9,10},{10,1... | collective-permute-start | bytes 1572872 | tf_op jit(solution)/shard_map/ppermute | solution.py:435
  226.3 13.0 %collective-permute-start.22 = (bf16[128,2048]{1,0:T(8,128)(2,1)S(1)}, bf16[128,2048]{1,0:T(8,128)(2,1)S(1)}, u32[]{:S(2)}, u32[]{:S(2)}) collective-permute-start(bf16[128,2048]{1,0:T(8,128)(2,1)S(1)} %pad_maximum_fusion.2), channel_id=1, source_target_pairs={{0,4},{1,5},{2,6},{3,7},{4,0},{5,1},{6,2},{7,3},{8,12},{9,13},{10,... | collective-permute-start | bytes 1572872 | tf_op jit(solution)/shard_map/ppermute | solution.py:435
  234.9 16.0 %collective-permute-start.25 = (bf16[128,2048]{1,0:T(8,128)(2,1)S(1)}, bf16[128,2048]{1,0:T(8,128)(2,1)S(1)}, u32[]{:S(2)}, u32[]{:S(2)}) collective-permute-start(bf16[128,2048]{1,0:T(8,128)(2,1)S(1)} %get-tuple-element.41), channel_id=1, source_target_pairs={{0,1},{1,2},{2,3},{3,0},{4,5},{5,6},{6,7},{7,4},{8,9},{9,10},{10,1... | collective-permute-start | bytes 1572872 | tf_op jit(solution)/shard_map/ppermute | solution.py:435
  235.1 15.8 %collective-permute-start.20 = (bf16[128,2048]{1,0:T(8,128)(2,1)S(1)}, bf16[128,2048]{1,0:T(8,128)(2,1)S(1)}, u32[]{:S(2)}, u32[]{:S(2)}) collective-permute-start(bf16[128,2048]{1,0:T(8,128)(2,1)S(1)} %add_convert_fusion.2), channel_id=1, source_target_pairs={{0,4},{1,5},{2,6},{3,7},{4,0},{5,1},{6,2},{7,3},{8,12},{9,13},{10,... | collective-permute-start | bytes 1572872 | tf_op jit(solution)/shard_map/ppermute | solution.py:435
  239.6 11.4 %collective-permute-start.24 = (bf16[128,2048]{1,0:T(8,128)(2,1)S(1)}, bf16[128,2048]{1,0:T(8,128)(2,1)S(1)}, u32[]{:S(2)}, u32[]{:S(2)}) collective-permute-start(bf16[128,2048]{1,0:T(8,128)(2,1)S(1)} %add_convert_fusion.1), channel_id=1, source_target_pairs={{0,3},{1,0},{2,1},{3,2},{4,7},{5,4},{6,5},{7,6},{8,11},{9,8},{10,9... | collective-permute-start | bytes 1572872 | tf_op jit(solution)/shard_map/ppermute | solution.py:435

commit v3 on v2

--- a/solution.py
+++ b/solution.py
@@ -69,16 +69,15 @@
     y_at, y_size = lax.axis_index("y"), lax.axis_size("y")
     queries_real = length - y_at * depth > step * rows
 
-    def piece(n, at, count, masked, top, summed):
+    def piece(n, at, count, top, summed):
         query = q_ref[pl.ds(at // 64, sub // 64)].reshape(sub, HEAD_DIM)
         for start in range(0, depth, part):
             key = held[n, start : start + part]
             scores = lax.dot_general(
                 query, key, (((1,), (1,)), ((), ())), preferred_element_type=jnp.float32
             )
-            if masked:
-                place = lax.broadcasted_iota(jnp.int32, scores.shape, 1) + start
-                scores = jnp.where(place < count, scores, LOW)
+            place = lax.broadcasted_iota(jnp.int32, (1, part), 1) + start
+            scores = scores + jnp.where(place < count, 0.0, LOW)
             new_top = jnp.max(scores, axis=1, keepdims=True)
             if top is not None:
                 new_top = jnp.maximum(top, new_top)
@@ -100,33 +99,20 @@
         top_ref[pl.ds(at, sub), :] = jnp.broadcast_to(top, (sub, HEAD_DIM))
         sum_ref[pl.ds(at, sub), :] = summed
 
-    def attend(n, count, masked):
-        if masked:
-
-            def one(index, carry):
-                at = pl.multiple_of(index * sub, sub)
-                after(at, *piece(n, at, count, True, *before(at)))
-                return carry
-
-            lax.fori_loop(0, rows // sub, one, 0)
-        else:
-            places = range(0, rows, sub)
-            running = [before(at) for at in places]
-            done = [piece(n, at, count, False, *run) for at, run in zip(places, running)]
-            for at, run in zip(places, done):
-                after(at, *run)
+    def attend(n, count):
+        places = range(0, rows, sub)
+        running = [before(at) for at in places]
+        done = [piece(n, at, count, *run) for at, run in zip(places, running)]
+        for at, run in zip(places, done):
+            after(at, *run)
 
     def chunk(n, carry):
         turn = turns[0] + n * (turns[-1] - turns[0])
         count = length - lax.rem(y_at + turn + y_size, y_size) * depth
 
-        @pl.when(jnp.logical_and(queries_real, count >= depth))
+        @pl.when(jnp.logical_and(queries_real, count > 0))
         def _():
-            attend(n, count, False)
-
-        @pl.when(jnp.logical_and(queries_real, jnp.logical_and(count > 0, count < depth)))
-        def _():
-            attend(n, count, True)
+            attend(n, count)
 
         return carry
 
@@ -147,7 +133,7 @@
             out_ref[...] = jnp.zeros_like(out_ref)
 
 
-def attend_chunks(lengths, qkv, pairs, turns, carry, last, block=512, sub=256, part=512):
+def attend_chunks(lengths, qkv, pairs, turns, carry, last, block=1024, sub=256, part=512):
     sources, tokens = qkv.shape[0], qkv.shape[2]
     total = sources * tokens
     first = carry is None
@@ -215,133 +201,117 @@
 
 def logits_kernel(blocks, places, cols, lengths, own_ref, near_ref, far_ref, bias_ref, *refs):
     rows_in = refs[:blocks]
-    slope_ref, total_ref, rows_ref, logits_ref = refs[blocks:]
-    step = pl.program_id(0)
-
-    @pl.when(step == 0)
-    def _():
-        at = 0
-        for ref in rows_in:
-            rows_ref[pl.ds(at, ref.shape[0]), :] = ref[...]
-            at += ref.shape[0]
-
-    first = 0
-    for ref in (own_ref, near_ref, far_ref):
-        tiles = ref.shape[1] // cols
-
-        @pl.when(jnp.logical_and(step >= first, step < first + tiles))
-        def _():
-            where = pl.ds(pl.multiple_of((step - first) * cols, cols), cols)
-            logits_ref[...] = jnp.dot(
-                rows_ref[...], ref[:, where], preferred_element_type=jnp.float32
-            )
-
-        first += tiles
-    logits = logits_ref[...] + bias_ref[...]
+    slope_ref, total_ref, rows_ref = refs[blocks:]
+    at = 0
+    for ref in rows_in:
+        rows_ref[pl.ds(at, ref.shape[0]), :] = ref[...]
+        at += ref.shape[0]
     tokens = 64
     y_at, c_at, u_at, w_at, z_at = [lax.axis_index(axis) for axis in AXES]
     _, c_size, u_size, w_size, z_size = [lax.axis_size(axis) for axis in AXES]
-    sums = [jnp.zeros((1, cols), jnp.float32), jnp.zeros((1, cols), jnp.float32)]
+    real = []
     for part in range(rows_ref.shape[0] // tokens):
-        piece = logits[part * tokens : (part + 1) * tokens]
-        base = 1.0 + jnp.maximum(piece, 0.0)
-        power2 = base * base
-        power4 = power2 * power2
-        place = lax.broadcasted_iota(jnp.int32, piece.shape, 0)
         w_by, z_by = places[part // 2]
         shard = (y_at * c_size + c_at) * u_size + u_at
         shard = shard * w_size + lax.rem(w_at + w_by, w_size)
         shard = shard * z_size + lax.rem(z_at + z_by + z_size, z_size)
-        allowed = place < lengths[part % 2] - shard * tokens
-        boosted = jnp.where(allowed, power4 * power4, 0.0)
-        slope = jnp.where(
-            jnp.logical_and(allowed, piece > 0.0), power4 * (power2 * base), 0.0
-        )
-        slope_ref[pl.ds(part * tokens, tokens), :] = slope
-        sums[part % 2] = sums[part % 2] + jnp.sum(boosted, axis=0, keepdims=True)
-    total_ref[0:1, :] = sums[0]
-    total_ref[1:2, :] = sums[1]
+        real.append(lengths[part % 2] - shard * tokens)
+
+    first = 0
+    for ref in (own_ref, near_ref, far_ref):
+
+        def tile(index, carry, ref=ref, first=first):
+            here = pl.ds(pl.multiple_of(index * cols, cols), cols)
+            where = pl.ds(pl.multiple_of(first + index * cols, cols), cols)
+            logits = jnp.dot(rows_ref[...], ref[:, here], preferred_element_type=jnp.float32)
+            logits = logits + bias_ref[:, where]
+            sums = [jnp.zeros((1, cols), jnp.float32)] * 2
+            for part in range(rows_ref.shape[0] // tokens):
+                piece = logits[part * tokens : (part + 1) * tokens]
+                base = 1.0 + jnp.maximum(piece, 0.0)
+                power2 = base * base
+                power4 = power2 * power2
+                place = lax.broadcasted_iota(jnp.int32, piece.shape, 0)
+                allowed = place < real[part]
+                boosted = jnp.where(allowed, power4 * power4, 0.0)
+                slope = jnp.where(
+                    jnp.logical_and(allowed, piece > 0.0), power4 * (power2 * base), 0.0
+                )
+                slope_ref[pl.ds(part * tokens, tokens), where] = slope
+                sums[part % 2] = sums[part % 2] + jnp.sum(boosted, axis=0, keepdims=True)
+            total_ref[0:1, where] = sums[0]
+            total_ref[1:2, where] = sums[1]
+            return carry
+
+        lax.fori_loop(0, ref.shape[1] // cols, tile, 0)
+        first += ref.shape[1]
+
+
+def simple_call(body, out_shape, operands, scratch=(), grant=4, flops=0, smem=False):
+    nbytes = sum(o.size * o.dtype.itemsize for o in operands)
+    in_specs = [pl.BlockSpec(memory_space=pltpu.VMEM)] * len(operands)
+    if smem:
+        in_specs[0] = pl.BlockSpec(memory_space=pltpu.SMEM)
+    return pl.pallas_call(
+        body,
+        in_specs=in_specs,
+        out_specs=jax.tree.map(lambda _: pl.BlockSpec(memory_space=pltpu.VMEM), out_shape),
+        out_shape=out_shape,
+        scratch_shapes=list(scratch),
+        cost_estimate=pl.CostEstimate(flops=flops, bytes_accessed=2 * nbytes, transcendentals=0),
+        compiler_params=pltpu.CompilerParams(vmem_limit_bytes=grant << 20),
+    )(*operands)
 
 
 def boost(lengths, weights, bias, blocks, places, cols=256):
     width = weights[0].shape[0]
-    sizes = [w.shape[1] for w in weights]
-    entries = sum(sizes)
+    entries = sum(w.shape[1] for w in weights)
     rows = sum(b.shape[0] for b in blocks)
-    tiles = entries // cols
 
     def body(*refs):
         logits_kernel(len(blocks), places, cols, *refs)
 
-    return pl.pallas_call(
+    return simple_call(
         body,
-        grid_spec=pltpu.PrefetchScalarGridSpec(
-            num_scalar_prefetch=1,
-            grid=(tiles,),
-            in_specs=[pl.BlockSpec(memory_space=pltpu.VMEM)] * 3
-            + [pl.BlockSpec((1, cols), lambda j, counts: (0, j))]
-            + [pl.BlockSpec(b.shape, lambda j, counts: (0, 0)) for b in blocks],
-            out_specs=[
-                pl.BlockSpec((rows, cols), lambda j, counts: (0, j)),
-                pl.BlockSpec((2, cols), lambda j, counts: (0, j)),
-            ],
-            scratch_shapes=[
-                pltpu.VMEM((rows, width), jnp.bfloat16),
-                pltpu.VMEM((rows, cols), jnp.float32),
-            ],
-        ),
-        out_shape=[
-            pltpu.HBM((rows, entries), jnp.float32),
+        [
+            jax.ShapeDtypeStruct((rows, entries), jnp.float32),
             jax.ShapeDtypeStruct((2, entries), jnp.float32),
         ],
-        cost_estimate=pl.CostEstimate(
-            flops=4 * max(rows, 256) * width * entries,
-            bytes_accessed=width * entries * 2 + rows * entries * 4,
-            transcendentals=0,
-        ),
-        compiler_params=pltpu.CompilerParams(vmem_limit_bytes=28 << 20),
-        name="boost",
-    )(lengths, *weights, bias, *blocks)
-
-
-def gradient_kernel(outs, slope_ref, coef_ref, own_hbm, near_hbm, far_hbm, *refs):
-    out_refs, slopes, held, sems = refs[:outs], *refs[outs:]
+        [lengths, *weights, bias, *blocks],
+        scratch=[pltpu.VMEM((rows, width), jnp.bfloat16)],
+        grant=12,
+        flops=4 * max(rows, 256) * width * entries,
+        smem=True,
+    )
+
+
+def gradient_kernel(outs, cols, slope_ref, coef_ref, own_ref, near_ref, far_ref, *refs):
+    out_refs, slopes = refs[:outs], refs[outs]
     tokens = 64
-    step = pl.program_id(0)
-    tiles, cols = held.shape[0], held.shape[1]
-    sources = (own_hbm, near_hbm, far_hbm)
-
-    def copies(tile, feature):
+    for part in range(slopes.shape[0] // tokens):
+        where = pl.ds(part * tokens, tokens)
+        doc = part % 2
+        slopes[where, :] = (coef_ref[doc : doc + 1, :] * slope_ref[where, :]).astype(slopes.dtype)
+
+    def tile(index, carry):
+        where = pl.ds(pl.multiple_of(index * cols, cols), cols)
+        result, at = None, 0
+        for ref in (own_ref, near_ref, far_ref):
+            term = lax.dot_general(
+                slopes[:, at : at + ref.shape[1]],
+                ref[where, :],
+                (((1,), (1,)), ((), ())),
+                preferred_element_type=jnp.float32,
+            )
+            result = term if result is None else result + term
+            at += ref.shape[1]
         at = 0
-        for n, source in enumerate(sources):
-            yield pltpu.make_async_copy(
-                source.at[pl.ds(feature, cols), :],
-                held.at[tile, :, at : at + source.shape[1]],
-                sems.at[tile, n],
-            )
-            at += source.shape[1]
-
-    @pl.when(step == 0)
-    def _():
-        for tile in range(tiles):
-            for copy in copies(tile, tile * cols):
-                copy.start()
-        for part in range(slopes.shape[0] // tokens):
-            where = pl.ds(part * tokens, tokens)
-            doc = part % 2
-            slopes[where, :] = (coef_ref[doc : doc + 1, :] * slope_ref[where, :]).astype(
-                slopes.dtype
-            )
-
-    for copy in copies(step, 0):
-        copy.wait()
-    result = lax.dot_general(
-        slopes[...], held[step], (((1,), (1,)), ((), ())), preferred_element_type=jnp.float32
-    )
-    at = 0
-    for ref in out_refs:
-        ref[...] = result[at : at + ref.shape[0]].astype(ref.dtype)
-        at += ref.shape[0]
+        for ref in out_refs:
+            ref[:, where] = result[at : at + ref.shape[0]].astype(ref.dtype)
+            at += ref.shape[0]
+        return carry
+
+    lax.fori_loop(0, own_ref.shape[0] // cols, tile, 0)
 
 
 def gradient(slope, coefficient, weights, split, cols=256):
@@ -349,35 +319,104 @@
     width = weights[0].shape[0]
 
     def body(*refs):
-        gradient_kernel(len(split), *refs)
-
-    return pl.pallas_call(
+        gradient_kernel(len(split), cols, *refs)
+
+    return simple_call(
         body,
-        grid=(width // cols,),
-        in_specs=[
-            pl.BlockSpec((rows, entries), lambda j: (0, 0)),
-            pl.BlockSpec((2, entries), lambda j: (0, 0)),
-        ]
-        + [pl.BlockSpec(memory_space=pltpu.HBM)] * 3,
-        out_specs=[pl.BlockSpec((n, cols), lambda j: (0, j)) for n in split],
-        out_shape=[jax.ShapeDtypeStruct((n, width), jnp.bfloat16) for n in split],
-        scratch_shapes=[
-            pltpu.VMEM((rows, entries), jnp.bfloat16),
-            pltpu.VMEM((width // cols, cols, entries), jnp.bfloat16),
-            pltpu.SemaphoreType.DMA((width // cols, 3)),
+        [jax.ShapeDtypeStruct((n, width), jnp.bfloat16) for n in split],
+        [slope, coefficient, *weights],
+        scratch=[pltpu.VMEM((rows, entries), jnp.bfloat16)],
+        grant=12,
+        flops=4 * max(rows, 256) * width * entries,
+    )
+
+
+def swap_halves(array):
+    half = array.shape[1] // 2
+    swapped = jnp.concatenate([array[:, half:], array[:, :half]], axis=1)
+    return jnp.where(lax.axis_index("c") == 0, array, swapped)
+
+
+def own_and_other(parts, entries):
+    def body(*refs):
+        sums = refs[0][...]
+        for ref in refs[1 : len(parts)]:
+            sums = sums + ref[...]
+        own, other = sums[:, :entries], swap_halves(sums[:, entries:])
+        out_ref, swapped_ref = refs[len(parts) :]
+        out_ref[0:2, :], out_ref[2:4, :] = own, other
+        swapped_ref[0:2, :], swapped_ref[2:4, :] = other, own
+
+    shape = jax.ShapeDtypeStruct((4, entries), jnp.float32)
+    return simple_call(body, [shape, shape], parts)
+
+
+def spread_sum(one, two, peers):
+    def body(one_ref, two_ref, out_ref):
+        total = one_ref[...] + two_ref[...]
+        for n in range(peers):
+            out_ref[n] = total
+
+    shape = jax.ShapeDtypeStruct((peers,) + one.shape, jnp.float32)
+    return simple_call(body, shape, [one, two])
+
+
+def pool(lengths, gathered):
+    peers, _, entries = gathered.shape
+    docs = lengths.shape[0]
+
+    def body(lengths_ref, gathered_ref, pooled_ref, coef_ref):
+        totals = gathered_ref[0]
+        for n in range(1, peers):
+            totals = totals + gathered_ref[n]
+        doc = lax.broadcasted_iota(jnp.int32, (docs, 1), 0)
+        real = jnp.where(doc == 0, lengths_ref[0], lengths_ref[1]).astype(jnp.float32)
+        parts = []
+        for n in range(2):
+            total = totals[n * docs : (n + 1) * docs]
+            pooled = jnp.log(total / real) / sharpness
+            if n == 0:
+                pooled_ref[...] = pooled
+            usage = (pooled[0:1] + pooled[1:2]) / docs
+            parts.append(2.0 * flops_weight / docs * usage / total)
+        coef_ref[:, :entries] = parts[0]
+        coef_ref[:, entries:] = swap_halves(parts[1])
+
+    return simple_call(
+        body,
+        [
+            jax.ShapeDtypeStruct((docs, entries), jnp.float32),
+            jax.ShapeDtypeStruct((docs, 2 * entries), jnp.float32),
         ],
-        cost_estimate=pl.CostEstimate(
-            flops=4 * max(rows, 256) * width * entries,
-            bytes_accessed=width * entries * 2 + rows * entries * 4,
-            transcendentals=0,
-        ),
-        compiler_params=pltpu.CompilerParams(vmem_limit_bytes=28 << 20),
-        name="gradient",
-    )(
-        pltpu.with_memory_space_constraint(slope, pltpu.HBM),
-        coefficient,
-        *[pltpu.with_memory_space_constraint(w, pltpu.HBM) for w in weights],
+        [lengths, gathered],
+        smem=True,
     )
+
+
+def rows_of(array, start, count):
+    def body(in_ref, out_ref):
+        out_ref[...] = in_ref[start : start + count, :]
+
+    shape = jax.ShapeDtypeStruct((count, array.shape[1]), array.dtype)
+    return simple_call(body, shape, [array])
+
+
+def add(base, *terms, start=0):
+    end = start + terms[0].shape[0]
+
+    def body(base_ref, *refs):
+        out_ref = refs[-1]
+        if start > 0:
+            out_ref[:start, :] = base_ref[:start, :]
+        if end < base.shape[0]:
+            out_ref[end:, :] = base_ref[end:, :]
+        total = base_ref[start:end, :].astype(jnp.float32)
+        for ref in refs[:-1]:
+            total = total + ref[...].astype(jnp.float32)
+        out_ref[start:end, :] = total.astype(out_ref.dtype)
+
+    shape = jax.ShapeDtypeStruct(base.shape, base.dtype)
+    return simple_call(body, shape, [base, *terms])
 
 
 def norm_kernel(docs, heads, back_ref, residual_ref, gain_ref, out_ref):
@@ -413,10 +452,6 @@
     )(back, residual, gain.reshape(1, width))
 
 
-def add(*terms):
-    return sum(t.astype(jnp.float32) for t in terms).astype(jnp.bfloat16)
-
-
 def local(
     queries, key_vectors, value_vectors, residual, norm_gain, head_weight, head_bias, doc_lengths
 ):
@@ -451,11 +486,7 @@
     weights = (head_weight, near, far)
     other_bias = move(head_bias.reshape(1, entries), u=1)
 
-    def in_halves(array):
-        swapped = jnp.concatenate([array[:, half:], array[:, :half]], axis=1)
-        return jnp.where(c_at == 0, array, swapped)
-
-    bias = jnp.concatenate([head_bias.reshape(1, entries), in_halves(other_bias)], axis=1)
+    bias = jnp.concatenate([head_bias.reshape(1, entries), swap_halves(other_bias)], axis=1)
 
     carry = attend_chunks(doc_lengths, qkv, [(qkv, 1), (qkv, 2)], [0], None, False)
     carry = attend_chunks(
@@ -480,29 +511,21 @@
     rows[1, -1] = move(rows[0, -1], w=1)
     rows[0, 2] = move(rows[0, -1], z=1)
     rows[1, 1] = move(rows[1, 0], z=-1)
-    far_first = move(rows[1, -1][:tokens], z=1)
-    far_second = move(rows[1, 1][tokens:], z=-1)
+    far_first = move(rows_of(rows[1, -1], 0, tokens), z=1)
+    far_second = move(rows_of(rows[1, 1], tokens, tokens), z=-1)
 
     waves = [[(0, 0)], [(1, 0), (0, -1), (0, 1)], [(1, -1), (0, 2), (1, 1)], [(1, 2)]]
-    slopes, sums = [], 0.0
+    slopes, sums = [], []
     for wave in waves:
         blocks = [far_first, far_second] if wave == [(1, 2)] else [rows[at] for at in wave]
         slope, part = boost(doc_lengths, weights, bias, blocks, wave)
         slopes.append(slope)
-        sums = sums + part
-
-    own_sums, other_sums = sums[:, :entries], in_halves(sums[:, entries:])
-    ordered = jnp.concatenate([own_sums, other_sums], axis=0)
-    swapped = move(jnp.concatenate([other_sums, own_sums], axis=0), u=1)
-    ordered = ordered + swapped
-    peers = y_size * c_size
-    spread = jnp.broadcast_to(ordered[None], (peers,) + ordered.shape)
+        sums.append(part)
+
+    mine, swapped = own_and_other(sums, entries)
+    spread = spread_sum(mine, move(swapped, u=1), y_size * c_size)
     gathered = lax.all_to_all(spread, ("y", "c"), split_axis=0, concat_axis=0, tiled=True)
-    totals = jnp.sum(gathered, axis=0).reshape(2, docs, entries)
-    pooled = jnp.log(totals / doc_lengths[None, :, None].astype(jnp.float32)) / sharpness
-    coefficient = 2.0 * flops_weight / docs * jnp.mean(pooled, axis=1)[:, None, :] / totals
-    own_pooled = pooled[0]
-    coef = jnp.concatenate([coefficient[0], in_halves(coefficient[1])], axis=1)
+    own_pooled, coef = pool(doc_lengths, gathered)
 
     block = docs * tokens
 
@@ -514,8 +537,8 @@
     second = move(second, z=1)
     left, across, right = terms(2, [block] * 3)
     across = move(across, z=-1)
-    left = jnp.concatenate([add(left[:tokens], first), left[tokens:]])
-    right = jnp.concatenate([right[:tokens], add(right[tokens:], second)])
+    left = add(left, first)
+    right = add(right, second, start=tokens)
     left = move(left, w=1)
     right = move(right, z=1)
     pair, before, after = terms(1, [block] * 3)

time: 253 us -> 236 us (0.933)
  Pallas kernels: 106 us -> 90.8 us
  blocking collectives: 0 us -> 10.1 us
  starting transfers between devices: 58.1 us -> 48.3 us
    pallas_call x8 -> x18, Pallas kernels: 65.6 us -> 55.4 us  [simple_call(): pl.pallas_call(body, in_specs=in_specs, out_specs=jax.tree.map(lambda _:...]
    all_to_all x0 -> x1, blocking collectives: none -> 10.1 us  [local(): lax.all_to_all(spread, ('y', 'c'), split_axis=0, concat_axis=0, tiled=True)]
    ppermute x26, waiting for transfers between devices: 39 us -> 45.7 us  [move(): return lax.ppermute(array, AXES, shift_perm(sizes, **by))]
    all_to_all x1 -> x0, waiting for transfers between devices: 6.02 us -> none  [local(): lax.all_to_all(spread, ('y', 'c'), split_axis=0, concat_axis=0, tiled=True)]
    pallas_call x3, Pallas kernels: 40.3 us -> 34.9 us  [attend_chunks(): pl.pallas_call(body, grid_spec=pltpu.PrefetchScalarGridSpec(num_scalar_pr...]
    ppermute x26, starting transfers between devices: 40 us -> 35.4 us  [move(): return lax.ppermute(array, AXES, shift_perm(sizes, **by))]
    all_to_all x1 -> x0, starting transfers between devices: 3.37 us -> none  [local(): lax.all_to_all(spread, ('y', 'c'), split_axis=0, concat_axis=0, tiled=True)]
  transfers between devices with their start and end apart: 29 -> 28, of which waited for: 12 -> 14; matrix products, arithmetic and copies ran while one was open for 2% -> 1% of each run, Pallas kernels for 36% -> 33%
where the time goes in v3:
time: 236 us; the launch traced here: 235 us
  Pallas kernels  90.8 us (38%)
  waiting for transfers between devices  74.3 us (31%)
  starting transfers between devices  48.3 us (20%)
  blocking collectives  10.1 us (4%)
  local copies, waits for them, and re-layouts  9.58 us (4%)
    pallas_call x18, Pallas kernels, simple_call(): pl.pallas_call(body, in_specs=in_specs, out_specs=jax.tree.map(lambda _:...  55.4 us
    ppermute x26, waiting for transfers between devices, move(): return lax.ppermute(array, AXES, shift_perm(sizes, **by))  45.7 us
    ppermute x26, starting transfers between devices, move(): return lax.ppermute(array, AXES, shift_perm(sizes, **by))  35.4 us
    pallas_call x3, Pallas kernels, attend_chunks(): pl.pallas_call(body, grid_spec=pltpu.PrefetchScalarGridSpec(num_scalar_pr...  34.9 us
    all_to_all x1, waiting for transfers between devices, local(): lax.all_to_all(stacked, PLANE, split_axis=0, concat_axis=0, tiled=True)  16.8 us
    all_to_all x1, waiting for transfers between devices, local(): lax.all_to_all(attended, PLANE, split_axis=0, concat_axis=0, tiled=True)  11.8 us
    all_to_all x1, blocking collectives, local(): lax.all_to_all(spread, ('y', 'c'), split_axis=0, concat_axis=0, tiled=True)  10.1 us
    all_to_all x1, starting transfers between devices, local(): lax.all_to_all(stacked, PLANE, split_axis=0, concat_axis=0, tiled=True)  8.28 us
  transfers between devices with their start and end apart: 28, of which 14 were waited for; matrix products, arithmetic and copies ran while one was open for 1% of the time, Pallas kernels for 33%

profile of v3, /device:TPU:0, one launch (start us, length us, event | category | flops | bytes accessed | tf_op | source)
XLA Modules:
  0.0 235.3 jit_solution(690573008996750803)
XLA Ops:
  0.6 1.5 reshape.24
  2.1 0.2 copy.20
  2.3 0.3 reshape.25
  2.7 0.2 copy.21
  2.9 0.3 reshape.26
  3.2 0.2 copy.22
  3.5 1.4 pad_maximum_fusion
  4.8 8.3 %all-to-all-start = ((bf16[32,3,64,128]{3,2,1,0:T(8,128)(2,1)}), bf16[32,3,64,128]{3,2,1,0:T(8,128)(2,1)S(1)}, u32[]{:S(2)}, u32[]{:S(2)}) async-start(bf16[32,3,64,128]{3,2,1,0:T(8,128)(2,1)} %pad_maximum_fusion), calls=%async_computation | async-start | bytes 3145728 | tf_op jit(solution)/shard_map/all_to_all | solution.py:473
  13.1 3.1 %constant_dynamic-slice_fusion = bf16[2048,512]{1,0:T(8,128)(2,1)} fusion(bf16[2048,1024]{1,0:T(8,128)(2,1)} %refs_2_.7, s32[]{:T(128)S(6)} %select_n.11), kind=kLoop, calls=%fused_computation.7 | loop fusion | bytes 4194308 | tf_op jit(solution)/shard_map/dynamic_slice | solution.py:484
  16.2 3.3 %collective-permute-start = (bf16[2048,512]{1,0:T(8,128)(2,1)}, bf16[2048,512]{1,0:T(8,128)(2,1)}, u32[]{:S(2)}, u32[]{:S(2)}) collective-permute-start(bf16[2048,512]{1,0:T(8,128)(2,1)} %constant_dynamic-slice_fusion), channel_id=1, source_target_pairs={{0,8},{1,9},{2,10},{3,11},{4,12},{5,13},{6,14},{7,15},{8,0},{9,1},... | collective-permute-start | bytes 6291464 | tf_op jit(solution)/shard_map/ppermute | solution.py:470
  19.5 16.8 %all-to-all-done.refs_1_.refs_2_.refs_3_ = bf16[32,3,64,128]{3,2,1,0:T(8,128)(2,1)S(1)} async-done(((bf16[32,3,64,128]{3,2,1,0:T(8,128)(2,1)}), bf16[32,3,64,128]{3,2,1,0:T(8,128)(2,1)S(1)}, u32[]{:S(2)}, u32[]{:S(2)}) %all-to-all-start) | async-done | bytes 1572896 | tf_op jit(solution)/shard_map/all_to_all | solution.py:473
  36.4 1.6 collective-permute-start.3
  38.0 1.7 collective-permute-start.5
  39.7 0.4 collective-permute-start.7
  40.1 2.9 %collective-permute-start.8 = (bf16[32,64,128]{2,1,0:T(8,128)(2,1)S(1)}, bf16[32,64,128]{2,1,0:T(8,128)(2,1)S(1)}, u32[]{:S(2)}, u32[]{:S(2)}) collective-permute-start(bf16[32,64,128]{2,1,0:T(8,128)(2,1)S(1)} %get-tuple-element.51), channel_id=1, source_target_pairs={{0,96},{1,97},{2,98},{3,99},{4,100},{5,101},{6,102},{7,103},{8,104... | collective-permute-start | bytes 1572872 | tf_op jit(solution)/shard_map/ppermute | solution.py:470
  42.9 6.6 %attend_first.1 = (f32[2048,128]{1,0:T(8,128)S(1)}, f32[2048,256]{1,0:T(8,128)S(1)}) custom-call(s32[2]{0:T(128)S(1)} %copy-done.2, bf16[32,3,64,128]{3,2,1,0:T(8,128)(2,1)S(1)} %all-to-all-done.refs_1_.refs_2_.refs_3_, bf16[32,3,64,128]{3,2,1,0:T(8,128)(2,1)S(1)} %all-to-all-done.refs_1_.refs_2_.refs_3_, ...), custom_call_target="tpu_custom_call" | custom-call | flops 4294967296 | bytes 4194304 | tf_op jit(solution)/shard_map/attend_first/pallas_call | solution.py:182
  49.5 2.9 %collective-permute-done.3.refs_2_ = bf16[32,64,128]{2,1,0:T(8,128)(2,1)S(1)} collective-permute-done((bf16[32,64,128]{2,1,0:T(8,128)(2,1)S(1)}, bf16[32,64,128]{2,1,0:T(8,128)(2,1)S(1)}, u32[]{:S(2)}, u32[]{:S(2)}) %collective-permute-start.3) | collective-permute-done | bytes 524320 | tf_op jit(solution)/shard_map/ppermute | solution.py:470
  52.5 0.4 collective-permute-start.4
  52.8 2.9 %collective-permute-start.6 = (bf16[32,64,128]{2,1,0:T(8,128)(2,1)S(1)}, bf16[32,64,128]{2,1,0:T(8,128)(2,1)S(1)}, u32[]{:S(2)}, u32[]{:S(2)}) collective-permute-start(bf16[32,64,128]{2,1,0:T(8,128)(2,1)S(1)} %collective-permute-done.5.refs_5_), channel_id=1, source_target_pairs={{0,96},{1,97},{2,98},{3,99},{4,100},{5,101},{6,102},{7,103},{8,104... | collective-permute-start | bytes 1572872 | tf_op jit(solution)/shard_map/ppermute | solution.py:470
  55.7 8.0 %collective-permute-done.7.refs_3_ = bf16[32,64,128]{2,1,0:T(8,128)(2,1)S(1)} collective-permute-done((bf16[32,64,128]{2,1,0:T(8,128)(2,1)S(1)}, bf16[32,64,128]{2,1,0:T(8,128)(2,1)S(1)}, u32[]{:S(2)}, u32[]{:S(2)}) %collective-permute-start.7) | collective-permute-done | bytes 524320 | tf_op jit(solution)/shard_map/ppermute | solution.py:470
  63.7 0.4 collective-permute-done.8.refs_4_
  64.1 18.1 %attend_next.1 = (f32[2048,128]{1,0:T(8,128)S(1)}, f32[2048,256]{1,0:T(8,128)S(1)}) custom-call(s32[2]{0:T(128)S(1)} %copy-done.2, bf16[32,3,64,128]{3,2,1,0:T(8,128)(2,1)S(1)} %all-to-all-done.refs_1_.refs_2_.refs_3_, bf16[32,64,128]{2,1,0:T(8,128)(2,1)S(1)} %collective-permute-done.3.refs_2_, bf16[32,64,128]{2,1,0:T(8,128)(2,1)S(1)} %collective-permute-done.7.refs_3_, ...), custom_call_target="tpu_custom_call" | custom-call | flops 8589934592 | bytes 4194304 | tf_op jit(solution)/shard_map/attend_next/pallas_call | solution.py:182
  82.3 10.3 %attend_last.1 = bf16[32,64,128]{2,1,0:T(8,128)(2,1)} custom-call(s32[2]{0:T(128)S(1)} %copy-done.2, bf16[32,3,64,128]{3,2,1,0:T(8,128)(2,1)S(1)} %all-to-all-done.refs_1_.refs_2_.refs_3_, bf16[32,64,128]{2,1,0:T(8,128)(2,1)S(1)} %collective-permute-done.4.refs_2_, bf16[32,64,128]{2,1,0:T(8,128)(2,1)S(1)} %collective-permute-done.6.refs_3_, ...), custom_call_target="tpu_custom_call" | custom-call | flops 4294967296 | bytes 4194304 | tf_op jit(solution)/shard_map/attend_last/pallas_call | solution.py:182
  92.6 4.6 %all-to-all-start.1 = ((bf16[32,64,128]{2,1,0:T(8,128)(2,1)}), bf16[32,64,128]{2,1,0:T(8,128)(2,1)S(1)}, u32[]{:S(2)}, u32[]{:S(2)}) async-start(bf16[32,64,128]{2,1,0:T(8,128)(2,1)} %attend_last.1), calls=%async_computation.1 | async-start | bytes 1048576 | tf_op jit(solution)/shard_map/all_to_all | solution.py:503
  97.3 11.8 %all-to-all-done.1.refs_0_ = bf16[32,64,128]{2,1,0:T(8,128)(2,1)S(1)} async-done(((bf16[32,64,128]{2,1,0:T(8,128)(2,1)}), bf16[32,64,128]{2,1,0:T(8,128)(2,1)S(1)}, u32[]{:S(2)}, u32[]{:S(2)}) %all-to-all-start.1) | async-done | bytes 524320 | tf_op jit(solution)/shard_map/all_to_all | solution.py:503
  109.1 0.4 normalized.1.refs_5_
  109.6 0.3 collective-permute-start.10
  109.9 0.6 collective-permute-start.9
  110.5 1.8 collective-permute-start.2
  112.3 11.6 %collective-permute-done.10.refs_6_ = bf16[128,2048]{1,0:T(8,128)(2,1)S(1)} collective-permute-done((bf16[128,2048]{1,0:T(8,128)(2,1)S(1)}, bf16[128,2048]{1,0:T(8,128)(2,1)S(1)}, u32[]{:S(2)}, u32[]{:S(2)}) %collective-permute-start.10) | collective-permute-done | bytes 524320 | tf_op jit(solution)/shard_map/ppermute | solution.py:470
  123.9 1.0 collective-permute-start.12
  124.9 3.2 %collective-permute-start.14 = (bf16[128,2048]{1,0:T(8,128)(2,1)S(1)}, bf16[128,2048]{1,0:T(8,128)(2,1)S(1)}, u32[]{:S(2)}, u32[]{:S(2)}) collective-permute-start(bf16[128,2048]{1,0:T(8,128)(2,1)S(1)} %collective-permute-done.9.refs_5_), channel_id=1, source_target_pairs={{0,3},{1,0},{2,1},{3,2},{4,7},{5,4},{6,5},{7,6},{8,11},{9,8},{10,9... | collective-permute-start | bytes 1572872 | tf_op jit(solution)/shard_map/ppermute | solution.py:470
  128.3 7.8 %collective-permute-done.12.refs_5_.in_ref = bf16[128,2048]{1,0:T(8,128)(2,1)S(1)} collective-permute-done((bf16[128,2048]{1,0:T(8,128)(2,1)S(1)}, bf16[128,2048]{1,0:T(8,128)(2,1)S(1)}, u32[]{:S(2)}, u32[]{:S(2)}) %collective-permute-start.12) | collective-permute-done | bytes 524320 | tf_op jit(solution)/shard_map/ppermute | solution.py:470
  136.1 0.8 collective-permute-start.15
  136.8 3.6 %collective-permute-done.14.refs_7_.in_ref = bf16[128,2048]{1,0:T(8,128)(2,1)S(1)} collective-permute-done((bf16[128,2048]{1,0:T(8,128)(2,1)S(1)}, bf16[128,2048]{1,0:T(8,128)(2,1)S(1)}, u32[]{:S(2)}, u32[]{:S(2)}) %collective-permute-start.14) | collective-permute-done | bytes 524320 | tf_op jit(solution)/shard_map/ppermute | solution.py:470
  140.5 3.8 %collective-permute-start.16 = (bf16[64,2048]{1,0:T(8,128)(2,1)S(1)}, bf16[64,2048]{1,0:T(8,128)(2,1)S(1)}, u32[]{:S(2)}, u32[]{:S(2)}) collective-permute-start(bf16[64,2048]{1,0:T(8,128)(2,1)S(1)} %shard_map.99), channel_id=1, source_target_pairs={{0,3},{1,0},{2,1},{3,2},{4,7},{5,4},{6,5},{7,6},{8,11},{9,8},{10,9... | collective-permute-start | bytes 786440 | tf_op jit(solution)/shard_map/ppermute | solution.py:470
  144.3 2.2 copy-done
  146.5 8.0 %shard_map.97 = (f32[384,2048]{1,0:T(8,128)S(1)}, f32[2,2048]{1,0:T(2,128)S(1)}) custom-call(s32[2]{0:T(128)S(1)} %copy-done.2, bf16[2048,1024]{1,0:T(8,128)(2,1)S(1)} %copy-done, bf16[2048,512]{1,0:T(8,128)(2,1)} %collective-permute-done.refs_2_.refs_3_, bf16[2048,512]{1,0:T(8,128)(2,1)} %collective-permute-done.1.refs_3_.refs_4_, ...), custom_call_target="tpu_custom_call" | custom-call | flops 6442450944 | bytes 19939344 | tf_op jit(solution)/shard_map/pallas_call | solution.py:255
  154.4 8.0 %shard_map.96 = (f32[384,2048]{1,0:T(8,128)S(1)}, f32[2,2048]{1,0:T(2,128)S(1)}) custom-call(s32[2]{0:T(128)S(1)} %copy-done.2, bf16[2048,1024]{1,0:T(8,128)(2,1)S(1)} %copy-done, bf16[2048,512]{1,0:T(8,128)(2,1)} %collective-permute-done.refs_2_.refs_3_, bf16[2048,512]{1,0:T(8,128)(2,1)} %collective-permute-done.1.refs_3_.refs_4_, ...), custom_call_target="tpu_custom_call" | custom-call | flops 6442450944 | bytes 19939344 | tf_op jit(solution)/shard_map/pallas_call | solution.py:255
  162.4 5.2 %shard_map.95 = (f32[128,2048]{1,0:T(8,128)S(1)}, f32[2,2048]{1,0:T(2,128)S(1)}) custom-call(s32[2]{0:T(128)S(1)} %copy-done.2, bf16[2048,1024]{1,0:T(8,128)(2,1)S(1)} %copy-done, bf16[2048,512]{1,0:T(8,128)(2,1)} %collective-permute-done.refs_2_.refs_3_, bf16[2048,512]{1,0:T(8,128)(2,1)} %collective-permute-done.1.refs_3_.refs_4_, ...), custom_call_target="tpu_custom_call" | custom-call | flops 4294967296 | bytes 17842192 | tf_op jit(solution)/shard_map/pallas_call | solution.py:255
  167.7 5.2 %shard_map.100 = (f32[128,2048]{1,0:T(8,128)S(1)}, f32[2,2048]{1,0:T(2,128)S(1)}) custom-call(s32[2]{0:T(128)S(1)} %copy-done.2, bf16[2048,1024]{1,0:T(8,128)(2,1)S(1)} %copy-done, bf16[2048,512]{1,0:T(8,128)(2,1)} %collective-permute-done.refs_2_.refs_3_, bf16[2048,512]{1,0:T(8,128)(2,1)} %collective-permute-done.1.refs_3_.refs_4_, ...), custom_call_target="tpu_custom_call" | custom-call | flops 4294967296 | bytes 17842192 | tf_op jit(solution)/shard_map/pallas_call | solution.py:255
  173.0 2.4 %collective-permute-start.17 = (f32[4,1024]{1,0:T(4,128)S(1)}, f32[4,1024]{1,0:T(4,128)S(1)}, u32[]{:S(2)}, u32[]{:S(2)}) collective-permute-start(f32[4,1024]{1,0:T(4,128)S(1)} %get-tuple-element.35), channel_id=1, source_target_pairs={{0,8},{1,9},{2,10},{3,11},{4,12},{5,13},{6,14},{7,15},{8,0},{9,1},... | collective-permute-start | bytes 49160 | tf_op jit(solution)/shard_map/ppermute | solution.py:470
  175.4 2.9 %collective-permute-done.17.two_ref = f32[4,1024]{1,0:T(4,128)S(1)} collective-permute-done((f32[4,1024]{1,0:T(4,128)S(1)}, f32[4,1024]{1,0:T(4,128)S(1)}, u32[]{:S(2)}, u32[]{:S(2)}) %collective-permute-start.17) | collective-permute-done | bytes 16416 | tf_op jit(solution)/shard_map/ppermute | solution.py:470
  178.3 10.1 %all_to_all.15.gathered_ref = f32[8,4,1024]{2,1,0:T(4,128)S(1)} all-to-all(f32[8,4,1024]{2,1,0:T(4,128)S(1)} %shard_map.102), channel_id=1, replica_groups=mesh['y'=4,'c'=2,'u'=2,'w'=2,'z'=4] {'y','c'}, dimensions={0} | all-to-all | bytes 262144 | tf_op jit(solution)/shard_map/all_to_all | solution.py:527
  188.4 1.2 shard_map.103
  189.5 6.2 %shard_map.107 = (bf16[64,2048]{1,0:T(8,128)(2,1)S(1)}, bf16[64,2048]{1,0:T(8,128)(2,1)S(1)}) custom-call(f32[128,2048]{1,0:T(8,128)S(1)} %get-tuple-element.43.refs_0_, f32[2,2048]{1,0:T(2,128)S(1)} %get-tuple-element.38.refs_1_, bf16[2048,1024]{1,0:T(8,128)(2,1)S(1)} %copy-done, bf16[2048,512]{1,0:T(8,128)(2,1)} %collective-permute-done.refs_2_.refs_3_, ...), custom_call_target="tpu_custom_call" | custom-call | flops 4294967296 | bytes 18907136 | tf_op jit(solution)/shard_map/pallas_call | solution.py:255
  195.7 0.9 collective-permute-start.21
  196.6 1.2 collective-permute-start.18
  197.8 7.3 %shard_map.106 = (bf16[128,2048]{1,0:T(8,128)(2,1)S(1)}, bf16[128,2048]{1,0:T(8,128)(2,1)S(1)}, bf16[128,2048]{1,0:T(8,128)(2,1)S(1)}) custom-call(f32[384,2048]{1,0:T(8,128)S(1)} %get-tuple-element.41.refs_0_, f32[2,2048]{1,0:T(2,128)S(1)} %get-tuple-element.38.refs_1_, bf16[2048,1024]{1,0:T(8,128)(2,1)S(1)} %copy-done, ...), custom_call_target="tpu_custom_call" | custom-call | flops 6442450944 | bytes 23101440 | tf_op jit(solution)/shard_map/pallas_call | solution.py:255
  205.2 2.1 collective-permute-start.23
  207.4 0.8 collective-permute-start.22
  208.3 0.3 collective-permute-start.19
  208.6 7.3 %shard_map.105 = (bf16[128,2048]{1,0:T(8,128)(2,1)S(1)}, bf16[128,2048]{1,0:T(8,128)(2,1)S(1)}, bf16[128,2048]{1,0:T(8,128)(2,1)S(1)}) custom-call(f32[384,2048]{1,0:T(8,128)S(1)} %get-tuple-element.39.refs_0_, f32[2,2048]{1,0:T(2,128)S(1)} %get-tuple-element.38.refs_1_, bf16[2048,1024]{1,0:T(8,128)(2,1)S(1)} %copy-done, ...), custom_call_target="tpu_custom_call" | custom-call | flops 6442450944 | bytes 23101440 | tf_op jit(solution)/shard_map/pallas_call | solution.py:255
  216.0 2.2 collective-permute-done.23.refs_1_
  218.1 2.0 collective-permute-done.22.refs_0_
  220.1 0.2 shard_map.111
  220.3 1.4 collective-permute-start.24
  221.7 2.6 %collective-permute-done.19.refs_0_ = bf16[128,2048]{1,0:T(8,128)(2,1)S(1)} collective-permute-done((bf16[128,2048]{1,0:T(8,128)(2,1)S(1)}, bf16[128,2048]{1,0:T(8,128)(2,1)S(1)}, u32[]{:S(2)}, u32[]{:S(2)}) %collective-permute-start.19) | collective-permute-done | bytes 524320 | tf_op jit(solution)/shard_map/ppermute | solution.py:470
  224.5 1.4 collective-permute-start.20
  225.9 6.1 %shard_map.104.base_ref = bf16[128,2048]{1,0:T(8,128)(2,1)S(1)} custom-call(f32[128,2048]{1,0:T(8,128)S(1)} %get-tuple-element.37.refs_0_, f32[2,2048]{1,0:T(2,128)S(1)} %get-tuple-element.38.refs_1_, bf16[2048,1024]{1,0:T(8,128)(2,1)S(1)} %copy-done, bf16[2048,512]{1,0:T(8,128)(2,1)} %collective-permute-done.refs_2_.refs_3_, ...), custom_call_target="tpu_custom_call" | custom-call | flops 4294967296 | bytes 18907136 | tf_op jit(solution)/shard_map/pallas_call | solution.py:255
  232.0 1.1 collective-permute-done.25.refs_2_
  233.1 0.6 collective-permute-done.20.refs_0_
  233.7 0.3 shard_map.112
  234.0 1.3 copy.31
  (43 shorter events, 0.9 us)
Async XLA Ops:
  0.6 1.7 copy-start.3
  0.6 2.3 copy-start.4
  4.8 31.5 %all-to-all-start = ((bf16[32,3,64,128]{3,2,1,0:T(8,128)(2,1)}), bf16[32,3,64,128]{3,2,1,0:T(8,128)(2,1)S(1)}, u32[]{:S(2)}, u32[]{:S(2)}) async-start(bf16[32,3,64,128]{3,2,1,0:T(8,128)(2,1)} %pad_maximum_fusion), calls=%async_computation | async-start | bytes 3145728 | tf_op jit(solution)/shard_map/all_to_all | solution.py:473
  16.2 26.8 %copy-start.2 = (s32[2]{0:T(128)S(1)}, s32[2]{0:T(128)}, u32[]{:S(2)}) copy-start(s32[2]{0:T(128)} %lengths_ref.1) | copy-start | bytes 28
  16.2 66.0 %collective-permute-start = (bf16[2048,512]{1,0:T(8,128)(2,1)}, bf16[2048,512]{1,0:T(8,128)(2,1)}, u32[]{:S(2)}, u32[]{:S(2)}) collective-permute-start(bf16[2048,512]{1,0:T(8,128)(2,1)} %constant_dynamic-slice_fusion), channel_id=1, source_target_pairs={{0,8},{1,9},{2,10},{3,11},{4,12},{5,13},{6,14},{7,15},{8,0},{9,1},... | collective-permute-start | bytes 6291464 | tf_op jit(solution)/shard_map/ppermute | solution.py:470
  36.4 16.1 %collective-permute-start.3 = (bf16[32,64,128]{2,1,0:T(8,128)(2,1)S(1)}, bf16[32,64,128]{2,1,0:T(8,128)(2,1)S(1)}, u32[]{:S(2)}, u32[]{:S(2)}) collective-permute-start(bf16[32,64,128]{2,1,0:T(8,128)(2,1)S(1)} %get-tuple-element.51), channel_id=1, source_target_pairs={{0,32},{1,33},{2,34},{3,35},{4,36},{5,37},{6,38},{7,39},{8,40},{9,... | collective-permute-start | bytes 1572872 | tf_op jit(solution)/shard_map/ppermute | solution.py:470
  38.0 14.8 %collective-permute-start.5 = (bf16[32,64,128]{2,1,0:T(8,128)(2,1)S(1)}, bf16[32,64,128]{2,1,0:T(8,128)(2,1)S(1)}, u32[]{:S(2)}, u32[]{:S(2)}) collective-permute-start(bf16[32,64,128]{2,1,0:T(8,128)(2,1)S(1)} %get-tuple-element.50), channel_id=1, source_target_pairs={{0,96},{1,97},{2,98},{3,99},{4,100},{5,101},{6,102},{7,103},{8,104... | collective-permute-start | bytes 1572872 | tf_op jit(solution)/shard_map/ppermute | solution.py:470
  39.7 24.0 %collective-permute-start.7 = (bf16[32,64,128]{2,1,0:T(8,128)(2,1)S(1)}, bf16[32,64,128]{2,1,0:T(8,128)(2,1)S(1)}, u32[]{:S(2)}, u32[]{:S(2)}) collective-permute-start(bf16[32,64,128]{2,1,0:T(8,128)(2,1)S(1)} %get-tuple-element.50), channel_id=1, source_target_pairs={{0,32},{1,33},{2,34},{3,35},{4,36},{5,37},{6,38},{7,39},{8,40},{9,... | collective-permute-start | bytes 1572872 | tf_op jit(solution)/shard_map/ppermute | solution.py:470
  40.1 24.0 %collective-permute-start.8 = (bf16[32,64,128]{2,1,0:T(8,128)(2,1)S(1)}, bf16[32,64,128]{2,1,0:T(8,128)(2,1)S(1)}, u32[]{:S(2)}, u32[]{:S(2)}) collective-permute-start(bf16[32,64,128]{2,1,0:T(8,128)(2,1)S(1)} %get-tuple-element.51), channel_id=1, source_target_pairs={{0,96},{1,97},{2,98},{3,99},{4,100},{5,101},{6,102},{7,103},{8,104... | collective-permute-start | bytes 1572872 | tf_op jit(solution)/shard_map/ppermute | solution.py:470
  52.5 29.8 %collective-permute-start.4 = (bf16[32,64,128]{2,1,0:T(8,128)(2,1)S(1)}, bf16[32,64,128]{2,1,0:T(8,128)(2,1)S(1)}, u32[]{:S(2)}, u32[]{:S(2)}) collective-permute-start(bf16[32,64,128]{2,1,0:T(8,128)(2,1)S(1)} %collective-permute-done.3.refs_2_), channel_id=1, source_target_pairs={{0,32},{1,33},{2,34},{3,35},{4,36},{5,37},{6,38},{7,39},{8,40},{9,... | collective-permute-start | bytes 1572872 | tf_op jit(solution)/shard_map/ppermute | solution.py:470
  52.8 29.4 %collective-permute-start.6 = (bf16[32,64,128]{2,1,0:T(8,128)(2,1)S(1)}, bf16[32,64,128]{2,1,0:T(8,128)(2,1)S(1)}, u32[]{:S(2)}, u32[]{:S(2)}) collective-permute-start(bf16[32,64,128]{2,1,0:T(8,128)(2,1)S(1)} %collective-permute-done.5.refs_5_), channel_id=1, source_target_pairs={{0,96},{1,97},{2,98},{3,99},{4,100},{5,101},{6,102},{7,103},{8,104... | collective-permute-start | bytes 1572872 | tf_op jit(solution)/shard_map/ppermute | solution.py:470
  82.2 62.1 %collective-permute-start.1 = (bf16[2048,512]{1,0:T(8,128)(2,1)}, bf16[2048,512]{1,0:T(8,128)(2,1)}, u32[]{:S(2)}, u32[]{:S(2)}) collective-permute-start(bf16[2048,512]{1,0:T(8,128)(2,1)} %collective-permute-done.refs_2_.refs_3_), channel_id=1, source_target_pairs={{0,16},{1,17},{2,18},{3,19},{4,20},{5,21},{6,22},{7,23},{8,24},{9,... | collective-permute-start | bytes 6291464 | tf_op jit(solution)/shard_map/ppermute | solution.py:470
  82.3 14.9 %copy-start.5 = (bf16[64,2,2048]{2,1,0:T(2,128)(2,1)S(1)}, bf16[64,2,2048]{2,1,0:T(2,128)(2,1)}, u32[]{:S(2)}) copy-start(bf16[64,2,2048]{2,1,0:T(2,128)(2,1)} %param.11) | copy-start | bytes 1572868
  92.6 16.6 %copy-start.1 = (f32[2048]{0:T(1024)S(1)}, f32[2048]{0:T(1024)}, u32[]{:S(2)}) copy-start(f32[2048]{0:T(1024)} %param.12) | copy-start | bytes 24580
  92.6 18.0 %copy-start.6 = (f32[1024]{0:T(1024)S(1)}, f32[1024]{0:T(1024)}, u32[]{:S(2)}) copy-start(f32[1024]{0:T(1024)} %param.14) | copy-start | bytes 12292
  92.6 16.6 %all-to-all-start.1 = ((bf16[32,64,128]{2,1,0:T(8,128)(2,1)}), bf16[32,64,128]{2,1,0:T(8,128)(2,1)S(1)}, u32[]{:S(2)}, u32[]{:S(2)}) async-start(bf16[32,64,128]{2,1,0:T(8,128)(2,1)} %attend_last.1), calls=%async_computation.1 | async-start | bytes 1048576 | tf_op jit(solution)/shard_map/all_to_all | solution.py:503
  109.6 14.3 %collective-permute-start.10 = (bf16[128,2048]{1,0:T(8,128)(2,1)S(1)}, bf16[128,2048]{1,0:T(8,128)(2,1)S(1)}, u32[]{:S(2)}, u32[]{:S(2)}) collective-permute-start(bf16[128,2048]{1,0:T(8,128)(2,1)S(1)} %normalized.1.refs_5_), channel_id=1, source_target_pairs={{0,1},{1,2},{2,3},{3,0},{4,5},{5,6},{6,7},{7,4},{8,9},{9,10},{10,1... | collective-permute-start | bytes 1572872 | tf_op jit(solution)/shard_map/ppermute | solution.py:470
  109.9 15.0 %collective-permute-start.9 = (bf16[128,2048]{1,0:T(8,128)(2,1)S(1)}, bf16[128,2048]{1,0:T(8,128)(2,1)S(1)}, u32[]{:S(2)}, u32[]{:S(2)}) collective-permute-start(bf16[128,2048]{1,0:T(8,128)(2,1)S(1)} %normalized.1.refs_5_), channel_id=1, source_target_pairs={{0,4},{1,5},{2,6},{3,7},{4,0},{5,1},{6,2},{7,3},{8,12},{9,13},{10,... | collective-permute-start | bytes 1572872 | tf_op jit(solution)/shard_map/ppermute | solution.py:470
  110.5 17.7 %collective-permute-start.2 = (f32[1,1024]{1,0:T(1,128)S(1)}, f32[1,1024]{1,0:T(1,128)S(1)}, u32[]{:S(2)}, u32[]{:S(2)}) collective-permute-start(f32[1,1024]{1,0:T(1,128)S(1)} %bitcast.33), channel_id=1, source_target_pairs={{0,8},{1,9},{2,10},{3,11},{4,12},{5,13},{6,14},{7,15},{8,0},{9,1},... | collective-permute-start | bytes 12296 | tf_op jit(solution)/shard_map/ppermute | solution.py:470
  123.9 12.2 %collective-permute-start.12 = (bf16[128,2048]{1,0:T(8,128)(2,1)S(1)}, bf16[128,2048]{1,0:T(8,128)(2,1)S(1)}, u32[]{:S(2)}, u32[]{:S(2)}) collective-permute-start(bf16[128,2048]{1,0:T(8,128)(2,1)S(1)} %collective-permute-done.10.refs_6_), channel_id=1, source_target_pairs={{0,4},{1,5},{2,6},{3,7},{4,0},{5,1},{6,2},{7,3},{8,12},{9,13},{10,... | collective-permute-start | bytes 1572872 | tf_op jit(solution)/shard_map/ppermute | solution.py:470
  124.9 19.3 %collective-permute-start.13 = (bf16[128,2048]{1,0:T(8,128)(2,1)S(1)}, bf16[128,2048]{1,0:T(8,128)(2,1)S(1)}, u32[]{:S(2)}, u32[]{:S(2)}) collective-permute-start(bf16[128,2048]{1,0:T(8,128)(2,1)S(1)} %collective-permute-done.10.refs_6_), channel_id=1, source_target_pairs={{0,1},{1,2},{2,3},{3,0},{4,5},{5,6},{6,7},{7,4},{8,9},{9,10},{10,1... | collective-permute-start | bytes 1572872 | tf_op jit(solution)/shard_map/ppermute | solution.py:470
  124.9 15.5 %collective-permute-start.14 = (bf16[128,2048]{1,0:T(8,128)(2,1)S(1)}, bf16[128,2048]{1,0:T(8,128)(2,1)S(1)}, u32[]{:S(2)}, u32[]{:S(2)}) collective-permute-start(bf16[128,2048]{1,0:T(8,128)(2,1)S(1)} %collective-permute-done.9.refs_5_), channel_id=1, source_target_pairs={{0,3},{1,0},{2,1},{3,2},{4,7},{5,4},{6,5},{7,6},{8,11},{9,8},{10,9... | collective-permute-start | bytes 1572872 | tf_op jit(solution)/shard_map/ppermute | solution.py:470
  128.2 26.2 %collective-permute-start.11 = (bf16[128,2048]{1,0:T(8,128)(2,1)S(1)}, bf16[128,2048]{1,0:T(8,128)(2,1)S(1)}, u32[]{:S(2)}, u32[]{:S(2)}) collective-permute-start(bf16[128,2048]{1,0:T(8,128)(2,1)S(1)} %normalized.1.refs_5_), channel_id=1, source_target_pairs={{0,3},{1,0},{2,1},{3,2},{4,7},{5,4},{6,5},{7,6},{8,11},{9,8},{10,9... | collective-permute-start | bytes 1572872 | tf_op jit(solution)/shard_map/ppermute | solution.py:470
  136.1 31.6 %collective-permute-start.15 = (bf16[64,2048]{1,0:T(8,128)(2,1)S(1)}, bf16[64,2048]{1,0:T(8,128)(2,1)S(1)}, u32[]{:S(2)}, u32[]{:S(2)}) collective-permute-start(bf16[64,2048]{1,0:T(8,128)(2,1)S(1)} %shard_map.98), channel_id=1, source_target_pairs={{0,1},{1,2},{2,3},{3,0},{4,5},{5,6},{6,7},{7,4},{8,9},{9,10},{10,1... | collective-permute-start | bytes 786440 | tf_op jit(solution)/shard_map/ppermute | solution.py:470
  140.5 27.2 %collective-permute-start.16 = (bf16[64,2048]{1,0:T(8,128)(2,1)S(1)}, bf16[64,2048]{1,0:T(8,128)(2,1)S(1)}, u32[]{:S(2)}, u32[]{:S(2)}) collective-permute-start(bf16[64,2048]{1,0:T(8,128)(2,1)S(1)} %shard_map.99), channel_id=1, source_target_pairs={{0,3},{1,0},{2,1},{3,2},{4,7},{5,4},{6,5},{7,6},{8,11},{9,8},{10,9... | collective-permute-start | bytes 786440 | tf_op jit(solution)/shard_map/ppermute | solution.py:470
  144.3 2.2 copy-start
  173.0 5.3 %collective-permute-start.17 = (f32[4,1024]{1,0:T(4,128)S(1)}, f32[4,1024]{1,0:T(4,128)S(1)}, u32[]{:S(2)}, u32[]{:S(2)}) collective-permute-start(f32[4,1024]{1,0:T(4,128)S(1)} %get-tuple-element.35), channel_id=1, source_target_pairs={{0,8},{1,9},{2,10},{3,11},{4,12},{5,13},{6,14},{7,15},{8,0},{9,1},... | collective-permute-start | bytes 49160 | tf_op jit(solution)/shard_map/ppermute | solution.py:470
  195.7 11.6 %collective-permute-start.21 = (bf16[64,2048]{1,0:T(8,128)(2,1)S(1)}, bf16[64,2048]{1,0:T(8,128)(2,1)S(1)}, u32[]{:S(2)}, u32[]{:S(2)}) collective-permute-start(bf16[64,2048]{1,0:T(8,128)(2,1)S(1)} %get-tuple-element.47), channel_id=1, source_target_pairs={{0,3},{1,0},{2,1},{3,2},{4,7},{5,4},{6,5},{7,6},{8,11},{9,8},{10,9... | collective-permute-start | bytes 786440 | tf_op jit(solution)/shard_map/ppermute | solution.py:470
  196.6 11.5 %collective-permute-start.18 = (bf16[64,2048]{1,0:T(8,128)(2,1)S(1)}, bf16[64,2048]{1,0:T(8,128)(2,1)S(1)}, u32[]{:S(2)}, u32[]{:S(2)}) collective-permute-start(bf16[64,2048]{1,0:T(8,128)(2,1)S(1)} %get-tuple-element.44), channel_id=1, source_target_pairs={{0,1},{1,2},{2,3},{3,0},{4,5},{5,6},{6,7},{7,4},{8,9},{9,10},{10,1... | collective-permute-start | bytes 786440 | tf_op jit(solution)/shard_map/ppermute | solution.py:470
  205.2 13.0 %collective-permute-start.23 = (bf16[128,2048]{1,0:T(8,128)(2,1)S(1)}, bf16[128,2048]{1,0:T(8,128)(2,1)S(1)}, u32[]{:S(2)}, u32[]{:S(2)}) collective-permute-start(bf16[128,2048]{1,0:T(8,128)(2,1)S(1)} %get-tuple-element.48), channel_id=1, source_target_pairs={{0,3},{1,0},{2,1},{3,2},{4,7},{5,4},{6,5},{7,6},{8,11},{9,8},{10,9... | collective-permute-start | bytes 1572872 | tf_op jit(solution)/shard_map/ppermute | solution.py:470
  207.4 12.7 %collective-permute-start.22 = (bf16[128,2048]{1,0:T(8,128)(2,1)S(1)}, bf16[128,2048]{1,0:T(8,128)(2,1)S(1)}, u32[]{:S(2)}, u32[]{:S(2)}) collective-permute-start(bf16[128,2048]{1,0:T(8,128)(2,1)S(1)} %shard_map.110), channel_id=1, source_target_pairs={{0,4},{1,5},{2,6},{3,7},{4,0},{5,1},{6,2},{7,3},{8,12},{9,13},{10,... | collective-permute-start | bytes 1572872 | tf_op jit(solution)/shard_map/ppermute | solution.py:470
  208.3 16.1 %collective-permute-start.19 = (bf16[128,2048]{1,0:T(8,128)(2,1)S(1)}, bf16[128,2048]{1,0:T(8,128)(2,1)S(1)}, u32[]{:S(2)}, u32[]{:S(2)}) collective-permute-start(bf16[128,2048]{1,0:T(8,128)(2,1)S(1)} %shard_map.108), channel_id=1, source_target_pairs={{0,1},{1,2},{2,3},{3,0},{4,5},{5,6},{6,7},{7,4},{8,9},{9,10},{10,1... | collective-permute-start | bytes 1572872 | tf_op jit(solution)/shard_map/ppermute | solution.py:470
  215.9 17.2 %collective-permute-start.25 = (bf16[128,2048]{1,0:T(8,128)(2,1)S(1)}, bf16[128,2048]{1,0:T(8,128)(2,1)S(1)}, u32[]{:S(2)}, u32[]{:S(2)}) collective-permute-start(bf16[128,2048]{1,0:T(8,128)(2,1)S(1)} %get-tuple-element.49), channel_id=1, source_target_pairs={{0,1},{1,2},{2,3},{3,0},{4,5},{5,6},{6,7},{7,4},{8,9},{9,10},{10,1... | collective-permute-start | bytes 1572872 | tf_op jit(solution)/shard_map/ppermute | solution.py:470
  220.3 12.8 %collective-permute-start.24 = (bf16[128,2048]{1,0:T(8,128)(2,1)S(1)}, bf16[128,2048]{1,0:T(8,128)(2,1)S(1)}, u32[]{:S(2)}, u32[]{:S(2)}) collective-permute-start(bf16[128,2048]{1,0:T(8,128)(2,1)S(1)} %shard_map.111), channel_id=1, source_target_pairs={{0,3},{1,0},{2,1},{3,2},{4,7},{5,4},{6,5},{7,6},{8,11},{9,8},{10,9... | collective-permute-start | bytes 1572872 | tf_op jit(solution)/shard_map/ppermute | solution.py:470
  224.5 9.3 %collective-permute-start.20 = (bf16[128,2048]{1,0:T(8,128)(2,1)S(1)}, bf16[128,2048]{1,0:T(8,128)(2,1)S(1)}, u32[]{:S(2)}, u32[]{:S(2)}) collective-permute-start(bf16[128,2048]{1,0:T(8,128)(2,1)S(1)} %shard_map.109), channel_id=1, source_target_pairs={{0,4},{1,5},{2,6},{3,7},{4,0},{5,1},{6,2},{7,3},{8,12},{9,13},{10,... | collective-permute-start | bytes 1572872 | tf_op jit(solution)/shard_map/ppermute | solution.py:470

commit v4 on v3

--- a/solution.py
+++ b/solution.py
@@ -199,7 +199,7 @@
     )(lengths, *operands)
 
 
-def logits_kernel(blocks, places, cols, lengths, own_ref, near_ref, far_ref, bias_ref, *refs):
+def logits_kernel(blocks, places, cols, lengths, weights_ref, bias_ref, *refs):
     rows_in = refs[:blocks]
     slope_ref, total_ref, rows_ref = refs[blocks:]
     at = 0
@@ -217,34 +217,68 @@
         shard = shard * z_size + lax.rem(z_at + z_by + z_size, z_size)
         real.append(lengths[part % 2] - shard * tokens)
 
-    first = 0
-    for ref in (own_ref, near_ref, far_ref):
-
-        def tile(index, carry, ref=ref, first=first):
-            here = pl.ds(pl.multiple_of(index * cols, cols), cols)
-            where = pl.ds(pl.multiple_of(first + index * cols, cols), cols)
-            logits = jnp.dot(rows_ref[...], ref[:, here], preferred_element_type=jnp.float32)
-            logits = logits + bias_ref[:, where]
-            sums = [jnp.zeros((1, cols), jnp.float32)] * 2
-            for part in range(rows_ref.shape[0] // tokens):
-                piece = logits[part * tokens : (part + 1) * tokens]
-                base = 1.0 + jnp.maximum(piece, 0.0)
-                power2 = base * base
-                power4 = power2 * power2
-                place = lax.broadcasted_iota(jnp.int32, piece.shape, 0)
-                allowed = place < real[part]
-                boosted = jnp.where(allowed, power4 * power4, 0.0)
-                slope = jnp.where(
-                    jnp.logical_and(allowed, piece > 0.0), power4 * (power2 * base), 0.0
+    def tile(index, carry):
+        where = pl.ds(pl.multiple_of(index * cols, cols), cols)
+        logits = jnp.dot(rows_ref[...], weights_ref[:, where], preferred_element_type=jnp.float32)
+        logits = logits + bias_ref[:, where]
+        sums = [jnp.zeros((1, cols), jnp.float32)] * 2
+        for part in range(rows_ref.shape[0] // tokens):
+            piece = logits[part * tokens : (part + 1) * tokens]
+            base = 1.0 + jnp.maximum(piece, 0.0)
+            power2 = base * base
+            power4 = power2 * power2
+            place = lax.broadcasted_iota(jnp.int32, piece.shape, 0)
+            allowed = place < real[part]
+            boosted = jnp.where(allowed, power4 * power4, 0.0)
+            slope = jnp.where(
+                jnp.logical_and(allowed, piece > 0.0), power4 * (power2 * base), 0.0
+            )
+            slope_ref[pl.ds(part * tokens, tokens), where] = slope
+            sums[part % 2] = sums[part % 2] + jnp.sum(boosted, axis=0, keepdims=True)
+        total_ref[0:1, where] = sums[0]
+        total_ref[1:2, where] = sums[1]
+        return carry
+
+    lax.fori_loop(0, weights_ref.shape[1] // cols, tile, 0)
+
+
+def side_by_side(own, near, far, own_bias, other_bias):
+    depth, entries = own.shape
+    half = near.shape[1]
+
+    def body(own_hbm, near_hbm, far_hbm, own_bias_ref, other_bias_ref, out_ref, bias_ref, sems):
+        copies = []
+        for n, (source, at) in enumerate(
+            ((own_hbm, 0), (near_hbm, entries), (far_hbm, entries + half))
+        ):
+            copies.append(
+                pltpu.make_async_copy(
+                    source, out_ref.at[:, at : at + source.shape[1]], sems.at[n]
                 )
-                slope_ref[pl.ds(part * tokens, tokens), where] = slope
-                sums[part % 2] = sums[part % 2] + jnp.sum(boosted, axis=0, keepdims=True)
-            total_ref[0:1, where] = sums[0]
-            total_ref[1:2, where] = sums[1]
-            return carry
-
-        lax.fori_loop(0, ref.shape[1] // cols, tile, 0)
-        first += ref.shape[1]
+            )
+        for copy in copies:
+            copy.start()
+        bias_ref[:, :entries] = own_bias_ref[...]
+        bias_ref[:, entries:] = swap_halves(other_bias_ref[...])
+        for copy in copies:
+            copy.wait()
+
+    return pl.pallas_call(
+        body,
+        in_specs=[pl.BlockSpec(memory_space=pl.ANY)] * 3
+        + [pl.BlockSpec(memory_space=pltpu.VMEM)] * 2,
+        out_specs=[pl.BlockSpec(memory_space=pltpu.VMEM)] * 2,
+        out_shape=[
+            jax.ShapeDtypeStruct((depth, 2 * entries), own.dtype),
+            jax.ShapeDtypeStruct((1, 2 * entries), jnp.float32),
+        ],
+        scratch_shapes=[pltpu.SemaphoreType.DMA((3,))],
+        cost_estimate=pl.CostEstimate(
+            flops=0, bytes_accessed=8 * depth * entries, transcendentals=0
+        ),
+        compiler_params=pltpu.CompilerParams(vmem_limit_bytes=4 << 20),
+        name="side_by_side",
+    )(pltpu.with_memory_space_constraint(own, pltpu.HBM), near, far, own_bias, other_bias)
 
 
 def simple_call(body, out_shape, operands, scratch=(), grant=4, flops=0, smem=False):
@@ -263,9 +297,8 @@
     )(*operands)
 
 
-def boost(lengths, weights, bias, blocks, places, cols=256):
-    width = weights[0].shape[0]
-    entries = sum(w.shape[1] for w in weights)
+def boost(lengths, weights, bias, blocks, places, cols=512):
+    width, entries = weights.shape
     rows = sum(b.shape[0] for b in blocks)
 
     def body(*refs):
@@ -277,7 +310,7 @@
             jax.ShapeDtypeStruct((rows, entries), jnp.float32),
             jax.ShapeDtypeStruct((2, entries), jnp.float32),
         ],
-        [lengths, *weights, bias, *blocks],
+        [lengths, weights, bias, *blocks],
         scratch=[pltpu.VMEM((rows, width), jnp.bfloat16)],
         grant=12,
         flops=4 * max(rows, 256) * width * entries,
@@ -285,7 +318,7 @@
     )
 
 
-def gradient_kernel(outs, cols, slope_ref, coef_ref, own_ref, near_ref, far_ref, *refs):
+def gradient_kernel(outs, cols, slope_ref, coef_ref, weights_ref, *refs):
     out_refs, slopes = refs[:outs], refs[outs]
     tokens = 64
     for part in range(slopes.shape[0] // tokens):
@@ -295,28 +328,24 @@
 
     def tile(index, carry):
         where = pl.ds(pl.multiple_of(index * cols, cols), cols)
-        result, at = None, 0
-        for ref in (own_ref, near_ref, far_ref):
-            term = lax.dot_general(
-                slopes[:, at : at + ref.shape[1]],
-                ref[where, :],
-                (((1,), (1,)), ((), ())),
-                preferred_element_type=jnp.float32,
-            )
-            result = term if result is None else result + term
-            at += ref.shape[1]
+        result = lax.dot_general(
+            slopes[...],
+            weights_ref[where, :],
+            (((1,), (1,)), ((), ())),
+            preferred_element_type=jnp.float32,
+        )
         at = 0
         for ref in out_refs:
             ref[:, where] = result[at : at + ref.shape[0]].astype(ref.dtype)
             at += ref.shape[0]
         return carry
 
-    lax.fori_loop(0, own_ref.shape[0] // cols, tile, 0)
-
-
-def gradient(slope, coefficient, weights, split, cols=256):
+    lax.fori_loop(0, weights_ref.shape[0] // cols, tile, 0)
+
+
+def gradient(slope, coefficient, weights, split, cols=512):
     rows, entries = slope.shape
-    width = weights[0].shape[0]
+    width = weights.shape[0]
 
     def body(*refs):
         gradient_kernel(len(split), cols, *refs)
@@ -324,7 +353,7 @@
     return simple_call(
         body,
         [jax.ShapeDtypeStruct((n, width), jnp.bfloat16) for n in split],
-        [slope, coefficient, *weights],
+        [slope, coefficient, weights],
         scratch=[pltpu.VMEM((rows, entries), jnp.bfloat16)],
         grant=12,
         flops=4 * max(rows, 256) * width * entries,
@@ -483,10 +512,8 @@
     half = entries // 2
     near = move(lax.dynamic_slice_in_dim(head_weight, c_at * half, half, 1), u=1)
     far = move(near, c=1)
-    weights = (head_weight, near, far)
-    other_bias = move(head_bias.reshape(1, entries), u=1)
-
-    bias = jnp.concatenate([head_bias.reshape(1, entries), swap_halves(other_bias)], axis=1)
+    own_bias = head_bias.reshape(1, entries)
+    other_bias = move(own_bias, u=1)
 
     carry = attend_chunks(doc_lengths, qkv, [(qkv, 1), (qkv, 2)], [0], None, False)
     carry = attend_chunks(
@@ -514,6 +541,7 @@
     far_first = move(rows_of(rows[1, -1], 0, tokens), z=1)
     far_second = move(rows_of(rows[1, 1], tokens, tokens), z=-1)
 
+    weights, bias = side_by_side(head_weight, near, far, own_bias, other_bias)
     waves = [[(0, 0)], [(1, 0), (0, -1), (0, 1)], [(1, -1), (0, 2), (1, 1)], [(1, 2)]]
     slopes, sums = [], []
     for wave in waves:

time: 236 us -> 238 us (level)
  waiting for transfers between devices: 74.3 us -> 94.5 us
  Pallas kernels: 90.8 us -> 73 us
    pallas_call x18, Pallas kernels: 55.4 us -> 34.1 us  [simple_call(): pl.pallas_call(body, in_specs=in_specs, out_specs=jax.tree.map(lambda _:...]
    ppermute x26, waiting for transfers between devices: 45.7 us -> 65.8 us  [move(): return lax.ppermute(array, AXES, shift_perm(sizes, **by))]
    pallas_call x0 -> x1, Pallas kernels: none -> 3.5 us  [side_by_side(): pl.pallas_call(body, in_specs=[pl.BlockSpec(memory_space=pl.ANY)] * 3 + [...]
  transfers between devices with their start and end apart: 28 -> 28, of which waited for: 14 -> 16; matrix products, arithmetic and copies ran while one was open for 1% -> 1% of each run, Pallas kernels for 33% -> 28%
where the time goes in v4:
time: 238 us; the launch traced here: 237 us
  waiting for transfers between devices  94.5 us (40%)
  Pallas kernels  73 us (31%)
  starting transfers between devices  49.6 us (21%)
  blocking collectives  10.4 us (4%)
  local copies, waits for them, and re-layouts  7.4 us (3%)
    ppermute x26, waiting for transfers between devices, move(): return lax.ppermute(array, AXES, shift_perm(sizes, **by))  65.8 us
    ppermute x26, starting transfers between devices, move(): return lax.ppermute(array, AXES, shift_perm(sizes, **by))  35.4 us
    pallas_call x3, Pallas kernels, attend_chunks(): pl.pallas_call(body, grid_spec=pltpu.PrefetchScalarGridSpec(num_scalar_pr...  34.9 us
    pallas_call x18, Pallas kernels, simple_call(): pl.pallas_call(body, in_specs=in_specs, out_specs=jax.tree.map(lambda _:...  34.1 us
    all_to_all x1, waiting for transfers between devices, local(): lax.all_to_all(stacked, PLANE, split_axis=0, concat_axis=0, tiled=True)  16.8 us
    all_to_all x1, waiting for transfers between devices, local(): lax.all_to_all(attended, PLANE, split_axis=0, concat_axis=0, tiled=True)  11.8 us
    all_to_all x1, blocking collectives, local(): lax.all_to_all(spread, ('y', 'c'), split_axis=0, concat_axis=0, tiled=True)  10.4 us
    all_to_all x1, starting transfers between devices, local(): lax.all_to_all(stacked, PLANE, split_axis=0, concat_axis=0, tiled=True)  8.28 us
  transfers between devices with their start and end apart: 28, of which 16 were waited for; matrix products, arithmetic and copies ran while one was open for 1% of the time, Pallas kernels for 28%

profile of v4, /device:TPU:0, one launch (start us, length us, event | category | flops | bytes accessed | tf_op | source)
XLA Modules:
  0.0 237.1 jit_solution(5807008083729339683)
XLA Ops:
  0.6 1.5 reshape.23
  2.1 0.2 copy.20
  2.3 0.3 reshape.24
  2.7 0.2 copy.21
  2.9 0.3 reshape.25
  3.2 0.2 copy.22
  3.5 1.4 pad_maximum_fusion
  4.8 8.3 %all-to-all-start = ((bf16[32,3,64,128]{3,2,1,0:T(8,128)(2,1)}), bf16[32,3,64,128]{3,2,1,0:T(8,128)(2,1)S(1)}, u32[]{:S(2)}, u32[]{:S(2)}) async-start(bf16[32,3,64,128]{3,2,1,0:T(8,128)(2,1)} %pad_maximum_fusion), calls=%async_computation | async-start | bytes 3145728 | tf_op jit(solution)/shard_map/all_to_all | solution.py:502
  13.1 3.1 %constant_dynamic-slice_fusion = bf16[2048,512]{1,0:T(8,128)(2,1)} fusion(bf16[2048,1024]{1,0:T(8,128)(2,1)} %own_hbm.1, s32[]{:T(128)S(6)} %select_n.3), kind=kLoop, calls=%fused_computation.5 | loop fusion | bytes 4194308 | tf_op jit(solution)/shard_map/dynamic_slice | solution.py:513
  16.2 3.3 %collective-permute-start = (bf16[2048,512]{1,0:T(8,128)(2,1)}, bf16[2048,512]{1,0:T(8,128)(2,1)}, u32[]{:S(2)}, u32[]{:S(2)}) collective-permute-start(bf16[2048,512]{1,0:T(8,128)(2,1)} %constant_dynamic-slice_fusion), channel_id=1, source_target_pairs={{0,8},{1,9},{2,10},{3,11},{4,12},{5,13},{6,14},{7,15},{8,0},{9,1},... | collective-permute-start | bytes 6291464 | tf_op jit(solution)/shard_map/ppermute | solution.py:499
  19.5 16.8 %all-to-all-done.refs_1_.refs_2_.refs_3_ = bf16[32,3,64,128]{3,2,1,0:T(8,128)(2,1)S(1)} async-done(((bf16[32,3,64,128]{3,2,1,0:T(8,128)(2,1)}), bf16[32,3,64,128]{3,2,1,0:T(8,128)(2,1)S(1)}, u32[]{:S(2)}, u32[]{:S(2)}) %all-to-all-start) | async-done | bytes 1572896 | tf_op jit(solution)/shard_map/all_to_all | solution.py:502
  36.4 1.6 collective-permute-start.3
  38.0 1.7 collective-permute-start.5
  39.7 0.4 collective-permute-start.7
  40.1 2.9 %collective-permute-start.8 = (bf16[32,64,128]{2,1,0:T(8,128)(2,1)S(1)}, bf16[32,64,128]{2,1,0:T(8,128)(2,1)S(1)}, u32[]{:S(2)}, u32[]{:S(2)}) collective-permute-start(bf16[32,64,128]{2,1,0:T(8,128)(2,1)S(1)} %get-tuple-element.55), channel_id=1, source_target_pairs={{0,96},{1,97},{2,98},{3,99},{4,100},{5,101},{6,102},{7,103},{8,104... | collective-permute-start | bytes 1572872 | tf_op jit(solution)/shard_map/ppermute | solution.py:499
  42.9 6.6 %attend_first.1 = (f32[2048,128]{1,0:T(8,128)S(1)}, f32[2048,256]{1,0:T(8,128)S(1)}) custom-call(s32[2]{0:T(128)S(1)} %copy-done.2, bf16[32,3,64,128]{3,2,1,0:T(8,128)(2,1)S(1)} %all-to-all-done.refs_1_.refs_2_.refs_3_, bf16[32,3,64,128]{3,2,1,0:T(8,128)(2,1)S(1)} %all-to-all-done.refs_1_.refs_2_.refs_3_, ...), custom_call_target="tpu_custom_call" | custom-call | flops 4294967296 | bytes 4194304 | tf_op jit(solution)/shard_map/attend_first/pallas_call | solution.py:182
  49.5 2.9 %collective-permute-done.3.refs_2_ = bf16[32,64,128]{2,1,0:T(8,128)(2,1)S(1)} collective-permute-done((bf16[32,64,128]{2,1,0:T(8,128)(2,1)S(1)}, bf16[32,64,128]{2,1,0:T(8,128)(2,1)S(1)}, u32[]{:S(2)}, u32[]{:S(2)}) %collective-permute-start.3) | collective-permute-done | bytes 524320 | tf_op jit(solution)/shard_map/ppermute | solution.py:499
  52.5 0.4 collective-permute-start.4
  52.8 2.9 %collective-permute-start.6 = (bf16[32,64,128]{2,1,0:T(8,128)(2,1)S(1)}, bf16[32,64,128]{2,1,0:T(8,128)(2,1)S(1)}, u32[]{:S(2)}, u32[]{:S(2)}) collective-permute-start(bf16[32,64,128]{2,1,0:T(8,128)(2,1)S(1)} %collective-permute-done.5.refs_5_), channel_id=1, source_target_pairs={{0,96},{1,97},{2,98},{3,99},{4,100},{5,101},{6,102},{7,103},{8,104... | collective-permute-start | bytes 1572872 | tf_op jit(solution)/shard_map/ppermute | solution.py:499
  55.7 23.7 %collective-permute-done.near_hbm = bf16[2048,512]{1,0:T(8,128)(2,1)} collective-permute-done((bf16[2048,512]{1,0:T(8,128)(2,1)}, bf16[2048,512]{1,0:T(8,128)(2,1)}, u32[]{:S(2)}, u32[]{:S(2)}) %collective-permute-start) | collective-permute-done | bytes 2097184 | tf_op jit(solution)/shard_map/ppermute | solution.py:499
  79.5 18.1 %attend_next.1 = (f32[2048,128]{1,0:T(8,128)S(1)}, f32[2048,256]{1,0:T(8,128)S(1)}) custom-call(s32[2]{0:T(128)S(1)} %copy-done.2, bf16[32,3,64,128]{3,2,1,0:T(8,128)(2,1)S(1)} %all-to-all-done.refs_1_.refs_2_.refs_3_, bf16[32,64,128]{2,1,0:T(8,128)(2,1)S(1)} %collective-permute-done.3.refs_2_, bf16[32,64,128]{2,1,0:T(8,128)(2,1)S(1)} %collective-permute-done.7.refs_3_, ...), custom_call_target="tpu_custom_call" | custom-call | flops 8589934592 | bytes 4194304 | tf_op jit(solution)/shard_map/attend_next/pallas_call | solution.py:182
  97.6 10.3 %attend_last.1 = bf16[32,64,128]{2,1,0:T(8,128)(2,1)} custom-call(s32[2]{0:T(128)S(1)} %copy-done.2, bf16[32,3,64,128]{3,2,1,0:T(8,128)(2,1)S(1)} %all-to-all-done.refs_1_.refs_2_.refs_3_, bf16[32,64,128]{2,1,0:T(8,128)(2,1)S(1)} %collective-permute-done.4.refs_2_, bf16[32,64,128]{2,1,0:T(8,128)(2,1)S(1)} %collective-permute-done.6.refs_3_, ...), custom_call_target="tpu_custom_call" | custom-call | flops 4294967296 | bytes 4194304 | tf_op jit(solution)/shard_map/attend_last/pallas_call | solution.py:182
  107.9 5.9 %all-to-all-start.1 = ((bf16[32,64,128]{2,1,0:T(8,128)(2,1)}), bf16[32,64,128]{2,1,0:T(8,128)(2,1)S(1)}, u32[]{:S(2)}, u32[]{:S(2)}) async-start(bf16[32,64,128]{2,1,0:T(8,128)(2,1)} %attend_last.1), calls=%async_computation.1 | async-start | bytes 1048576 | tf_op jit(solution)/shard_map/all_to_all | solution.py:530
  113.9 11.8 %all-to-all-done.1.refs_0_ = bf16[32,64,128]{2,1,0:T(8,128)(2,1)S(1)} async-done(((bf16[32,64,128]{2,1,0:T(8,128)(2,1)}), bf16[32,64,128]{2,1,0:T(8,128)(2,1)S(1)}, u32[]{:S(2)}, u32[]{:S(2)}) %all-to-all-start.1) | async-done | bytes 524320 | tf_op jit(solution)/shard_map/all_to_all | solution.py:530
  125.7 0.4 normalized.1.refs_3_
  126.2 0.3 collective-permute-start.10
  126.5 0.6 collective-permute-start.9
  127.1 13.4 %collective-permute-done.10.refs_4_ = bf16[128,2048]{1,0:T(8,128)(2,1)S(1)} collective-permute-done((bf16[128,2048]{1,0:T(8,128)(2,1)S(1)}, bf16[128,2048]{1,0:T(8,128)(2,1)S(1)}, u32[]{:S(2)}, u32[]{:S(2)}) %collective-permute-start.10) | collective-permute-done | bytes 524320 | tf_op jit(solution)/shard_map/ppermute | solution.py:499
  140.5 1.0 collective-permute-start.12
  141.5 1.2 collective-permute-start.14
  142.7 0.8 collective-permute-start.13
  143.6 2.4 collective-permute-start.2
  145.9 6.8 %collective-permute-done.12.refs_3_.in_ref = bf16[128,2048]{1,0:T(8,128)(2,1)S(1)} collective-permute-done((bf16[128,2048]{1,0:T(8,128)(2,1)S(1)}, bf16[128,2048]{1,0:T(8,128)(2,1)S(1)}, u32[]{:S(2)}, u32[]{:S(2)}) %collective-permute-start.12) | collective-permute-done | bytes 524320 | tf_op jit(solution)/shard_map/ppermute | solution.py:499
  152.7 0.8 collective-permute-start.11
  153.5 1.1 collective-permute-done.14.refs_5_.in_ref
  154.8 0.2 collective-permute-done.2.other_bias_ref
  155.1 2.9 %collective-permute-start.16 = (bf16[64,2048]{1,0:T(8,128)(2,1)S(1)}, bf16[64,2048]{1,0:T(8,128)(2,1)S(1)}, u32[]{:S(2)}, u32[]{:S(2)}) collective-permute-start(bf16[64,2048]{1,0:T(8,128)(2,1)S(1)} %shard_map.99), channel_id=1, source_target_pairs={{0,3},{1,0},{2,1},{3,2},{4,7},{5,4},{6,5},{7,6},{8,11},{9,8},{10,9... | collective-permute-start | bytes 786440 | tf_op jit(solution)/shard_map/ppermute | solution.py:499
  158.0 3.5 %side_by_side.1 = (bf16[2048,2048]{1,0:T(8,128)(2,1)S(1)}, f32[1,2048]{1,0:T(1,128)S(1)}) custom-call(bf16[2048,1024]{1,0:T(8,128)(2,1)} %own_hbm.1, bf16[2048,512]{1,0:T(8,128)(2,1)} %collective-permute-done.near_hbm, bf16[2048,512]{1,0:T(8,128)(2,1)} %collective-permute-done.1.far_hbm, f32[1,1024]{1,0:T(1,128)S(1)} %bitcast.30, ...), custom_call_target="tpu_custom_call" | custom-call | bytes 16777216 | tf_op jit(solution)/shard_map/side_by_side/pallas_call | solution.py:266
  161.5 5.7 %shard_map.97 = (f32[384,2048]{1,0:T(8,128)S(1)}, f32[2,2048]{1,0:T(2,128)S(1)}) custom-call(s32[2]{0:T(128)S(1)} %copy-done.2, bf16[2048,2048]{1,0:T(8,128)(2,1)S(1)} %get-tuple-element.28.refs_1_.refs_2_, f32[1,2048]{1,0:T(1,128)S(1)} %get-tuple-element.29.refs_2_, bf16[128,2048]{1,0:T(8,128)(2,1)S(1)} %collective-permute-done.12.refs_3_.in_ref, ...), custom_call_target="tpu_custom_call" | custom-call | flops 6442450944 | bytes 19939344 | tf_op jit(solution)/shard_map/pallas_call | solution.py:289
  167.2 0.3 collective-permute-done.11.refs_5_
  167.5 5.7 %shard_map.96 = (f32[384,2048]{1,0:T(8,128)S(1)}, f32[2,2048]{1,0:T(2,128)S(1)}) custom-call(s32[2]{0:T(128)S(1)} %copy-done.2, bf16[2048,2048]{1,0:T(8,128)(2,1)S(1)} %get-tuple-element.28.refs_1_.refs_2_, f32[1,2048]{1,0:T(1,128)S(1)} %get-tuple-element.29.refs_2_, bf16[128,2048]{1,0:T(8,128)(2,1)S(1)} %collective-permute-done.9.refs_3_, ...), custom_call_target="tpu_custom_call" | custom-call | flops 6442450944 | bytes 19939344 | tf_op jit(solution)/shard_map/pallas_call | solution.py:289
  173.2 2.8 %shard_map.95 = (f32[128,2048]{1,0:T(8,128)S(1)}, f32[2,2048]{1,0:T(2,128)S(1)}) custom-call(s32[2]{0:T(128)S(1)} %copy-done.2, bf16[2048,2048]{1,0:T(8,128)(2,1)S(1)} %get-tuple-element.28.refs_1_.refs_2_, f32[1,2048]{1,0:T(1,128)S(1)} %get-tuple-element.29.refs_2_, bf16[128,2048]{1,0:T(8,128)(2,1)S(1)} %normalized.1.refs_3_), custom_call_target="tpu_custom_call" | custom-call | flops 4294967296 | bytes 17842192 | tf_op jit(solution)/shard_map/pallas_call | solution.py:289
  176.0 2.8 %shard_map.100 = (f32[128,2048]{1,0:T(8,128)S(1)}, f32[2,2048]{1,0:T(2,128)S(1)}) custom-call(s32[2]{0:T(128)S(1)} %copy-done.2, bf16[2048,2048]{1,0:T(8,128)(2,1)S(1)} %get-tuple-element.28.refs_1_.refs_2_, f32[1,2048]{1,0:T(1,128)S(1)} %get-tuple-element.29.refs_2_, bf16[64,2048]{1,0:T(8,128)(2,1)S(1)} %collective-permute-done.15.refs_3_, ...), custom_call_target="tpu_custom_call" | custom-call | flops 4294967296 | bytes 17842192 | tf_op jit(solution)/shard_map/pallas_call | solution.py:289
  178.8 2.7 %collective-permute-start.17 = (f32[4,1024]{1,0:T(4,128)S(1)}, f32[4,1024]{1,0:T(4,128)S(1)}, u32[]{:S(2)}, u32[]{:S(2)}) collective-permute-start(f32[4,1024]{1,0:T(4,128)S(1)} %get-tuple-element.39), channel_id=1, source_target_pairs={{0,8},{1,9},{2,10},{3,11},{4,12},{5,13},{6,14},{7,15},{8,0},{9,1},... | collective-permute-start | bytes 49160 | tf_op jit(solution)/shard_map/ppermute | solution.py:499
  181.5 2.6 %collective-permute-done.17.two_ref = f32[4,1024]{1,0:T(4,128)S(1)} collective-permute-done((f32[4,1024]{1,0:T(4,128)S(1)}, f32[4,1024]{1,0:T(4,128)S(1)}, u32[]{:S(2)}, u32[]{:S(2)}) %collective-permute-start.17) | collective-permute-done | bytes 16416 | tf_op jit(solution)/shard_map/ppermute | solution.py:499
  184.2 10.4 %all_to_all.15.gathered_ref = f32[8,4,1024]{2,1,0:T(4,128)S(1)} all-to-all(f32[8,4,1024]{2,1,0:T(4,128)S(1)} %shard_map.102), channel_id=1, replica_groups=mesh['y'=4,'c'=2,'u'=2,'w'=2,'z'=4] {'y','c'}, dimensions={0} | all-to-all | bytes 262144 | tf_op jit(solution)/shard_map/all_to_all | solution.py:555
  194.6 1.2 shard_map.103
  195.7 3.4 %shard_map.107 = (bf16[64,2048]{1,0:T(8,128)(2,1)S(1)}, bf16[64,2048]{1,0:T(8,128)(2,1)S(1)}) custom-call(f32[128,2048]{1,0:T(8,128)S(1)} %get-tuple-element.47.refs_0_, f32[2,2048]{1,0:T(2,128)S(1)} %get-tuple-element.42.refs_1_, bf16[2048,2048]{1,0:T(8,128)(2,1)S(1)} %get-tuple-element.28.refs_1_.refs_2_), custom_call_target="tpu_custom_call" | custom-call | flops 4294967296 | bytes 18907136 | tf_op jit(solution)/shard_map/pallas_call | solution.py:289
  199.1 2.1 collective-permute-start.21
  201.2 4.2 %shard_map.106 = (bf16[128,2048]{1,0:T(8,128)(2,1)S(1)}, bf16[128,2048]{1,0:T(8,128)(2,1)S(1)}, bf16[128,2048]{1,0:T(8,128)(2,1)S(1)}) custom-call(f32[384,2048]{1,0:T(8,128)S(1)} %get-tuple-element.45.refs_0_, f32[2,2048]{1,0:T(2,128)S(1)} %get-tuple-element.42.refs_1_, bf16[2048,2048]{1,0:T(8,128)(2,1)S(1)} %get-tuple-element.28.refs_1_.refs_2_), custom_call_target="tpu_custom_call" | custom-call | flops 6442450944 | bytes 23101440 | tf_op jit(solution)/shard_map/pallas_call | solution.py:289
  205.4 3.3 %collective-permute-start.23 = (bf16[128,2048]{1,0:T(8,128)(2,1)S(1)}, bf16[128,2048]{1,0:T(8,128)(2,1)S(1)}, u32[]{:S(2)}, u32[]{:S(2)}) collective-permute-start(bf16[128,2048]{1,0:T(8,128)(2,1)S(1)} %get-tuple-element.52), channel_id=1, source_target_pairs={{0,3},{1,0},{2,1},{3,2},{4,7},{5,4},{6,5},{7,6},{8,11},{9,8},{10,9... | collective-permute-start | bytes 1572872 | tf_op jit(solution)/shard_map/ppermute | solution.py:499
  208.8 1.1 collective-permute-start.22
  210.2 4.2 %shard_map.105 = (bf16[128,2048]{1,0:T(8,128)(2,1)S(1)}, bf16[128,2048]{1,0:T(8,128)(2,1)S(1)}, bf16[128,2048]{1,0:T(8,128)(2,1)S(1)}) custom-call(f32[384,2048]{1,0:T(8,128)S(1)} %get-tuple-element.43.refs_0_, f32[2,2048]{1,0:T(2,128)S(1)} %get-tuple-element.42.refs_1_, bf16[2048,2048]{1,0:T(8,128)(2,1)S(1)} %get-tuple-element.28.refs_1_.refs_2_), custom_call_target="tpu_custom_call" | custom-call | flops 6442450944 | bytes 23101440 | tf_op jit(solution)/shard_map/pallas_call | solution.py:289
  214.5 4.7 %collective-permute-done.23.refs_1_ = bf16[128,2048]{1,0:T(8,128)(2,1)S(1)} collective-permute-done((bf16[128,2048]{1,0:T(8,128)(2,1)S(1)}, bf16[128,2048]{1,0:T(8,128)(2,1)S(1)}, u32[]{:S(2)}, u32[]{:S(2)}) %collective-permute-start.23) | collective-permute-done | bytes 524320 | tf_op jit(solution)/shard_map/ppermute | solution.py:499
  219.2 2.4 collective-permute-done.22.refs_0_
  221.5 0.2 shard_map.111
  221.7 1.6 collective-permute-start.24
  223.3 2.8 %collective-permute-done.19.refs_0_ = bf16[128,2048]{1,0:T(8,128)(2,1)S(1)} collective-permute-done((bf16[128,2048]{1,0:T(8,128)(2,1)S(1)}, bf16[128,2048]{1,0:T(8,128)(2,1)S(1)}, u32[]{:S(2)}, u32[]{:S(2)}) %collective-permute-start.19) | collective-permute-done | bytes 524320 | tf_op jit(solution)/shard_map/ppermute | solution.py:499
  226.3 1.1 collective-permute-start.20
  227.4 3.4 %shard_map.104.base_ref = bf16[128,2048]{1,0:T(8,128)(2,1)S(1)} custom-call(f32[128,2048]{1,0:T(8,128)S(1)} %get-tuple-element.41.refs_0_, f32[2,2048]{1,0:T(2,128)S(1)} %get-tuple-element.42.refs_1_, bf16[2048,2048]{1,0:T(8,128)(2,1)S(1)} %get-tuple-element.28.refs_1_.refs_2_), custom_call_target="tpu_custom_call" | custom-call | flops 4294967296 | bytes 18907136 | tf_op jit(solution)/shard_map/pallas_call | solution.py:289
  230.8 4.1 %collective-permute-done.25.refs_2_ = bf16[128,2048]{1,0:T(8,128)(2,1)S(1)} collective-permute-done((bf16[128,2048]{1,0:T(8,128)(2,1)S(1)}, bf16[128,2048]{1,0:T(8,128)(2,1)S(1)}, u32[]{:S(2)}, u32[]{:S(2)}) %collective-permute-start.25) | collective-permute-done | bytes 524320 | tf_op jit(solution)/shard_map/ppermute | solution.py:499
  234.9 0.6 collective-permute-done.20.refs_0_
  235.5 0.3 shard_map.112
  235.8 1.3 copy.31
  (39 shorter events, 1.0 us)
Async XLA Ops:
  0.6 1.7 copy-start.3
  0.6 2.3 copy-start.4
  4.8 31.5 %all-to-all-start = ((bf16[32,3,64,128]{3,2,1,0:T(8,128)(2,1)}), bf16[32,3,64,128]{3,2,1,0:T(8,128)(2,1)S(1)}, u32[]{:S(2)}, u32[]{:S(2)}) async-start(bf16[32,3,64,128]{3,2,1,0:T(8,128)(2,1)} %pad_maximum_fusion), calls=%async_computation | async-start | bytes 3145728 | tf_op jit(solution)/shard_map/all_to_all | solution.py:502
  16.2 26.8 %copy-start.2 = (s32[2]{0:T(128)S(1)}, s32[2]{0:T(128)}, u32[]{:S(2)}) copy-start(s32[2]{0:T(128)} %lengths_ref.1) | copy-start | bytes 28
  16.2 63.3 %collective-permute-start = (bf16[2048,512]{1,0:T(8,128)(2,1)}, bf16[2048,512]{1,0:T(8,128)(2,1)}, u32[]{:S(2)}, u32[]{:S(2)}) collective-permute-start(bf16[2048,512]{1,0:T(8,128)(2,1)} %constant_dynamic-slice_fusion), channel_id=1, source_target_pairs={{0,8},{1,9},{2,10},{3,11},{4,12},{5,13},{6,14},{7,15},{8,0},{9,1},... | collective-permute-start | bytes 6291464 | tf_op jit(solution)/shard_map/ppermute | solution.py:499
  36.4 16.1 %collective-permute-start.3 = (bf16[32,64,128]{2,1,0:T(8,128)(2,1)S(1)}, bf16[32,64,128]{2,1,0:T(8,128)(2,1)S(1)}, u32[]{:S(2)}, u32[]{:S(2)}) collective-permute-start(bf16[32,64,128]{2,1,0:T(8,128)(2,1)S(1)} %get-tuple-element.55), channel_id=1, source_target_pairs={{0,32},{1,33},{2,34},{3,35},{4,36},{5,37},{6,38},{7,39},{8,40},{9,... | collective-permute-start | bytes 1572872 | tf_op jit(solution)/shard_map/ppermute | solution.py:499
  38.0 14.8 %collective-permute-start.5 = (bf16[32,64,128]{2,1,0:T(8,128)(2,1)S(1)}, bf16[32,64,128]{2,1,0:T(8,128)(2,1)S(1)}, u32[]{:S(2)}, u32[]{:S(2)}) collective-permute-start(bf16[32,64,128]{2,1,0:T(8,128)(2,1)S(1)} %get-tuple-element.54), channel_id=1, source_target_pairs={{0,96},{1,97},{2,98},{3,99},{4,100},{5,101},{6,102},{7,103},{8,104... | collective-permute-start | bytes 1572872 | tf_op jit(solution)/shard_map/ppermute | solution.py:499
  39.7 39.8 %collective-permute-start.7 = (bf16[32,64,128]{2,1,0:T(8,128)(2,1)S(1)}, bf16[32,64,128]{2,1,0:T(8,128)(2,1)S(1)}, u32[]{:S(2)}, u32[]{:S(2)}) collective-permute-start(bf16[32,64,128]{2,1,0:T(8,128)(2,1)S(1)} %get-tuple-element.54), channel_id=1, source_target_pairs={{0,32},{1,33},{2,34},{3,35},{4,36},{5,37},{6,38},{7,39},{8,40},{9,... | collective-permute-start | bytes 1572872 | tf_op jit(solution)/shard_map/ppermute | solution.py:499
  40.1 39.4 %collective-permute-start.8 = (bf16[32,64,128]{2,1,0:T(8,128)(2,1)S(1)}, bf16[32,64,128]{2,1,0:T(8,128)(2,1)S(1)}, u32[]{:S(2)}, u32[]{:S(2)}) collective-permute-start(bf16[32,64,128]{2,1,0:T(8,128)(2,1)S(1)} %get-tuple-element.55), channel_id=1, source_target_pairs={{0,96},{1,97},{2,98},{3,99},{4,100},{5,101},{6,102},{7,103},{8,104... | collective-permute-start | bytes 1572872 | tf_op jit(solution)/shard_map/ppermute | solution.py:499
  52.5 45.1 %collective-permute-start.4 = (bf16[32,64,128]{2,1,0:T(8,128)(2,1)S(1)}, bf16[32,64,128]{2,1,0:T(8,128)(2,1)S(1)}, u32[]{:S(2)}, u32[]{:S(2)}) collective-permute-start(bf16[32,64,128]{2,1,0:T(8,128)(2,1)S(1)} %collective-permute-done.3.refs_2_), channel_id=1, source_target_pairs={{0,32},{1,33},{2,34},{3,35},{4,36},{5,37},{6,38},{7,39},{8,40},{9,... | collective-permute-start | bytes 1572872 | tf_op jit(solution)/shard_map/ppermute | solution.py:499
  52.8 44.7 %collective-permute-start.6 = (bf16[32,64,128]{2,1,0:T(8,128)(2,1)S(1)}, bf16[32,64,128]{2,1,0:T(8,128)(2,1)S(1)}, u32[]{:S(2)}, u32[]{:S(2)}) collective-permute-start(bf16[32,64,128]{2,1,0:T(8,128)(2,1)S(1)} %collective-permute-done.5.refs_5_), channel_id=1, source_target_pairs={{0,96},{1,97},{2,98},{3,99},{4,100},{5,101},{6,102},{7,103},{8,104... | collective-permute-start | bytes 1572872 | tf_op jit(solution)/shard_map/ppermute | solution.py:499
  79.5 78.5 %collective-permute-start.1 = (bf16[2048,512]{1,0:T(8,128)(2,1)}, bf16[2048,512]{1,0:T(8,128)(2,1)}, u32[]{:S(2)}, u32[]{:S(2)}) collective-permute-start(bf16[2048,512]{1,0:T(8,128)(2,1)} %collective-permute-done.near_hbm), channel_id=1, source_target_pairs={{0,16},{1,17},{2,18},{3,19},{4,20},{5,21},{6,22},{7,23},{8,24},{9,... | collective-permute-start | bytes 6291464 | tf_op jit(solution)/shard_map/ppermute | solution.py:499
  97.6 16.2 %copy-start.5 = (bf16[64,2,2048]{2,1,0:T(2,128)(2,1)S(1)}, bf16[64,2,2048]{2,1,0:T(2,128)(2,1)}, u32[]{:S(2)}) copy-start(bf16[64,2,2048]{2,1,0:T(2,128)(2,1)} %param.11) | copy-start | bytes 1572868
  107.9 17.9 %copy-start = (f32[2048]{0:T(1024)S(1)}, f32[2048]{0:T(1024)}, u32[]{:S(2)}) copy-start(f32[2048]{0:T(1024)} %param.12) | copy-start | bytes 24580
  107.9 35.7 %copy-start.1 = (f32[1024]{0:T(1024)S(1)}, f32[1024]{0:T(1024)}, u32[]{:S(2)}) copy-start(f32[1024]{0:T(1024)} %param.14) | copy-start | bytes 12292
  107.9 17.9 %all-to-all-start.1 = ((bf16[32,64,128]{2,1,0:T(8,128)(2,1)}), bf16[32,64,128]{2,1,0:T(8,128)(2,1)S(1)}, u32[]{:S(2)}, u32[]{:S(2)}) async-start(bf16[32,64,128]{2,1,0:T(8,128)(2,1)} %attend_last.1), calls=%async_computation.1 | async-start | bytes 1048576 | tf_op jit(solution)/shard_map/all_to_all | solution.py:530
  126.2 14.3 %collective-permute-start.10 = (bf16[128,2048]{1,0:T(8,128)(2,1)S(1)}, bf16[128,2048]{1,0:T(8,128)(2,1)S(1)}, u32[]{:S(2)}, u32[]{:S(2)}) collective-permute-start(bf16[128,2048]{1,0:T(8,128)(2,1)S(1)} %normalized.1.refs_3_), channel_id=1, source_target_pairs={{0,1},{1,2},{2,3},{3,0},{4,5},{5,6},{6,7},{7,4},{8,9},{9,10},{10,1... | collective-permute-start | bytes 1572872 | tf_op jit(solution)/shard_map/ppermute | solution.py:499
  126.5 15.0 %collective-permute-start.9 = (bf16[128,2048]{1,0:T(8,128)(2,1)S(1)}, bf16[128,2048]{1,0:T(8,128)(2,1)S(1)}, u32[]{:S(2)}, u32[]{:S(2)}) collective-permute-start(bf16[128,2048]{1,0:T(8,128)(2,1)S(1)} %normalized.1.refs_3_), channel_id=1, source_target_pairs={{0,4},{1,5},{2,6},{3,7},{4,0},{5,1},{6,2},{7,3},{8,12},{9,13},{10,... | collective-permute-start | bytes 1572872 | tf_op jit(solution)/shard_map/ppermute | solution.py:499
  140.5 12.2 %collective-permute-start.12 = (bf16[128,2048]{1,0:T(8,128)(2,1)S(1)}, bf16[128,2048]{1,0:T(8,128)(2,1)S(1)}, u32[]{:S(2)}, u32[]{:S(2)}) collective-permute-start(bf16[128,2048]{1,0:T(8,128)(2,1)S(1)} %collective-permute-done.10.refs_4_), channel_id=1, source_target_pairs={{0,4},{1,5},{2,6},{3,7},{4,0},{5,1},{6,2},{7,3},{8,12},{9,13},{10,... | collective-permute-start | bytes 1572872 | tf_op jit(solution)/shard_map/ppermute | solution.py:499
  141.5 13.1 %collective-permute-start.14 = (bf16[128,2048]{1,0:T(8,128)(2,1)S(1)}, bf16[128,2048]{1,0:T(8,128)(2,1)S(1)}, u32[]{:S(2)}, u32[]{:S(2)}) collective-permute-start(bf16[128,2048]{1,0:T(8,128)(2,1)S(1)} %collective-permute-done.9.refs_3_), channel_id=1, source_target_pairs={{0,3},{1,0},{2,1},{3,2},{4,7},{5,4},{6,5},{7,6},{8,11},{9,8},{10,9... | collective-permute-start | bytes 1572872 | tf_op jit(solution)/shard_map/ppermute | solution.py:499
  142.7 18.8 %collective-permute-start.13 = (bf16[128,2048]{1,0:T(8,128)(2,1)S(1)}, bf16[128,2048]{1,0:T(8,128)(2,1)S(1)}, u32[]{:S(2)}, u32[]{:S(2)}) collective-permute-start(bf16[128,2048]{1,0:T(8,128)(2,1)S(1)} %collective-permute-done.10.refs_4_), channel_id=1, source_target_pairs={{0,1},{1,2},{2,3},{3,0},{4,5},{5,6},{6,7},{7,4},{8,9},{9,10},{10,1... | collective-permute-start | bytes 1572872 | tf_op jit(solution)/shard_map/ppermute | solution.py:499
  143.6 11.5 %collective-permute-start.2 = (f32[1,1024]{1,0:T(1,128)S(1)}, f32[1,1024]{1,0:T(1,128)S(1)}, u32[]{:S(2)}, u32[]{:S(2)}) collective-permute-start(f32[1,1024]{1,0:T(1,128)S(1)} %bitcast.29), channel_id=1, source_target_pairs={{0,8},{1,9},{2,10},{3,11},{4,12},{5,13},{6,14},{7,15},{8,0},{9,1},... | collective-permute-start | bytes 12296 | tf_op jit(solution)/shard_map/ppermute | solution.py:499
  152.7 14.8 %collective-permute-start.11 = (bf16[128,2048]{1,0:T(8,128)(2,1)S(1)}, bf16[128,2048]{1,0:T(8,128)(2,1)S(1)}, u32[]{:S(2)}, u32[]{:S(2)}) collective-permute-start(bf16[128,2048]{1,0:T(8,128)(2,1)S(1)} %normalized.1.refs_3_), channel_id=1, source_target_pairs={{0,3},{1,0},{2,1},{3,2},{4,7},{5,4},{6,5},{7,6},{8,11},{9,8},{10,9... | collective-permute-start | bytes 1572872 | tf_op jit(solution)/shard_map/ppermute | solution.py:499
  154.6 21.3 %collective-permute-start.15 = (bf16[64,2048]{1,0:T(8,128)(2,1)S(1)}, bf16[64,2048]{1,0:T(8,128)(2,1)S(1)}, u32[]{:S(2)}, u32[]{:S(2)}) collective-permute-start(bf16[64,2048]{1,0:T(8,128)(2,1)S(1)} %shard_map.98), channel_id=1, source_target_pairs={{0,1},{1,2},{2,3},{3,0},{4,5},{5,6},{6,7},{7,4},{8,9},{9,10},{10,1... | collective-permute-start | bytes 786440 | tf_op jit(solution)/shard_map/ppermute | solution.py:499
  155.1 20.9 %collective-permute-start.16 = (bf16[64,2048]{1,0:T(8,128)(2,1)S(1)}, bf16[64,2048]{1,0:T(8,128)(2,1)S(1)}, u32[]{:S(2)}, u32[]{:S(2)}) collective-permute-start(bf16[64,2048]{1,0:T(8,128)(2,1)S(1)} %shard_map.99), channel_id=1, source_target_pairs={{0,3},{1,0},{2,1},{3,2},{4,7},{5,4},{6,5},{7,6},{8,11},{9,8},{10,9... | collective-permute-start | bytes 786440 | tf_op jit(solution)/shard_map/ppermute | solution.py:499
  178.8 5.3 %collective-permute-start.17 = (f32[4,1024]{1,0:T(4,128)S(1)}, f32[4,1024]{1,0:T(4,128)S(1)}, u32[]{:S(2)}, u32[]{:S(2)}) collective-permute-start(f32[4,1024]{1,0:T(4,128)S(1)} %get-tuple-element.39), channel_id=1, source_target_pairs={{0,8},{1,9},{2,10},{3,11},{4,12},{5,13},{6,14},{7,15},{8,0},{9,1},... | collective-permute-start | bytes 49160 | tf_op jit(solution)/shard_map/ppermute | solution.py:499
  199.1 9.6 %collective-permute-start.21 = (bf16[64,2048]{1,0:T(8,128)(2,1)S(1)}, bf16[64,2048]{1,0:T(8,128)(2,1)S(1)}, u32[]{:S(2)}, u32[]{:S(2)}) collective-permute-start(bf16[64,2048]{1,0:T(8,128)(2,1)S(1)} %get-tuple-element.51), channel_id=1, source_target_pairs={{0,3},{1,0},{2,1},{3,2},{4,7},{5,4},{6,5},{7,6},{8,11},{9,8},{10,9... | collective-permute-start | bytes 786440 | tf_op jit(solution)/shard_map/ppermute | solution.py:499
  201.2 8.8 %collective-permute-start.18 = (bf16[64,2048]{1,0:T(8,128)(2,1)S(1)}, bf16[64,2048]{1,0:T(8,128)(2,1)S(1)}, u32[]{:S(2)}, u32[]{:S(2)}) collective-permute-start(bf16[64,2048]{1,0:T(8,128)(2,1)S(1)} %get-tuple-element.48), channel_id=1, source_target_pairs={{0,1},{1,2},{2,3},{3,0},{4,5},{5,6},{6,7},{7,4},{8,9},{9,10},{10,1... | collective-permute-start | bytes 786440 | tf_op jit(solution)/shard_map/ppermute | solution.py:499
  205.4 13.7 %collective-permute-start.23 = (bf16[128,2048]{1,0:T(8,128)(2,1)S(1)}, bf16[128,2048]{1,0:T(8,128)(2,1)S(1)}, u32[]{:S(2)}, u32[]{:S(2)}) collective-permute-start(bf16[128,2048]{1,0:T(8,128)(2,1)S(1)} %get-tuple-element.52), channel_id=1, source_target_pairs={{0,3},{1,0},{2,1},{3,2},{4,7},{5,4},{6,5},{7,6},{8,11},{9,8},{10,9... | collective-permute-start | bytes 1572872 | tf_op jit(solution)/shard_map/ppermute | solution.py:499
  208.8 12.7 %collective-permute-start.22 = (bf16[128,2048]{1,0:T(8,128)(2,1)S(1)}, bf16[128,2048]{1,0:T(8,128)(2,1)S(1)}, u32[]{:S(2)}, u32[]{:S(2)}) collective-permute-start(bf16[128,2048]{1,0:T(8,128)(2,1)S(1)} %shard_map.110), channel_id=1, source_target_pairs={{0,4},{1,5},{2,6},{3,7},{4,0},{5,1},{6,2},{7,3},{8,12},{9,13},{10,... | collective-permute-start | bytes 1572872 | tf_op jit(solution)/shard_map/ppermute | solution.py:499
  210.1 16.1 %collective-permute-start.19 = (bf16[128,2048]{1,0:T(8,128)(2,1)S(1)}, bf16[128,2048]{1,0:T(8,128)(2,1)S(1)}, u32[]{:S(2)}, u32[]{:S(2)}) collective-permute-start(bf16[128,2048]{1,0:T(8,128)(2,1)S(1)} %shard_map.108), channel_id=1, source_target_pairs={{0,1},{1,2},{2,3},{3,0},{4,5},{5,6},{6,7},{7,4},{8,9},{9,10},{10,1... | collective-permute-start | bytes 1572872 | tf_op jit(solution)/shard_map/ppermute | solution.py:499
  214.4 20.6 %collective-permute-start.25 = (bf16[128,2048]{1,0:T(8,128)(2,1)S(1)}, bf16[128,2048]{1,0:T(8,128)(2,1)S(1)}, u32[]{:S(2)}, u32[]{:S(2)}) collective-permute-start(bf16[128,2048]{1,0:T(8,128)(2,1)S(1)} %get-tuple-element.53), channel_id=1, source_target_pairs={{0,1},{1,2},{2,3},{3,0},{4,5},{5,6},{6,7},{7,4},{8,9},{9,10},{10,1... | collective-permute-start | bytes 1572872 | tf_op jit(solution)/shard_map/ppermute | solution.py:499
  221.7 13.2 %collective-permute-start.24 = (bf16[128,2048]{1,0:T(8,128)(2,1)S(1)}, bf16[128,2048]{1,0:T(8,128)(2,1)S(1)}, u32[]{:S(2)}, u32[]{:S(2)}) collective-permute-start(bf16[128,2048]{1,0:T(8,128)(2,1)S(1)} %shard_map.111), channel_id=1, source_target_pairs={{0,3},{1,0},{2,1},{3,2},{4,7},{5,4},{6,5},{7,6},{8,11},{9,8},{10,9... | collective-permute-start | bytes 1572872 | tf_op jit(solution)/shard_map/ppermute | solution.py:499
  226.3 9.3 %collective-permute-start.20 = (bf16[128,2048]{1,0:T(8,128)(2,1)S(1)}, bf16[128,2048]{1,0:T(8,128)(2,1)S(1)}, u32[]{:S(2)}, u32[]{:S(2)}) collective-permute-start(bf16[128,2048]{1,0:T(8,128)(2,1)S(1)} %shard_map.109), channel_id=1, source_target_pairs={{0,4},{1,5},{2,6},{3,7},{4,0},{5,1},{6,2},{7,3},{8,12},{9,13},{10,... | collective-permute-start | bytes 1572872 | tf_op jit(solution)/shard_map/ppermute | solution.py:499

commit v5 on v4

--- a/solution.py
+++ b/solution.py
@@ -34,45 +34,46 @@
     return pairs
 
 
-def attention_kernel(first, last, turns, sub, part, lengths, q_ref, *refs):
+def attention_kernel(first, last, turns, sources, rows, sub, part, lengths, *refs):
     chunks = len(turns)
-    keys = refs[: 2 * chunks : 2]
-    values = refs[1 : 2 * chunks : 2]
-    rest = list(refs[2 * chunks :])
-    if not first:
-        top_in, sum_in = rest.pop(0), rest.pop(0)
-    if last:
-        out_ref = rest.pop(0)
-        top_ref, sum_ref = rest.pop(0), rest.pop(0)
-    else:
-        top_ref, sum_ref = rest.pop(0), rest.pop(0)
-    wide, held = rest.pop(0), rest.pop(0)
-    step = pl.program_id(0)
-    rows = top_ref.shape[0]
+    arrays, refs = refs[: 1 + 2 * chunks], list(refs[1 + 2 * chunks :])
+    carried = [] if first else [refs.pop(0), refs.pop(0)]
+    results = [refs.pop(0)] if last else [refs.pop(0), refs.pop(0)]
+    query_ref, key_ref, value_ref, wide, sems = refs
+    top_ref, sum_ref = carried if last else results
     depth = wide.shape[1]
+    tokens = query_ref.shape[1]
     scale = math.log2(math.e) / math.sqrt(HEAD_DIM)
 
-    @pl.when(step == 0)
-    def _():
-        for n in range(chunks):
-            wide[n, :, :HEAD_DIM] = values[n][...].reshape(depth, HEAD_DIM)
-            wide[n, :, HEAD_DIM:] = jnp.ones((depth, HEAD_DIM), wide.dtype)
-            held[n] = keys[n][...].reshape(depth, HEAD_DIM)
-
+    targets = [query_ref]
+    for n in range(chunks):
+        targets += [key_ref.at[n], value_ref.at[n]]
+    copies = []
+    for n, (array, which, target) in enumerate(zip(arrays, sources, targets)):
+        source = array if which is None else array.at[:, which]
+        copies.append(pltpu.make_async_copy(source, target, sems.at[n]))
+    for copy in copies:
+        copy.start()
+    for n in range(chunks):
+        wide[n, :, HEAD_DIM:] = jnp.ones((depth, HEAD_DIM), wide.dtype)
     if first:
         top_ref[...] = jnp.full_like(top_ref, LOW)
         sum_ref[...] = jnp.zeros_like(sum_ref)
-    else:
-        top_ref[...] = top_in[...]
-        sum_ref[...] = sum_in[...]
+    elif not last:
+        top_ref[...] = carried[0][...]
+        sum_ref[...] = carried[1][...]
+    for copy in copies:
+        copy.wait()
+    for n in range(chunks):
+        wide[n, :, :HEAD_DIM] = value_ref[n].reshape(depth, HEAD_DIM)
+
     length = lengths[lax.axis_index("c")]
     y_at, y_size = lax.axis_index("y"), lax.axis_size("y")
-    queries_real = length - y_at * depth > step * rows
 
     def piece(n, at, count, top, summed):
-        query = q_ref[pl.ds(at // 64, sub // 64)].reshape(sub, HEAD_DIM)
+        query = query_ref[pl.ds(at // tokens, sub // tokens)].reshape(sub, HEAD_DIM)
         for start in range(0, depth, part):
-            key = held[n, start : start + part]
+            key = key_ref[n, start // tokens : (start + part) // tokens].reshape(part, HEAD_DIM)
             scores = lax.dot_general(
                 query, key, (((1,), (1,)), ((), ())), preferred_element_type=jnp.float32
             )
@@ -92,103 +93,90 @@
             top, summed = new_top, added
         return top, summed
 
-    def before(at):
-        return (None, None) if first else (top_ref[pl.ds(at, sub), :1], sum_ref[pl.ds(at, sub), :])
-
-    def after(at, top, summed):
-        top_ref[pl.ds(at, sub), :] = jnp.broadcast_to(top, (sub, HEAD_DIM))
-        sum_ref[pl.ds(at, sub), :] = summed
-
-    def attend(n, count):
-        places = range(0, rows, sub)
-        running = [before(at) for at in places]
+    def finish(at, summed):
+        done = summed[:, :HEAD_DIM] / summed[:, HEAD_DIM:]
+        out = done.astype(results[0].dtype).reshape(sub // tokens, tokens, HEAD_DIM)
+        results[0][pl.ds(at // tokens, sub // tokens)] = out
+
+    def attend(index, n, count):
+        places = [
+            pl.multiple_of(index * rows + at, sub) for at in range(0, rows, sub)
+        ]
+        running = [
+            (None, None) if first else (top_ref[pl.ds(at, sub), :1], sum_ref[pl.ds(at, sub), :])
+            for at in places
+        ]
         done = [piece(n, at, count, *run) for at, run in zip(places, running)]
-        for at, run in zip(places, done):
-            after(at, *run)
-
-    def chunk(n, carry):
+        for at, (top, summed) in zip(places, done):
+            if last:
+                finish(at, summed)
+            else:
+                top_ref[pl.ds(at, sub), :] = jnp.broadcast_to(top, (sub, HEAD_DIM))
+                sum_ref[pl.ds(at, sub), :] = summed
+
+    blocks = depth // rows
+
+    def chunk(step, carry):
+        n, index = step // blocks, lax.rem(step, blocks)
         turn = turns[0] + n * (turns[-1] - turns[0])
         count = length - lax.rem(y_at + turn + y_size, y_size) * depth
+        queries_real = length - y_at * depth > index * rows
 
         @pl.when(jnp.logical_and(queries_real, count > 0))
         def _():
-            attend(n, count)
+            attend(index, 0 if chunks == 1 else n, count)
+
+        if last:
+
+            @pl.when(jnp.logical_and(queries_real, count <= 0))
+            def _():
+                for at in range(0, rows, sub):
+                    at = pl.multiple_of(index * rows + at, sub)
+                    finish(at, sum_ref[pl.ds(at, sub), :])
+
+            @pl.when(jnp.logical_not(queries_real))
+            def _():
+                where = pl.ds(index * (rows // tokens), rows // tokens)
+                results[0][where] = jnp.zeros((rows // tokens, tokens, HEAD_DIM), jnp.bfloat16)
 
         return carry
 
-    if chunks == 1:
-        chunk(0, 0)
+    lax.fori_loop(0, chunks * blocks, chunk, 0)
+
+
+def attend_chunks(lengths, qkv, pairs, turns, carry, last, rows=1024, sub=256, part=512):
+    blocks, _, tokens, _ = qkv.shape
+    total = blocks * tokens
+    first = carry is None
+    chunks = len(turns)
+    arrays = [qkv] + [array for array, _ in pairs]
+    sources = [0] + [which for _, which in pairs]
+    held = [] if first else list(carry)
+
+    def body(*refs):
+        attention_kernel(first, last, turns, sources, rows, sub, part, *refs)
+
+    if last:
+        out_shape = [jax.ShapeDtypeStruct((blocks, tokens, HEAD_DIM), jnp.bfloat16)]
     else:
-        lax.fori_loop(0, chunks, chunk, 0)
-
-    if last:
-
-        @pl.when(queries_real)
-        def _():
-            done = sum_ref[:, :HEAD_DIM] / sum_ref[:, HEAD_DIM:]
-            out_ref[...] = done.astype(out_ref.dtype).reshape(out_ref.shape)
-
-        @pl.when(jnp.logical_not(queries_real))
-        def _():
-            out_ref[...] = jnp.zeros_like(out_ref)
-
-
-def attend_chunks(lengths, qkv, pairs, turns, carry, last, block=1024, sub=256, part=512):
-    sources, tokens = qkv.shape[0], qkv.shape[2]
-    total = sources * tokens
-    first = carry is None
-    chunks = len(pairs) // 2
-
-    def whole(array, which):
-        if array.ndim == 4:
-            return pl.BlockSpec(
-                (sources, None, tokens, HEAD_DIM), lambda i, counts: (0, which, 0, 0)
-            )
-        return pl.BlockSpec((sources, tokens, HEAD_DIM), lambda i, counts: (0, 0, 0))
-
-    in_specs = [
-        pl.BlockSpec((block // tokens, None, tokens, HEAD_DIM), lambda i, counts: (i, 0, 0, 0))
-    ]
-    operands = [qkv]
-    for array, which in pairs:
-        in_specs.append(whole(array, which))
-        operands.append(array)
-    top_spec = pl.BlockSpec((block, HEAD_DIM), lambda i, counts: (i, 0))
-    sum_spec = pl.BlockSpec((block, 2 * HEAD_DIM), lambda i, counts: (i, 0))
-    if not first:
-        in_specs += [top_spec, sum_spec]
-        operands += list(carry)
-    scratch = [
-        pltpu.VMEM((chunks, total, 2 * HEAD_DIM), jnp.bfloat16),
-        pltpu.VMEM((chunks, total, HEAD_DIM), jnp.bfloat16),
-    ]
-    if last:
-        out_specs = pl.BlockSpec((block // tokens, tokens, HEAD_DIM), lambda i, counts: (i, 0, 0))
-        out_shape = jax.ShapeDtypeStruct((sources, tokens, HEAD_DIM), jnp.bfloat16)
-        scratch = [
-            pltpu.VMEM((block, HEAD_DIM), jnp.float32),
-            pltpu.VMEM((block, 2 * HEAD_DIM), jnp.float32),
-        ] + scratch
-    else:
-        out_specs = [top_spec, sum_spec]
         out_shape = [
             jax.ShapeDtypeStruct((total, HEAD_DIM), jnp.float32),
             jax.ShapeDtypeStruct((total, 2 * HEAD_DIM), jnp.float32),
         ]
-
-    def body(*refs):
-        attention_kernel(first, last, turns, sub, part, *refs)
-
     return pl.pallas_call(
         body,
-        grid_spec=pltpu.PrefetchScalarGridSpec(
-            num_scalar_prefetch=1,
-            grid=(total // block,),
-            in_specs=in_specs,
-            out_specs=out_specs,
-            scratch_shapes=scratch,
-        ),
+        in_specs=[pl.BlockSpec(memory_space=pltpu.SMEM)]
+        + [pl.BlockSpec(memory_space=pl.ANY)] * len(arrays)
+        + [pl.BlockSpec(memory_space=pltpu.VMEM)] * len(held),
+        out_specs=[pl.BlockSpec(memory_space=pltpu.VMEM)] * len(out_shape),
         out_shape=out_shape,
+        scratch_shapes=[
+            pltpu.VMEM((blocks, tokens, HEAD_DIM), jnp.bfloat16),
+            pltpu.VMEM((chunks, blocks, tokens, HEAD_DIM), jnp.bfloat16),
+            pltpu.VMEM((chunks, blocks, tokens, HEAD_DIM), jnp.bfloat16),
+            pltpu.VMEM((chunks, total, 2 * HEAD_DIM), jnp.bfloat16),
+            pltpu.SemaphoreType.DMA((len(arrays),)),
+        ],
         cost_estimate=pl.CostEstimate(
             flops=8 * total * total * HEAD_DIM * chunks,
             bytes_accessed=4 << 20,
@@ -196,7 +184,7 @@
         ),
         compiler_params=pltpu.CompilerParams(vmem_limit_bytes=24 << 20),
         name="attend_last" if last else ("attend_first" if first else "attend_next"),
-    )(lengths, *operands)
+    )(lengths, *arrays, *held)
 
 
 def logits_kernel(blocks, places, cols, lengths, weights_ref, bias_ref, *refs):
@@ -519,13 +507,13 @@
     carry = attend_chunks(
         doc_lengths,
         qkv,
-        [(key_left, 0), (value_left, 0), (key_right, 0), (value_right, 0)],
+        [(key_left, None), (value_left, None), (key_right, None), (value_right, None)],
         [-1, 1],
         carry,
         False,
     )
-    attended = attend_chunks(
-        doc_lengths, qkv, [(key_far, 0), (value_far, 0)], [2], carry, True
+    (attended,) = attend_chunks(
+        doc_lengths, qkv, [(key_far, None), (value_far, None)], [2], carry, True
     )
     back = lax.all_to_all(attended, PLANE, split_axis=0, concat_axis=0, tiled=True)
     inward = jnp.transpose(residual, (1, 0, 2))

time: 238 us -> 237 us (level)
  transfers between devices with their start and end apart: 28 -> 28, of which waited for: 16 -> 16; matrix products, arithmetic and copies ran while one was open for 1% -> 1% of each run, Pallas kernels for 28% -> 27%
where the time goes in v5:
time: 237 us
  waiting for transfers between devices  94.5 us (40%)
  Pallas kernels  72.7 us (31%)
  starting transfers between devices  49.5 us (21%)
  blocking collectives  10.4 us (4%)
  local copies, waits for them, and re-layouts  7.4 us (3%)
    ppermute x26, waiting for transfers between devices, move(): return lax.ppermute(array, AXES, shift_perm(sizes, **by))  65.9 us
    ppermute x26, starting transfers between devices, move(): return lax.ppermute(array, AXES, shift_perm(sizes, **by))  35.4 us
    pallas_call x3, Pallas kernels, attend_chunks(): pl.pallas_call(body, in_specs=[pl.BlockSpec(memory_space=pltpu.SMEM)] + [...  34.7 us
    pallas_call x18, Pallas kernels, simple_call(): pl.pallas_call(body, in_specs=in_specs, out_specs=jax.tree.map(lambda _:...  34.1 us
    all_to_all x1, waiting for transfers between devices, local(): lax.all_to_all(stacked, PLANE, split_axis=0, concat_axis=0, tiled=True)  16.8 us
    all_to_all x1, waiting for transfers between devices, local(): lax.all_to_all(attended, PLANE, split_axis=0, concat_axis=0, tiled=True)  11.8 us
    all_to_all x1, blocking collectives, local(): lax.all_to_all(spread, ('y', 'c'), split_axis=0, concat_axis=0, tiled=True)  10.4 us
    all_to_all x1, starting transfers between devices, local(): lax.all_to_all(stacked, PLANE, split_axis=0, concat_axis=0, tiled=True)  8.28 us
  transfers between devices with their start and end apart: 28, of which 16 were waited for; matrix products, arithmetic and copies ran while one was open for 1% of the time, Pallas kernels for 27%

profile of v5, /device:TPU:0, one launch (start us, length us, event | category | flops | bytes accessed | tf_op | source)
XLA Modules:
  0.0 236.8 jit_solution(5582357652277937004)
XLA Ops:
  0.6 1.5 reshape.23
  2.1 0.2 copy.20
  2.3 0.3 reshape.24
  2.7 0.2 copy.21
  2.9 0.3 reshape.25
  3.2 0.2 copy.22
  3.5 1.4 pad_maximum_fusion
  4.8 8.3 %all-to-all-start = ((bf16[32,3,64,128]{3,2,1,0:T(8,128)(2,1)}), bf16[32,3,64,128]{3,2,1,0:T(8,128)(2,1)S(1)}, u32[]{:S(2)}, u32[]{:S(2)}) async-start(bf16[32,3,64,128]{3,2,1,0:T(8,128)(2,1)} %pad_maximum_fusion), calls=%async_computation | async-start | bytes 3145728 | tf_op jit(solution)/shard_map/all_to_all | solution.py:490
  13.1 3.1 %constant_dynamic-slice_fusion = bf16[2048,512]{1,0:T(8,128)(2,1)} fusion(bf16[2048,1024]{1,0:T(8,128)(2,1)} %own_hbm.1, s32[]{:T(128)S(6)} %select_n.3), kind=kLoop, calls=%fused_computation.5 | loop fusion | bytes 4194308 | tf_op jit(solution)/shard_map/dynamic_slice | solution.py:501
  16.2 3.3 %collective-permute-start = (bf16[2048,512]{1,0:T(8,128)(2,1)}, bf16[2048,512]{1,0:T(8,128)(2,1)}, u32[]{:S(2)}, u32[]{:S(2)}) collective-permute-start(bf16[2048,512]{1,0:T(8,128)(2,1)} %constant_dynamic-slice_fusion), channel_id=1, source_target_pairs={{0,8},{1,9},{2,10},{3,11},{4,12},{5,13},{6,14},{7,15},{8,0},{9,1},... | collective-permute-start | bytes 6291464 | tf_op jit(solution)/shard_map/ppermute | solution.py:487
  19.5 16.8 %all-to-all-done.refs_1_.refs_2_.refs_3_ = bf16[32,3,64,128]{3,2,1,0:T(8,128)(2,1)S(1)} async-done(((bf16[32,3,64,128]{3,2,1,0:T(8,128)(2,1)}), bf16[32,3,64,128]{3,2,1,0:T(8,128)(2,1)S(1)}, u32[]{:S(2)}, u32[]{:S(2)}) %all-to-all-start) | async-done | bytes 1572896 | tf_op jit(solution)/shard_map/all_to_all | solution.py:490
  36.4 1.6 collective-permute-start.3
  38.0 1.7 collective-permute-start.5
  39.7 0.4 collective-permute-start.7
  40.1 2.9 %collective-permute-start.8 = (bf16[32,64,128]{2,1,0:T(8,128)(2,1)S(1)}, bf16[32,64,128]{2,1,0:T(8,128)(2,1)S(1)}, u32[]{:S(2)}, u32[]{:S(2)}) collective-permute-start(bf16[32,64,128]{2,1,0:T(8,128)(2,1)S(1)} %get-tuple-element.55), channel_id=1, source_target_pairs={{0,96},{1,97},{2,98},{3,99},{4,100},{5,101},{6,102},{7,103},{8,104... | collective-permute-start | bytes 1572872 | tf_op jit(solution)/shard_map/ppermute | solution.py:487
  42.9 6.5 %attend_first.1 = (f32[2048,128]{1,0:T(8,128)S(1)}, f32[2048,256]{1,0:T(8,128)S(1)}) custom-call(s32[2]{0:T(128)S(1)} %copy-done.2, bf16[32,3,64,128]{3,2,1,0:T(8,128)(2,1)S(1)} %all-to-all-done.refs_1_.refs_2_.refs_3_, bf16[32,3,64,128]{3,2,1,0:T(8,128)(2,1)S(1)} %all-to-all-done.refs_1_.refs_2_.refs_3_, ...), custom_call_target="tpu_custom_call" | custom-call | flops 4294967296 | bytes 4194304 | tf_op jit(solution)/shard_map/attend_first/pallas_call | solution.py:166
  49.5 3.0 %collective-permute-done.3.refs_2_ = bf16[32,64,128]{2,1,0:T(8,128)(2,1)S(1)} collective-permute-done((bf16[32,64,128]{2,1,0:T(8,128)(2,1)S(1)}, bf16[32,64,128]{2,1,0:T(8,128)(2,1)S(1)}, u32[]{:S(2)}, u32[]{:S(2)}) %collective-permute-start.3) | collective-permute-done | bytes 524320 | tf_op jit(solution)/shard_map/ppermute | solution.py:487
  52.5 0.4 collective-permute-start.4
  52.8 2.9 %collective-permute-start.6 = (bf16[32,64,128]{2,1,0:T(8,128)(2,1)S(1)}, bf16[32,64,128]{2,1,0:T(8,128)(2,1)S(1)}, u32[]{:S(2)}, u32[]{:S(2)}) collective-permute-start(bf16[32,64,128]{2,1,0:T(8,128)(2,1)S(1)} %collective-permute-done.5.refs_5_), channel_id=1, source_target_pairs={{0,96},{1,97},{2,98},{3,99},{4,100},{5,101},{6,102},{7,103},{8,104... | collective-permute-start | bytes 1572872 | tf_op jit(solution)/shard_map/ppermute | solution.py:487
  55.7 23.7 %collective-permute-done.near_hbm = bf16[2048,512]{1,0:T(8,128)(2,1)} collective-permute-done((bf16[2048,512]{1,0:T(8,128)(2,1)}, bf16[2048,512]{1,0:T(8,128)(2,1)}, u32[]{:S(2)}, u32[]{:S(2)}) %collective-permute-start) | collective-permute-done | bytes 2097184 | tf_op jit(solution)/shard_map/ppermute | solution.py:487
  79.5 18.1 %attend_next.1 = (f32[2048,128]{1,0:T(8,128)S(1)}, f32[2048,256]{1,0:T(8,128)S(1)}) custom-call(s32[2]{0:T(128)S(1)} %copy-done.2, bf16[32,3,64,128]{3,2,1,0:T(8,128)(2,1)S(1)} %all-to-all-done.refs_1_.refs_2_.refs_3_, bf16[32,64,128]{2,1,0:T(8,128)(2,1)S(1)} %collective-permute-done.3.refs_2_, bf16[32,64,128]{2,1,0:T(8,128)(2,1)S(1)} %collective-permute-done.7.refs_3_, ...), custom_call_target="tpu_custom_call" | custom-call | flops 8589934592 | bytes 4194304 | tf_op jit(solution)/shard_map/attend_next/pallas_call | solution.py:166
  97.6 10.1 %attend_last.1 = bf16[32,64,128]{2,1,0:T(8,128)(2,1)} custom-call(s32[2]{0:T(128)S(1)} %copy-done.2, bf16[32,3,64,128]{3,2,1,0:T(8,128)(2,1)S(1)} %all-to-all-done.refs_1_.refs_2_.refs_3_, bf16[32,64,128]{2,1,0:T(8,128)(2,1)S(1)} %collective-permute-done.4.refs_2_, bf16[32,64,128]{2,1,0:T(8,128)(2,1)S(1)} %collective-permute-done.6.refs_3_, ...), custom_call_target="tpu_custom_call" | custom-call | flops 4294967296 | bytes 4194304 | tf_op jit(solution)/shard_map/attend_last/pallas_call | solution.py:166
  107.7 5.8 %all-to-all-start.1 = ((bf16[32,64,128]{2,1,0:T(8,128)(2,1)}), bf16[32,64,128]{2,1,0:T(8,128)(2,1)S(1)}, u32[]{:S(2)}, u32[]{:S(2)}) async-start(bf16[32,64,128]{2,1,0:T(8,128)(2,1)} %attend_last.1), calls=%async_computation.1 | async-start | bytes 1048576 | tf_op jit(solution)/shard_map/all_to_all | solution.py:518
  113.6 11.8 %all-to-all-done.1.refs_0_ = bf16[32,64,128]{2,1,0:T(8,128)(2,1)S(1)} async-done(((bf16[32,64,128]{2,1,0:T(8,128)(2,1)}), bf16[32,64,128]{2,1,0:T(8,128)(2,1)S(1)}, u32[]{:S(2)}, u32[]{:S(2)}) %all-to-all-start.1) | async-done | bytes 524320 | tf_op jit(solution)/shard_map/all_to_all | solution.py:518
  125.4 0.4 normalized.1.refs_3_
  125.9 0.3 collective-permute-start.10
  126.2 0.6 collective-permute-start.9
  126.8 13.4 %collective-permute-done.10.refs_4_ = bf16[128,2048]{1,0:T(8,128)(2,1)S(1)} collective-permute-done((bf16[128,2048]{1,0:T(8,128)(2,1)S(1)}, bf16[128,2048]{1,0:T(8,128)(2,1)S(1)}, u32[]{:S(2)}, u32[]{:S(2)}) %collective-permute-start.10) | collective-permute-done | bytes 524320 | tf_op jit(solution)/shard_map/ppermute | solution.py:487
  140.2 1.0 collective-permute-start.12
  141.2 1.2 collective-permute-start.14
  142.4 0.8 collective-permute-start.13
  143.3 2.4 collective-permute-start.2
  145.6 6.8 %collective-permute-done.12.refs_3_.in_ref = bf16[128,2048]{1,0:T(8,128)(2,1)S(1)} collective-permute-done((bf16[128,2048]{1,0:T(8,128)(2,1)S(1)}, bf16[128,2048]{1,0:T(8,128)(2,1)S(1)}, u32[]{:S(2)}, u32[]{:S(2)}) %collective-permute-start.12) | collective-permute-done | bytes 524320 | tf_op jit(solution)/shard_map/ppermute | solution.py:487
  152.4 0.8 collective-permute-start.11
  153.2 1.1 collective-permute-done.14.refs_5_.in_ref
  154.6 0.2 collective-permute-done.2.other_bias_ref
  154.8 2.9 %collective-permute-start.16 = (bf16[64,2048]{1,0:T(8,128)(2,1)S(1)}, bf16[64,2048]{1,0:T(8,128)(2,1)S(1)}, u32[]{:S(2)}, u32[]{:S(2)}) collective-permute-start(bf16[64,2048]{1,0:T(8,128)(2,1)S(1)} %shard_map.99), channel_id=1, source_target_pairs={{0,3},{1,0},{2,1},{3,2},{4,7},{5,4},{6,5},{7,6},{8,11},{9,8},{10,9... | collective-permute-start | bytes 786440 | tf_op jit(solution)/shard_map/ppermute | solution.py:487
  157.7 3.5 %side_by_side.1 = (bf16[2048,2048]{1,0:T(8,128)(2,1)S(1)}, f32[1,2048]{1,0:T(1,128)S(1)}) custom-call(bf16[2048,1024]{1,0:T(8,128)(2,1)} %own_hbm.1, bf16[2048,512]{1,0:T(8,128)(2,1)} %collective-permute-done.near_hbm, bf16[2048,512]{1,0:T(8,128)(2,1)} %collective-permute-done.1.far_hbm, f32[1,1024]{1,0:T(1,128)S(1)} %bitcast.30, ...), custom_call_target="tpu_custom_call" | custom-call | bytes 16777216 | tf_op jit(solution)/shard_map/side_by_side/pallas_call | solution.py:254
  161.2 5.7 %shard_map.97 = (f32[384,2048]{1,0:T(8,128)S(1)}, f32[2,2048]{1,0:T(2,128)S(1)}) custom-call(s32[2]{0:T(128)S(1)} %copy-done.2, bf16[2048,2048]{1,0:T(8,128)(2,1)S(1)} %get-tuple-element.28.refs_1_.refs_2_, f32[1,2048]{1,0:T(1,128)S(1)} %get-tuple-element.29.refs_2_, bf16[128,2048]{1,0:T(8,128)(2,1)S(1)} %collective-permute-done.12.refs_3_.in_ref, ...), custom_call_target="tpu_custom_call" | custom-call | flops 6442450944 | bytes 19939344 | tf_op jit(solution)/shard_map/pallas_call | solution.py:277
  166.9 0.3 collective-permute-done.11.refs_5_
  167.2 5.7 %shard_map.96 = (f32[384,2048]{1,0:T(8,128)S(1)}, f32[2,2048]{1,0:T(2,128)S(1)}) custom-call(s32[2]{0:T(128)S(1)} %copy-done.2, bf16[2048,2048]{1,0:T(8,128)(2,1)S(1)} %get-tuple-element.28.refs_1_.refs_2_, f32[1,2048]{1,0:T(1,128)S(1)} %get-tuple-element.29.refs_2_, bf16[128,2048]{1,0:T(8,128)(2,1)S(1)} %collective-permute-done.9.refs_3_, ...), custom_call_target="tpu_custom_call" | custom-call | flops 6442450944 | bytes 19939344 | tf_op jit(solution)/shard_map/pallas_call | solution.py:277
  172.9 2.8 %shard_map.95 = (f32[128,2048]{1,0:T(8,128)S(1)}, f32[2,2048]{1,0:T(2,128)S(1)}) custom-call(s32[2]{0:T(128)S(1)} %copy-done.2, bf16[2048,2048]{1,0:T(8,128)(2,1)S(1)} %get-tuple-element.28.refs_1_.refs_2_, f32[1,2048]{1,0:T(1,128)S(1)} %get-tuple-element.29.refs_2_, bf16[128,2048]{1,0:T(8,128)(2,1)S(1)} %normalized.1.refs_3_), custom_call_target="tpu_custom_call" | custom-call | flops 4294967296 | bytes 17842192 | tf_op jit(solution)/shard_map/pallas_call | solution.py:277
  175.7 2.8 %shard_map.100 = (f32[128,2048]{1,0:T(8,128)S(1)}, f32[2,2048]{1,0:T(2,128)S(1)}) custom-call(s32[2]{0:T(128)S(1)} %copy-done.2, bf16[2048,2048]{1,0:T(8,128)(2,1)S(1)} %get-tuple-element.28.refs_1_.refs_2_, f32[1,2048]{1,0:T(1,128)S(1)} %get-tuple-element.29.refs_2_, bf16[64,2048]{1,0:T(8,128)(2,1)S(1)} %collective-permute-done.15.refs_3_, ...), custom_call_target="tpu_custom_call" | custom-call | flops 4294967296 | bytes 17842192 | tf_op jit(solution)/shard_map/pallas_call | solution.py:277
  178.6 2.7 %collective-permute-start.17 = (f32[4,1024]{1,0:T(4,128)S(1)}, f32[4,1024]{1,0:T(4,128)S(1)}, u32[]{:S(2)}, u32[]{:S(2)}) collective-permute-start(f32[4,1024]{1,0:T(4,128)S(1)} %get-tuple-element.39), channel_id=1, source_target_pairs={{0,8},{1,9},{2,10},{3,11},{4,12},{5,13},{6,14},{7,15},{8,0},{9,1},... | collective-permute-start | bytes 49160 | tf_op jit(solution)/shard_map/ppermute | solution.py:487
  181.3 2.6 %collective-permute-done.17.two_ref = f32[4,1024]{1,0:T(4,128)S(1)} collective-permute-done((f32[4,1024]{1,0:T(4,128)S(1)}, f32[4,1024]{1,0:T(4,128)S(1)}, u32[]{:S(2)}, u32[]{:S(2)}) %collective-permute-start.17) | collective-permute-done | bytes 16416 | tf_op jit(solution)/shard_map/ppermute | solution.py:487
  183.9 10.4 %all_to_all.15.gathered_ref = f32[8,4,1024]{2,1,0:T(4,128)S(1)} all-to-all(f32[8,4,1024]{2,1,0:T(4,128)S(1)} %shard_map.102), channel_id=1, replica_groups=mesh['y'=4,'c'=2,'u'=2,'w'=2,'z'=4] {'y','c'}, dimensions={0} | all-to-all | bytes 262144 | tf_op jit(solution)/shard_map/all_to_all | solution.py:543
  194.3 1.2 shard_map.103
  195.4 3.4 %shard_map.107 = (bf16[64,2048]{1,0:T(8,128)(2,1)S(1)}, bf16[64,2048]{1,0:T(8,128)(2,1)S(1)}) custom-call(f32[128,2048]{1,0:T(8,128)S(1)} %get-tuple-element.47.refs_0_, f32[2,2048]{1,0:T(2,128)S(1)} %get-tuple-element.42.refs_1_, bf16[2048,2048]{1,0:T(8,128)(2,1)S(1)} %get-tuple-element.28.refs_1_.refs_2_), custom_call_target="tpu_custom_call" | custom-call | flops 4294967296 | bytes 18907136 | tf_op jit(solution)/shard_map/pallas_call | solution.py:277
  198.8 2.1 collective-permute-start.21
  200.9 4.2 %shard_map.106 = (bf16[128,2048]{1,0:T(8,128)(2,1)S(1)}, bf16[128,2048]{1,0:T(8,128)(2,1)S(1)}, bf16[128,2048]{1,0:T(8,128)(2,1)S(1)}) custom-call(f32[384,2048]{1,0:T(8,128)S(1)} %get-tuple-element.45.refs_0_, f32[2,2048]{1,0:T(2,128)S(1)} %get-tuple-element.42.refs_1_, bf16[2048,2048]{1,0:T(8,128)(2,1)S(1)} %get-tuple-element.28.refs_1_.refs_2_), custom_call_target="tpu_custom_call" | custom-call | flops 6442450944 | bytes 23101440 | tf_op jit(solution)/shard_map/pallas_call | solution.py:277
  205.1 3.3 %collective-permute-start.23 = (bf16[128,2048]{1,0:T(8,128)(2,1)S(1)}, bf16[128,2048]{1,0:T(8,128)(2,1)S(1)}, u32[]{:S(2)}, u32[]{:S(2)}) collective-permute-start(bf16[128,2048]{1,0:T(8,128)(2,1)S(1)} %get-tuple-element.52), channel_id=1, source_target_pairs={{0,3},{1,0},{2,1},{3,2},{4,7},{5,4},{6,5},{7,6},{8,11},{9,8},{10,9... | collective-permute-start | bytes 1572872 | tf_op jit(solution)/shard_map/ppermute | solution.py:487
  208.5 1.1 collective-permute-start.22
  209.9 4.2 %shard_map.105 = (bf16[128,2048]{1,0:T(8,128)(2,1)S(1)}, bf16[128,2048]{1,0:T(8,128)(2,1)S(1)}, bf16[128,2048]{1,0:T(8,128)(2,1)S(1)}) custom-call(f32[384,2048]{1,0:T(8,128)S(1)} %get-tuple-element.43.refs_0_, f32[2,2048]{1,0:T(2,128)S(1)} %get-tuple-element.42.refs_1_, bf16[2048,2048]{1,0:T(8,128)(2,1)S(1)} %get-tuple-element.28.refs_1_.refs_2_), custom_call_target="tpu_custom_call" | custom-call | flops 6442450944 | bytes 23101440 | tf_op jit(solution)/shard_map/pallas_call | solution.py:277
  214.2 4.7 %collective-permute-done.23.refs_1_ = bf16[128,2048]{1,0:T(8,128)(2,1)S(1)} collective-permute-done((bf16[128,2048]{1,0:T(8,128)(2,1)S(1)}, bf16[128,2048]{1,0:T(8,128)(2,1)S(1)}, u32[]{:S(2)}, u32[]{:S(2)}) %collective-permute-start.23) | collective-permute-done | bytes 524320 | tf_op jit(solution)/shard_map/ppermute | solution.py:487
  218.9 2.4 collective-permute-done.22.refs_0_
  221.2 0.2 shard_map.111
  221.4 1.6 collective-permute-start.24
  223.0 2.8 %collective-permute-done.19.refs_0_ = bf16[128,2048]{1,0:T(8,128)(2,1)S(1)} collective-permute-done((bf16[128,2048]{1,0:T(8,128)(2,1)S(1)}, bf16[128,2048]{1,0:T(8,128)(2,1)S(1)}, u32[]{:S(2)}, u32[]{:S(2)}) %collective-permute-start.19) | collective-permute-done | bytes 524320 | tf_op jit(solution)/shard_map/ppermute | solution.py:487
  226.0 1.1 collective-permute-start.20
  227.1 3.4 %shard_map.104.base_ref = bf16[128,2048]{1,0:T(8,128)(2,1)S(1)} custom-call(f32[128,2048]{1,0:T(8,128)S(1)} %get-tuple-element.41.refs_0_, f32[2,2048]{1,0:T(2,128)S(1)} %get-tuple-element.42.refs_1_, bf16[2048,2048]{1,0:T(8,128)(2,1)S(1)} %get-tuple-element.28.refs_1_.refs_2_), custom_call_target="tpu_custom_call" | custom-call | flops 4294967296 | bytes 18907136 | tf_op jit(solution)/shard_map/pallas_call | solution.py:277
  230.5 4.1 %collective-permute-done.25.refs_2_ = bf16[128,2048]{1,0:T(8,128)(2,1)S(1)} collective-permute-done((bf16[128,2048]{1,0:T(8,128)(2,1)S(1)}, bf16[128,2048]{1,0:T(8,128)(2,1)S(1)}, u32[]{:S(2)}, u32[]{:S(2)}) %collective-permute-start.25) | collective-permute-done | bytes 524320 | tf_op jit(solution)/shard_map/ppermute | solution.py:487
  234.6 0.6 collective-permute-done.20.refs_0_
  235.2 0.3 shard_map.112
  235.5 1.3 copy.31
  (39 shorter events, 1.0 us)
Async XLA Ops:
  0.6 1.7 copy-start.3
  0.6 2.3 copy-start.4
  4.8 31.5 %all-to-all-start = ((bf16[32,3,64,128]{3,2,1,0:T(8,128)(2,1)}), bf16[32,3,64,128]{3,2,1,0:T(8,128)(2,1)S(1)}, u32[]{:S(2)}, u32[]{:S(2)}) async-start(bf16[32,3,64,128]{3,2,1,0:T(8,128)(2,1)} %pad_maximum_fusion), calls=%async_computation | async-start | bytes 3145728 | tf_op jit(solution)/shard_map/all_to_all | solution.py:490
  16.2 26.8 %copy-start.2 = (s32[2]{0:T(128)S(1)}, s32[2]{0:T(128)}, u32[]{:S(2)}) copy-start(s32[2]{0:T(128)} %lengths_ref.1) | copy-start | bytes 28
  16.2 63.3 %collective-permute-start = (bf16[2048,512]{1,0:T(8,128)(2,1)}, bf16[2048,512]{1,0:T(8,128)(2,1)}, u32[]{:S(2)}, u32[]{:S(2)}) collective-permute-start(bf16[2048,512]{1,0:T(8,128)(2,1)} %constant_dynamic-slice_fusion), channel_id=1, source_target_pairs={{0,8},{1,9},{2,10},{3,11},{4,12},{5,13},{6,14},{7,15},{8,0},{9,1},... | collective-permute-start | bytes 6291464 | tf_op jit(solution)/shard_map/ppermute | solution.py:487
  36.4 16.1 %collective-permute-start.3 = (bf16[32,64,128]{2,1,0:T(8,128)(2,1)S(1)}, bf16[32,64,128]{2,1,0:T(8,128)(2,1)S(1)}, u32[]{:S(2)}, u32[]{:S(2)}) collective-permute-start(bf16[32,64,128]{2,1,0:T(8,128)(2,1)S(1)} %get-tuple-element.55), channel_id=1, source_target_pairs={{0,32},{1,33},{2,34},{3,35},{4,36},{5,37},{6,38},{7,39},{8,40},{9,... | collective-permute-start | bytes 1572872 | tf_op jit(solution)/shard_map/ppermute | solution.py:487
  38.0 14.8 %collective-permute-start.5 = (bf16[32,64,128]{2,1,0:T(8,128)(2,1)S(1)}, bf16[32,64,128]{2,1,0:T(8,128)(2,1)S(1)}, u32[]{:S(2)}, u32[]{:S(2)}) collective-permute-start(bf16[32,64,128]{2,1,0:T(8,128)(2,1)S(1)} %get-tuple-element.54), channel_id=1, source_target_pairs={{0,96},{1,97},{2,98},{3,99},{4,100},{5,101},{6,102},{7,103},{8,104... | collective-permute-start | bytes 1572872 | tf_op jit(solution)/shard_map/ppermute | solution.py:487
  39.7 39.8 %collective-permute-start.7 = (bf16[32,64,128]{2,1,0:T(8,128)(2,1)S(1)}, bf16[32,64,128]{2,1,0:T(8,128)(2,1)S(1)}, u32[]{:S(2)}, u32[]{:S(2)}) collective-permute-start(bf16[32,64,128]{2,1,0:T(8,128)(2,1)S(1)} %get-tuple-element.54), channel_id=1, source_target_pairs={{0,32},{1,33},{2,34},{3,35},{4,36},{5,37},{6,38},{7,39},{8,40},{9,... | collective-permute-start | bytes 1572872 | tf_op jit(solution)/shard_map/ppermute | solution.py:487
  40.1 39.4 %collective-permute-start.8 = (bf16[32,64,128]{2,1,0:T(8,128)(2,1)S(1)}, bf16[32,64,128]{2,1,0:T(8,128)(2,1)S(1)}, u32[]{:S(2)}, u32[]{:S(2)}) collective-permute-start(bf16[32,64,128]{2,1,0:T(8,128)(2,1)S(1)} %get-tuple-element.55), channel_id=1, source_target_pairs={{0,96},{1,97},{2,98},{3,99},{4,100},{5,101},{6,102},{7,103},{8,104... | collective-permute-start | bytes 1572872 | tf_op jit(solution)/shard_map/ppermute | solution.py:487
  52.5 45.1 %collective-permute-start.4 = (bf16[32,64,128]{2,1,0:T(8,128)(2,1)S(1)}, bf16[32,64,128]{2,1,0:T(8,128)(2,1)S(1)}, u32[]{:S(2)}, u32[]{:S(2)}) collective-permute-start(bf16[32,64,128]{2,1,0:T(8,128)(2,1)S(1)} %collective-permute-done.3.refs_2_), channel_id=1, source_target_pairs={{0,32},{1,33},{2,34},{3,35},{4,36},{5,37},{6,38},{7,39},{8,40},{9,... | collective-permute-start | bytes 1572872 | tf_op jit(solution)/shard_map/ppermute | solution.py:487
  52.8 44.7 %collective-permute-start.6 = (bf16[32,64,128]{2,1,0:T(8,128)(2,1)S(1)}, bf16[32,64,128]{2,1,0:T(8,128)(2,1)S(1)}, u32[]{:S(2)}, u32[]{:S(2)}) collective-permute-start(bf16[32,64,128]{2,1,0:T(8,128)(2,1)S(1)} %collective-permute-done.5.refs_5_), channel_id=1, source_target_pairs={{0,96},{1,97},{2,98},{3,99},{4,100},{5,101},{6,102},{7,103},{8,104... | collective-permute-start | bytes 1572872 | tf_op jit(solution)/shard_map/ppermute | solution.py:487
  79.5 78.2 %collective-permute-start.1 = (bf16[2048,512]{1,0:T(8,128)(2,1)}, bf16[2048,512]{1,0:T(8,128)(2,1)}, u32[]{:S(2)}, u32[]{:S(2)}) collective-permute-start(bf16[2048,512]{1,0:T(8,128)(2,1)} %collective-permute-done.near_hbm), channel_id=1, source_target_pairs={{0,16},{1,17},{2,18},{3,19},{4,20},{5,21},{6,22},{7,23},{8,24},{9,... | collective-permute-start | bytes 6291464 | tf_op jit(solution)/shard_map/ppermute | solution.py:487
  97.6 15.9 %copy-start.5 = (bf16[64,2,2048]{2,1,0:T(2,128)(2,1)S(1)}, bf16[64,2,2048]{2,1,0:T(2,128)(2,1)}, u32[]{:S(2)}) copy-start(bf16[64,2,2048]{2,1,0:T(2,128)(2,1)} %param.11) | copy-start | bytes 1572868
  107.7 17.8 %copy-start = (f32[2048]{0:T(1024)S(1)}, f32[2048]{0:T(1024)}, u32[]{:S(2)}) copy-start(f32[2048]{0:T(1024)} %param.12) | copy-start | bytes 24580
  107.7 35.6 %copy-start.1 = (f32[1024]{0:T(1024)S(1)}, f32[1024]{0:T(1024)}, u32[]{:S(2)}) copy-start(f32[1024]{0:T(1024)} %param.14) | copy-start | bytes 12292
  107.7 17.7 %all-to-all-start.1 = ((bf16[32,64,128]{2,1,0:T(8,128)(2,1)}), bf16[32,64,128]{2,1,0:T(8,128)(2,1)S(1)}, u32[]{:S(2)}, u32[]{:S(2)}) async-start(bf16[32,64,128]{2,1,0:T(8,128)(2,1)} %attend_last.1), calls=%async_computation.1 | async-start | bytes 1048576 | tf_op jit(solution)/shard_map/all_to_all | solution.py:518
  125.9 14.3 %collective-permute-start.10 = (bf16[128,2048]{1,0:T(8,128)(2,1)S(1)}, bf16[128,2048]{1,0:T(8,128)(2,1)S(1)}, u32[]{:S(2)}, u32[]{:S(2)}) collective-permute-start(bf16[128,2048]{1,0:T(8,128)(2,1)S(1)} %normalized.1.refs_3_), channel_id=1, source_target_pairs={{0,1},{1,2},{2,3},{3,0},{4,5},{5,6},{6,7},{7,4},{8,9},{9,10},{10,1... | collective-permute-start | bytes 1572872 | tf_op jit(solution)/shard_map/ppermute | solution.py:487
  126.2 15.0 %collective-permute-start.9 = (bf16[128,2048]{1,0:T(8,128)(2,1)S(1)}, bf16[128,2048]{1,0:T(8,128)(2,1)S(1)}, u32[]{:S(2)}, u32[]{:S(2)}) collective-permute-start(bf16[128,2048]{1,0:T(8,128)(2,1)S(1)} %normalized.1.refs_3_), channel_id=1, source_target_pairs={{0,4},{1,5},{2,6},{3,7},{4,0},{5,1},{6,2},{7,3},{8,12},{9,13},{10,... | collective-permute-start | bytes 1572872 | tf_op jit(solution)/shard_map/ppermute | solution.py:487
  140.2 12.2 %collective-permute-start.12 = (bf16[128,2048]{1,0:T(8,128)(2,1)S(1)}, bf16[128,2048]{1,0:T(8,128)(2,1)S(1)}, u32[]{:S(2)}, u32[]{:S(2)}) collective-permute-start(bf16[128,2048]{1,0:T(8,128)(2,1)S(1)} %collective-permute-done.10.refs_4_), channel_id=1, source_target_pairs={{0,4},{1,5},{2,6},{3,7},{4,0},{5,1},{6,2},{7,3},{8,12},{9,13},{10,... | collective-permute-start | bytes 1572872 | tf_op jit(solution)/shard_map/ppermute | solution.py:487
  141.2 13.1 %collective-permute-start.14 = (bf16[128,2048]{1,0:T(8,128)(2,1)S(1)}, bf16[128,2048]{1,0:T(8,128)(2,1)S(1)}, u32[]{:S(2)}, u32[]{:S(2)}) collective-permute-start(bf16[128,2048]{1,0:T(8,128)(2,1)S(1)} %collective-permute-done.9.refs_3_), channel_id=1, source_target_pairs={{0,3},{1,0},{2,1},{3,2},{4,7},{5,4},{6,5},{7,6},{8,11},{9,8},{10,9... | collective-permute-start | bytes 1572872 | tf_op jit(solution)/shard_map/ppermute | solution.py:487
  142.4 18.8 %collective-permute-start.13 = (bf16[128,2048]{1,0:T(8,128)(2,1)S(1)}, bf16[128,2048]{1,0:T(8,128)(2,1)S(1)}, u32[]{:S(2)}, u32[]{:S(2)}) collective-permute-start(bf16[128,2048]{1,0:T(8,128)(2,1)S(1)} %collective-permute-done.10.refs_4_), channel_id=1, source_target_pairs={{0,1},{1,2},{2,3},{3,0},{4,5},{5,6},{6,7},{7,4},{8,9},{9,10},{10,1... | collective-permute-start | bytes 1572872 | tf_op jit(solution)/shard_map/ppermute | solution.py:487
  143.3 11.5 %collective-permute-start.2 = (f32[1,1024]{1,0:T(1,128)S(1)}, f32[1,1024]{1,0:T(1,128)S(1)}, u32[]{:S(2)}, u32[]{:S(2)}) collective-permute-start(f32[1,1024]{1,0:T(1,128)S(1)} %bitcast.29), channel_id=1, source_target_pairs={{0,8},{1,9},{2,10},{3,11},{4,12},{5,13},{6,14},{7,15},{8,0},{9,1},... | collective-permute-start | bytes 12296 | tf_op jit(solution)/shard_map/ppermute | solution.py:487
  152.4 14.8 %collective-permute-start.11 = (bf16[128,2048]{1,0:T(8,128)(2,1)S(1)}, bf16[128,2048]{1,0:T(8,128)(2,1)S(1)}, u32[]{:S(2)}, u32[]{:S(2)}) collective-permute-start(bf16[128,2048]{1,0:T(8,128)(2,1)S(1)} %normalized.1.refs_3_), channel_id=1, source_target_pairs={{0,3},{1,0},{2,1},{3,2},{4,7},{5,4},{6,5},{7,6},{8,11},{9,8},{10,9... | collective-permute-start | bytes 1572872 | tf_op jit(solution)/shard_map/ppermute | solution.py:487
  154.4 21.3 %collective-permute-start.15 = (bf16[64,2048]{1,0:T(8,128)(2,1)S(1)}, bf16[64,2048]{1,0:T(8,128)(2,1)S(1)}, u32[]{:S(2)}, u32[]{:S(2)}) collective-permute-start(bf16[64,2048]{1,0:T(8,128)(2,1)S(1)} %shard_map.98), channel_id=1, source_target_pairs={{0,1},{1,2},{2,3},{3,0},{4,5},{5,6},{6,7},{7,4},{8,9},{9,10},{10,1... | collective-permute-start | bytes 786440 | tf_op jit(solution)/shard_map/ppermute | solution.py:487
  154.8 20.9 %collective-permute-start.16 = (bf16[64,2048]{1,0:T(8,128)(2,1)S(1)}, bf16[64,2048]{1,0:T(8,128)(2,1)S(1)}, u32[]{:S(2)}, u32[]{:S(2)}) collective-permute-start(bf16[64,2048]{1,0:T(8,128)(2,1)S(1)} %shard_map.99), channel_id=1, source_target_pairs={{0,3},{1,0},{2,1},{3,2},{4,7},{5,4},{6,5},{7,6},{8,11},{9,8},{10,9... | collective-permute-start | bytes 786440 | tf_op jit(solution)/shard_map/ppermute | solution.py:487
  178.6 5.3 %collective-permute-start.17 = (f32[4,1024]{1,0:T(4,128)S(1)}, f32[4,1024]{1,0:T(4,128)S(1)}, u32[]{:S(2)}, u32[]{:S(2)}) collective-permute-start(f32[4,1024]{1,0:T(4,128)S(1)} %get-tuple-element.39), channel_id=1, source_target_pairs={{0,8},{1,9},{2,10},{3,11},{4,12},{5,13},{6,14},{7,15},{8,0},{9,1},... | collective-permute-start | bytes 49160 | tf_op jit(solution)/shard_map/ppermute | solution.py:487
  198.8 9.6 %collective-permute-start.21 = (bf16[64,2048]{1,0:T(8,128)(2,1)S(1)}, bf16[64,2048]{1,0:T(8,128)(2,1)S(1)}, u32[]{:S(2)}, u32[]{:S(2)}) collective-permute-start(bf16[64,2048]{1,0:T(8,128)(2,1)S(1)} %get-tuple-element.51), channel_id=1, source_target_pairs={{0,3},{1,0},{2,1},{3,2},{4,7},{5,4},{6,5},{7,6},{8,11},{9,8},{10,9... | collective-permute-start | bytes 786440 | tf_op jit(solution)/shard_map/ppermute | solution.py:487
  200.9 8.8 %collective-permute-start.18 = (bf16[64,2048]{1,0:T(8,128)(2,1)S(1)}, bf16[64,2048]{1,0:T(8,128)(2,1)S(1)}, u32[]{:S(2)}, u32[]{:S(2)}) collective-permute-start(bf16[64,2048]{1,0:T(8,128)(2,1)S(1)} %get-tuple-element.48), channel_id=1, source_target_pairs={{0,1},{1,2},{2,3},{3,0},{4,5},{5,6},{6,7},{7,4},{8,9},{9,10},{10,1... | collective-permute-start | bytes 786440 | tf_op jit(solution)/shard_map/ppermute | solution.py:487
  205.1 13.7 %collective-permute-start.23 = (bf16[128,2048]{1,0:T(8,128)(2,1)S(1)}, bf16[128,2048]{1,0:T(8,128)(2,1)S(1)}, u32[]{:S(2)}, u32[]{:S(2)}) collective-permute-start(bf16[128,2048]{1,0:T(8,128)(2,1)S(1)} %get-tuple-element.52), channel_id=1, source_target_pairs={{0,3},{1,0},{2,1},{3,2},{4,7},{5,4},{6,5},{7,6},{8,11},{9,8},{10,9... | collective-permute-start | bytes 1572872 | tf_op jit(solution)/shard_map/ppermute | solution.py:487
  208.5 12.7 %collective-permute-start.22 = (bf16[128,2048]{1,0:T(8,128)(2,1)S(1)}, bf16[128,2048]{1,0:T(8,128)(2,1)S(1)}, u32[]{:S(2)}, u32[]{:S(2)}) collective-permute-start(bf16[128,2048]{1,0:T(8,128)(2,1)S(1)} %shard_map.110), channel_id=1, source_target_pairs={{0,4},{1,5},{2,6},{3,7},{4,0},{5,1},{6,2},{7,3},{8,12},{9,13},{10,... | collective-permute-start | bytes 1572872 | tf_op jit(solution)/shard_map/ppermute | solution.py:487
  209.8 16.1 %collective-permute-start.19 = (bf16[128,2048]{1,0:T(8,128)(2,1)S(1)}, bf16[128,2048]{1,0:T(8,128)(2,1)S(1)}, u32[]{:S(2)}, u32[]{:S(2)}) collective-permute-start(bf16[128,2048]{1,0:T(8,128)(2,1)S(1)} %shard_map.108), channel_id=1, source_target_pairs={{0,1},{1,2},{2,3},{3,0},{4,5},{5,6},{6,7},{7,4},{8,9},{9,10},{10,1... | collective-permute-start | bytes 1572872 | tf_op jit(solution)/shard_map/ppermute | solution.py:487
  214.1 20.6 %collective-permute-start.25 = (bf16[128,2048]{1,0:T(8,128)(2,1)S(1)}, bf16[128,2048]{1,0:T(8,128)(2,1)S(1)}, u32[]{:S(2)}, u32[]{:S(2)}) collective-permute-start(bf16[128,2048]{1,0:T(8,128)(2,1)S(1)} %get-tuple-element.53), channel_id=1, source_target_pairs={{0,1},{1,2},{2,3},{3,0},{4,5},{5,6},{6,7},{7,4},{8,9},{9,10},{10,1... | collective-permute-start | bytes 1572872 | tf_op jit(solution)/shard_map/ppermute | solution.py:487
  221.4 13.2 %collective-permute-start.24 = (bf16[128,2048]{1,0:T(8,128)(2,1)S(1)}, bf16[128,2048]{1,0:T(8,128)(2,1)S(1)}, u32[]{:S(2)}, u32[]{:S(2)}) collective-permute-start(bf16[128,2048]{1,0:T(8,128)(2,1)S(1)} %shard_map.111), channel_id=1, source_target_pairs={{0,3},{1,0},{2,1},{3,2},{4,7},{5,4},{6,5},{7,6},{8,11},{9,8},{10,9... | collective-permute-start | bytes 1572872 | tf_op jit(solution)/shard_map/ppermute | solution.py:487
  226.0 9.3 %collective-permute-start.20 = (bf16[128,2048]{1,0:T(8,128)(2,1)S(1)}, bf16[128,2048]{1,0:T(8,128)(2,1)S(1)}, u32[]{:S(2)}, u32[]{:S(2)}) collective-permute-start(bf16[128,2048]{1,0:T(8,128)(2,1)S(1)} %shard_map.109), channel_id=1, source_target_pairs={{0,4},{1,5},{2,6},{3,7},{4,0},{5,1},{6,2},{7,3},{8,12},{9,13},{10,... | collective-permute-start | bytes 1572872 | tf_op jit(solution)/shard_map/ppermute | solution.py:487

commit v6 on v5

--- a/solution.py
+++ b/solution.py
@@ -70,7 +70,8 @@
     length = lengths[lax.axis_index("c")]
     y_at, y_size = lax.axis_index("y"), lax.axis_size("y")
 
-    def piece(n, at, count, top, summed):
+    def piece(n, at, count):
+        top, summed = None, None
         query = query_ref[pl.ds(at // tokens, sub // tokens)].reshape(sub, HEAD_DIM)
         for start in range(0, depth, part):
             key = key_ref[n, start // tokens : (start + part) // tokens].reshape(part, HEAD_DIM)
@@ -102,12 +103,15 @@
         places = [
             pl.multiple_of(index * rows + at, sub) for at in range(0, rows, sub)
         ]
-        running = [
-            (None, None) if first else (top_ref[pl.ds(at, sub), :1], sum_ref[pl.ds(at, sub), :])
-            for at in places
-        ]
-        done = [piece(n, at, count, *run) for at, run in zip(places, running)]
+        done = [piece(n, at, count) for at in places]
         for at, (top, summed) in zip(places, done):
+            if not first:
+                old_top = top_ref[pl.ds(at, sub), :1]
+                new_top = jnp.maximum(old_top, top)
+                summed = sum_ref[pl.ds(at, sub), :] * jnp.exp2(
+                    (old_top - new_top) * scale
+                ) + summed * jnp.exp2((top - new_top) * scale)
+                top = new_top
             if last:
                 finish(at, summed)
             else:

time: 237 us -> 231 us (0.975)
  Pallas kernels: 72.7 us -> 66.2 us
    pallas_call x3, Pallas kernels: 34.7 us -> 28.1 us  [attend_chunks(): pl.pallas_call(body, in_specs=[pl.BlockSpec(memory_space=pltpu.SMEM)] + [...]
  transfers between devices with their start and end apart: 28 -> 28, of which waited for: 16 -> 16; matrix products, arithmetic and copies ran while one was open for 1% -> 1% of each run, Pallas kernels for 27% -> 25%
where the time goes in v6:
time: 231 us; the launch traced here: 230 us
  waiting for transfers between devices  94.3 us (41%)
  Pallas kernels  66.2 us (29%)
  starting transfers between devices  49.7 us (22%)
  blocking collectives  10.4 us (5%)
  local copies, waits for them, and re-layouts  7.4 us (3%)
    ppermute x26, waiting for transfers between devices, move(): return lax.ppermute(array, AXES, shift_perm(sizes, **by))  65.7 us
    ppermute x26, starting transfers between devices, move(): return lax.ppermute(array, AXES, shift_perm(sizes, **by))  35.6 us
    pallas_call x18, Pallas kernels, simple_call(): pl.pallas_call(body, in_specs=in_specs, out_specs=jax.tree.map(lambda _:...  34.1 us
    pallas_call x3, Pallas kernels, attend_chunks(): pl.pallas_call(body, in_specs=[pl.BlockSpec(memory_space=pltpu.SMEM)] + [...  28.1 us
    all_to_all x1, waiting for transfers between devices, local(): lax.all_to_all(stacked, PLANE, split_axis=0, concat_axis=0, tiled=True)  16.8 us
    all_to_all x1, waiting for transfers between devices, local(): lax.all_to_all(attended, PLANE, split_axis=0, concat_axis=0, tiled=True)  11.8 us
    all_to_all x1, blocking collectives, local(): lax.all_to_all(spread, ('y', 'c'), split_axis=0, concat_axis=0, tiled=True)  10.4 us
    all_to_all x1, starting transfers between devices, local(): lax.all_to_all(stacked, PLANE, split_axis=0, concat_axis=0, tiled=True)  8.28 us
  transfers between devices with their start and end apart: 28, of which 16 were waited for; matrix products, arithmetic and copies ran while one was open for 1% of the time, Pallas kernels for 25%

profile of v6, /device:TPU:0, one launch (start us, length us, event | category | flops | bytes accessed | tf_op | source)
XLA Modules:
  0.0 230.3 jit_solution(18329630998834635276)
XLA Ops:
  0.6 1.5 reshape.23
  2.1 0.2 copy.20
  2.3 0.3 reshape.24
  2.7 0.2 copy.21
  2.9 0.3 reshape.25
  3.2 0.2 copy.22
  3.5 1.4 pad_maximum_fusion
  4.8 8.3 %all-to-all-start = ((bf16[32,3,64,128]{3,2,1,0:T(8,128)(2,1)}), bf16[32,3,64,128]{3,2,1,0:T(8,128)(2,1)S(1)}, u32[]{:S(2)}, u32[]{:S(2)}) async-start(bf16[32,3,64,128]{3,2,1,0:T(8,128)(2,1)} %pad_maximum_fusion), calls=%async_computation | async-start | bytes 3145728 | tf_op jit(solution)/shard_map/all_to_all | solution.py:494
  13.1 3.1 %constant_dynamic-slice_fusion = bf16[2048,512]{1,0:T(8,128)(2,1)} fusion(bf16[2048,1024]{1,0:T(8,128)(2,1)} %own_hbm.1, s32[]{:T(128)S(6)} %select_n.3), kind=kLoop, calls=%fused_computation.5 | loop fusion | bytes 4194308 | tf_op jit(solution)/shard_map/dynamic_slice | solution.py:505
  16.2 3.3 %collective-permute-start = (bf16[2048,512]{1,0:T(8,128)(2,1)}, bf16[2048,512]{1,0:T(8,128)(2,1)}, u32[]{:S(2)}, u32[]{:S(2)}) collective-permute-start(bf16[2048,512]{1,0:T(8,128)(2,1)} %constant_dynamic-slice_fusion), channel_id=1, source_target_pairs={{0,8},{1,9},{2,10},{3,11},{4,12},{5,13},{6,14},{7,15},{8,0},{9,1},... | collective-permute-start | bytes 6291464 | tf_op jit(solution)/shard_map/ppermute | solution.py:491
  19.5 16.8 %all-to-all-done.refs_1_.refs_2_.refs_3_ = bf16[32,3,64,128]{3,2,1,0:T(8,128)(2,1)S(1)} async-done(((bf16[32,3,64,128]{3,2,1,0:T(8,128)(2,1)}), bf16[32,3,64,128]{3,2,1,0:T(8,128)(2,1)S(1)}, u32[]{:S(2)}, u32[]{:S(2)}) %all-to-all-start) | async-done | bytes 1572896 | tf_op jit(solution)/shard_map/all_to_all | solution.py:494
  36.4 1.6 collective-permute-start.3
  38.0 1.7 collective-permute-start.5
  39.7 0.4 collective-permute-start.7
  40.1 2.9 %collective-permute-start.8 = (bf16[32,64,128]{2,1,0:T(8,128)(2,1)S(1)}, bf16[32,64,128]{2,1,0:T(8,128)(2,1)S(1)}, u32[]{:S(2)}, u32[]{:S(2)}) collective-permute-start(bf16[32,64,128]{2,1,0:T(8,128)(2,1)S(1)} %get-tuple-element.55), channel_id=1, source_target_pairs={{0,96},{1,97},{2,98},{3,99},{4,100},{5,101},{6,102},{7,103},{8,104... | collective-permute-start | bytes 1572872 | tf_op jit(solution)/shard_map/ppermute | solution.py:491
  42.9 6.5 %attend_first.1 = (f32[2048,128]{1,0:T(8,128)S(1)}, f32[2048,256]{1,0:T(8,128)S(1)}) custom-call(s32[2]{0:T(128)S(1)} %copy-done.2, bf16[32,3,64,128]{3,2,1,0:T(8,128)(2,1)S(1)} %all-to-all-done.refs_1_.refs_2_.refs_3_, bf16[32,3,64,128]{3,2,1,0:T(8,128)(2,1)S(1)} %all-to-all-done.refs_1_.refs_2_.refs_3_, ...), custom_call_target="tpu_custom_call" | custom-call | flops 4294967296 | bytes 4194304 | tf_op jit(solution)/shard_map/attend_first/pallas_call | solution.py:170
  49.5 3.0 %collective-permute-done.3.refs_2_ = bf16[32,64,128]{2,1,0:T(8,128)(2,1)S(1)} collective-permute-done((bf16[32,64,128]{2,1,0:T(8,128)(2,1)S(1)}, bf16[32,64,128]{2,1,0:T(8,128)(2,1)S(1)}, u32[]{:S(2)}, u32[]{:S(2)}) %collective-permute-start.3) | collective-permute-done | bytes 524320 | tf_op jit(solution)/shard_map/ppermute | solution.py:491
  52.5 0.4 collective-permute-start.4
  52.8 2.9 %collective-permute-start.6 = (bf16[32,64,128]{2,1,0:T(8,128)(2,1)S(1)}, bf16[32,64,128]{2,1,0:T(8,128)(2,1)S(1)}, u32[]{:S(2)}, u32[]{:S(2)}) collective-permute-start(bf16[32,64,128]{2,1,0:T(8,128)(2,1)S(1)} %collective-permute-done.5.refs_5_), channel_id=1, source_target_pairs={{0,96},{1,97},{2,98},{3,99},{4,100},{5,101},{6,102},{7,103},{8,104... | collective-permute-start | bytes 1572872 | tf_op jit(solution)/shard_map/ppermute | solution.py:491
  55.7 23.7 %collective-permute-done.near_hbm = bf16[2048,512]{1,0:T(8,128)(2,1)} collective-permute-done((bf16[2048,512]{1,0:T(8,128)(2,1)}, bf16[2048,512]{1,0:T(8,128)(2,1)}, u32[]{:S(2)}, u32[]{:S(2)}) %collective-permute-start) | collective-permute-done | bytes 2097184 | tf_op jit(solution)/shard_map/ppermute | solution.py:491
  79.5 13.8 %attend_next.1 = (f32[2048,128]{1,0:T(8,128)S(1)}, f32[2048,256]{1,0:T(8,128)S(1)}) custom-call(s32[2]{0:T(128)S(1)} %copy-done.2, bf16[32,3,64,128]{3,2,1,0:T(8,128)(2,1)S(1)} %all-to-all-done.refs_1_.refs_2_.refs_3_, bf16[32,64,128]{2,1,0:T(8,128)(2,1)S(1)} %collective-permute-done.3.refs_2_, bf16[32,64,128]{2,1,0:T(8,128)(2,1)S(1)} %collective-permute-done.7.refs_3_, ...), custom_call_target="tpu_custom_call" | custom-call | flops 8589934592 | bytes 4194304 | tf_op jit(solution)/shard_map/attend_next/pallas_call | solution.py:170
  93.3 7.8 %attend_last.1 = bf16[32,64,128]{2,1,0:T(8,128)(2,1)} custom-call(s32[2]{0:T(128)S(1)} %copy-done.2, bf16[32,3,64,128]{3,2,1,0:T(8,128)(2,1)S(1)} %all-to-all-done.refs_1_.refs_2_.refs_3_, bf16[32,64,128]{2,1,0:T(8,128)(2,1)S(1)} %collective-permute-done.4.refs_2_, bf16[32,64,128]{2,1,0:T(8,128)(2,1)S(1)} %collective-permute-done.6.refs_3_, ...), custom_call_target="tpu_custom_call" | custom-call | flops 4294967296 | bytes 4194304 | tf_op jit(solution)/shard_map/attend_last/pallas_call | solution.py:170
  101.1 5.8 %all-to-all-start.1 = ((bf16[32,64,128]{2,1,0:T(8,128)(2,1)}), bf16[32,64,128]{2,1,0:T(8,128)(2,1)S(1)}, u32[]{:S(2)}, u32[]{:S(2)}) async-start(bf16[32,64,128]{2,1,0:T(8,128)(2,1)} %attend_last.1), calls=%async_computation.1 | async-start | bytes 1048576 | tf_op jit(solution)/shard_map/all_to_all | solution.py:522
  107.1 11.8 %all-to-all-done.1.refs_0_ = bf16[32,64,128]{2,1,0:T(8,128)(2,1)S(1)} async-done(((bf16[32,64,128]{2,1,0:T(8,128)(2,1)}), bf16[32,64,128]{2,1,0:T(8,128)(2,1)S(1)}, u32[]{:S(2)}, u32[]{:S(2)}) %all-to-all-start.1) | async-done | bytes 524320 | tf_op jit(solution)/shard_map/all_to_all | solution.py:522
  118.9 0.4 normalized.1.refs_3_
  119.3 0.3 collective-permute-start.10
  119.6 0.6 collective-permute-start.9
  120.2 13.4 %collective-permute-done.10.refs_4_ = bf16[128,2048]{1,0:T(8,128)(2,1)S(1)} collective-permute-done((bf16[128,2048]{1,0:T(8,128)(2,1)S(1)}, bf16[128,2048]{1,0:T(8,128)(2,1)S(1)}, u32[]{:S(2)}, u32[]{:S(2)}) %collective-permute-start.10) | collective-permute-done | bytes 524320 | tf_op jit(solution)/shard_map/ppermute | solution.py:491
  133.6 1.0 collective-permute-start.12
  134.7 1.2 collective-permute-start.14
  135.9 0.8 collective-permute-start.13
  136.7 2.4 %collective-permute-start.2 = (f32[1,1024]{1,0:T(1,128)S(1)}, f32[1,1024]{1,0:T(1,128)S(1)}, u32[]{:S(2)}, u32[]{:S(2)}) collective-permute-start(f32[1,1024]{1,0:T(1,128)S(1)} %bitcast.29), channel_id=1, source_target_pairs={{0,8},{1,9},{2,10},{3,11},{4,12},{5,13},{6,14},{7,15},{8,0},{9,1},... | collective-permute-start | bytes 12296 | tf_op jit(solution)/shard_map/ppermute | solution.py:491
  139.1 6.8 %collective-permute-done.12.refs_3_.in_ref = bf16[128,2048]{1,0:T(8,128)(2,1)S(1)} collective-permute-done((bf16[128,2048]{1,0:T(8,128)(2,1)S(1)}, bf16[128,2048]{1,0:T(8,128)(2,1)S(1)}, u32[]{:S(2)}, u32[]{:S(2)}) %collective-permute-start.12) | collective-permute-done | bytes 524320 | tf_op jit(solution)/shard_map/ppermute | solution.py:491
  145.8 0.8 collective-permute-start.11
  146.7 1.1 collective-permute-done.14.refs_5_.in_ref
  147.8 0.2 collective-permute-start.15
  148.0 0.2 collective-permute-done.2.other_bias_ref
  148.2 3.1 %collective-permute-start.16 = (bf16[64,2048]{1,0:T(8,128)(2,1)S(1)}, bf16[64,2048]{1,0:T(8,128)(2,1)S(1)}, u32[]{:S(2)}, u32[]{:S(2)}) collective-permute-start(bf16[64,2048]{1,0:T(8,128)(2,1)S(1)} %shard_map.99), channel_id=1, source_target_pairs={{0,3},{1,0},{2,1},{3,2},{4,7},{5,4},{6,5},{7,6},{8,11},{9,8},{10,9... | collective-permute-start | bytes 786440 | tf_op jit(solution)/shard_map/ppermute | solution.py:491
  151.3 3.5 %side_by_side.1 = (bf16[2048,2048]{1,0:T(8,128)(2,1)S(1)}, f32[1,2048]{1,0:T(1,128)S(1)}) custom-call(bf16[2048,1024]{1,0:T(8,128)(2,1)} %own_hbm.1, bf16[2048,512]{1,0:T(8,128)(2,1)} %collective-permute-done.near_hbm, bf16[2048,512]{1,0:T(8,128)(2,1)} %collective-permute-done.1.far_hbm, f32[1,1024]{1,0:T(1,128)S(1)} %bitcast.30, ...), custom_call_target="tpu_custom_call" | custom-call | bytes 16777216 | tf_op jit(solution)/shard_map/side_by_side/pallas_call | solution.py:258
  154.9 5.7 %shard_map.97 = (f32[384,2048]{1,0:T(8,128)S(1)}, f32[2,2048]{1,0:T(2,128)S(1)}) custom-call(s32[2]{0:T(128)S(1)} %copy-done.2, bf16[2048,2048]{1,0:T(8,128)(2,1)S(1)} %get-tuple-element.28.refs_1_.refs_2_, f32[1,2048]{1,0:T(1,128)S(1)} %get-tuple-element.29.refs_2_, bf16[128,2048]{1,0:T(8,128)(2,1)S(1)} %collective-permute-done.12.refs_3_.in_ref, ...), custom_call_target="tpu_custom_call" | custom-call | flops 6442450944 | bytes 19939344 | tf_op jit(solution)/shard_map/pallas_call | solution.py:281
  160.6 5.7 %shard_map.96 = (f32[384,2048]{1,0:T(8,128)S(1)}, f32[2,2048]{1,0:T(2,128)S(1)}) custom-call(s32[2]{0:T(128)S(1)} %copy-done.2, bf16[2048,2048]{1,0:T(8,128)(2,1)S(1)} %get-tuple-element.28.refs_1_.refs_2_, f32[1,2048]{1,0:T(1,128)S(1)} %get-tuple-element.29.refs_2_, bf16[128,2048]{1,0:T(8,128)(2,1)S(1)} %collective-permute-done.9.refs_3_, ...), custom_call_target="tpu_custom_call" | custom-call | flops 6442450944 | bytes 19939344 | tf_op jit(solution)/shard_map/pallas_call | solution.py:281
  166.3 2.8 %shard_map.95 = (f32[128,2048]{1,0:T(8,128)S(1)}, f32[2,2048]{1,0:T(2,128)S(1)}) custom-call(s32[2]{0:T(128)S(1)} %copy-done.2, bf16[2048,2048]{1,0:T(8,128)(2,1)S(1)} %get-tuple-element.28.refs_1_.refs_2_, f32[1,2048]{1,0:T(1,128)S(1)} %get-tuple-element.29.refs_2_, bf16[128,2048]{1,0:T(8,128)(2,1)S(1)} %normalized.1.refs_3_), custom_call_target="tpu_custom_call" | custom-call | flops 4294967296 | bytes 17842192 | tf_op jit(solution)/shard_map/pallas_call | solution.py:281
  169.1 2.8 %shard_map.100 = (f32[128,2048]{1,0:T(8,128)S(1)}, f32[2,2048]{1,0:T(2,128)S(1)}) custom-call(s32[2]{0:T(128)S(1)} %copy-done.2, bf16[2048,2048]{1,0:T(8,128)(2,1)S(1)} %get-tuple-element.28.refs_1_.refs_2_, f32[1,2048]{1,0:T(1,128)S(1)} %get-tuple-element.29.refs_2_, bf16[64,2048]{1,0:T(8,128)(2,1)S(1)} %collective-permute-done.15.refs_3_, ...), custom_call_target="tpu_custom_call" | custom-call | flops 4294967296 | bytes 17842192 | tf_op jit(solution)/shard_map/pallas_call | solution.py:281
  172.0 2.7 %collective-permute-start.17 = (f32[4,1024]{1,0:T(4,128)S(1)}, f32[4,1024]{1,0:T(4,128)S(1)}, u32[]{:S(2)}, u32[]{:S(2)}) collective-permute-start(f32[4,1024]{1,0:T(4,128)S(1)} %get-tuple-element.39), channel_id=1, source_target_pairs={{0,8},{1,9},{2,10},{3,11},{4,12},{5,13},{6,14},{7,15},{8,0},{9,1},... | collective-permute-start | bytes 49160 | tf_op jit(solution)/shard_map/ppermute | solution.py:491
  174.7 2.6 %collective-permute-done.17.two_ref = f32[4,1024]{1,0:T(4,128)S(1)} collective-permute-done((f32[4,1024]{1,0:T(4,128)S(1)}, f32[4,1024]{1,0:T(4,128)S(1)}, u32[]{:S(2)}, u32[]{:S(2)}) %collective-permute-start.17) | collective-permute-done | bytes 16416 | tf_op jit(solution)/shard_map/ppermute | solution.py:491
  177.3 10.4 %all_to_all.15.gathered_ref = f32[8,4,1024]{2,1,0:T(4,128)S(1)} all-to-all(f32[8,4,1024]{2,1,0:T(4,128)S(1)} %shard_map.102), channel_id=1, replica_groups=mesh['y'=4,'c'=2,'u'=2,'w'=2,'z'=4] {'y','c'}, dimensions={0} | all-to-all | bytes 262144 | tf_op jit(solution)/shard_map/all_to_all | solution.py:547
  187.7 1.2 shard_map.103
  188.9 3.4 %shard_map.107 = (bf16[64,2048]{1,0:T(8,128)(2,1)S(1)}, bf16[64,2048]{1,0:T(8,128)(2,1)S(1)}) custom-call(f32[128,2048]{1,0:T(8,128)S(1)} %get-tuple-element.47.refs_0_, f32[2,2048]{1,0:T(2,128)S(1)} %get-tuple-element.42.refs_1_, bf16[2048,2048]{1,0:T(8,128)(2,1)S(1)} %get-tuple-element.28.refs_1_.refs_2_), custom_call_target="tpu_custom_call" | custom-call | flops 4294967296 | bytes 18907136 | tf_op jit(solution)/shard_map/pallas_call | solution.py:281
  192.3 2.1 collective-permute-start.21
  194.4 4.2 %shard_map.106 = (bf16[128,2048]{1,0:T(8,128)(2,1)S(1)}, bf16[128,2048]{1,0:T(8,128)(2,1)S(1)}, bf16[128,2048]{1,0:T(8,128)(2,1)S(1)}) custom-call(f32[384,2048]{1,0:T(8,128)S(1)} %get-tuple-element.45.refs_0_, f32[2,2048]{1,0:T(2,128)S(1)} %get-tuple-element.42.refs_1_, bf16[2048,2048]{1,0:T(8,128)(2,1)S(1)} %get-tuple-element.28.refs_1_.refs_2_), custom_call_target="tpu_custom_call" | custom-call | flops 6442450944 | bytes 23101440 | tf_op jit(solution)/shard_map/pallas_call | solution.py:281
  198.6 3.3 %collective-permute-start.23 = (bf16[128,2048]{1,0:T(8,128)(2,1)S(1)}, bf16[128,2048]{1,0:T(8,128)(2,1)S(1)}, u32[]{:S(2)}, u32[]{:S(2)}) collective-permute-start(bf16[128,2048]{1,0:T(8,128)(2,1)S(1)} %get-tuple-element.52), channel_id=1, source_target_pairs={{0,3},{1,0},{2,1},{3,2},{4,7},{5,4},{6,5},{7,6},{8,11},{9,8},{10,9... | collective-permute-start | bytes 1572872 | tf_op jit(solution)/shard_map/ppermute | solution.py:491
  202.0 1.1 collective-permute-start.22
  203.3 4.2 %shard_map.105 = (bf16[128,2048]{1,0:T(8,128)(2,1)S(1)}, bf16[128,2048]{1,0:T(8,128)(2,1)S(1)}, bf16[128,2048]{1,0:T(8,128)(2,1)S(1)}) custom-call(f32[384,2048]{1,0:T(8,128)S(1)} %get-tuple-element.43.refs_0_, f32[2,2048]{1,0:T(2,128)S(1)} %get-tuple-element.42.refs_1_, bf16[2048,2048]{1,0:T(8,128)(2,1)S(1)} %get-tuple-element.28.refs_1_.refs_2_), custom_call_target="tpu_custom_call" | custom-call | flops 6442450944 | bytes 23101440 | tf_op jit(solution)/shard_map/pallas_call | solution.py:281
  207.6 4.7 %collective-permute-done.23.refs_1_ = bf16[128,2048]{1,0:T(8,128)(2,1)S(1)} collective-permute-done((bf16[128,2048]{1,0:T(8,128)(2,1)S(1)}, bf16[128,2048]{1,0:T(8,128)(2,1)S(1)}, u32[]{:S(2)}, u32[]{:S(2)}) %collective-permute-start.23) | collective-permute-done | bytes 524320 | tf_op jit(solution)/shard_map/ppermute | solution.py:491
  212.3 2.4 %collective-permute-done.22.refs_0_ = bf16[128,2048]{1,0:T(8,128)(2,1)S(1)} collective-permute-done((bf16[128,2048]{1,0:T(8,128)(2,1)S(1)}, bf16[128,2048]{1,0:T(8,128)(2,1)S(1)}, u32[]{:S(2)}, u32[]{:S(2)}) %collective-permute-start.22) | collective-permute-done | bytes 524320 | tf_op jit(solution)/shard_map/ppermute | solution.py:491
  214.7 0.2 shard_map.111
  214.9 1.6 collective-permute-start.24
  216.5 2.8 %collective-permute-done.19.refs_0_ = bf16[128,2048]{1,0:T(8,128)(2,1)S(1)} collective-permute-done((bf16[128,2048]{1,0:T(8,128)(2,1)S(1)}, bf16[128,2048]{1,0:T(8,128)(2,1)S(1)}, u32[]{:S(2)}, u32[]{:S(2)}) %collective-permute-start.19) | collective-permute-done | bytes 524320 | tf_op jit(solution)/shard_map/ppermute | solution.py:491
  219.4 1.1 collective-permute-start.20
  220.5 3.4 %shard_map.104.base_ref = bf16[128,2048]{1,0:T(8,128)(2,1)S(1)} custom-call(f32[128,2048]{1,0:T(8,128)S(1)} %get-tuple-element.41.refs_0_, f32[2,2048]{1,0:T(2,128)S(1)} %get-tuple-element.42.refs_1_, bf16[2048,2048]{1,0:T(8,128)(2,1)S(1)} %get-tuple-element.28.refs_1_.refs_2_), custom_call_target="tpu_custom_call" | custom-call | flops 4294967296 | bytes 18907136 | tf_op jit(solution)/shard_map/pallas_call | solution.py:281
  223.9 4.1 %collective-permute-done.25.refs_2_ = bf16[128,2048]{1,0:T(8,128)(2,1)S(1)} collective-permute-done((bf16[128,2048]{1,0:T(8,128)(2,1)S(1)}, bf16[128,2048]{1,0:T(8,128)(2,1)S(1)}, u32[]{:S(2)}, u32[]{:S(2)}) %collective-permute-start.25) | collective-permute-done | bytes 524320 | tf_op jit(solution)/shard_map/ppermute | solution.py:491
  228.1 0.6 collective-permute-done.20.refs_0_
  228.7 0.3 shard_map.112
  228.9 1.3 copy.31
  (39 shorter events, 0.9 us)
Async XLA Ops:
  0.6 1.7 copy-start.3
  0.6 2.3 copy-start.4
  4.8 31.5 %all-to-all-start = ((bf16[32,3,64,128]{3,2,1,0:T(8,128)(2,1)}), bf16[32,3,64,128]{3,2,1,0:T(8,128)(2,1)S(1)}, u32[]{:S(2)}, u32[]{:S(2)}) async-start(bf16[32,3,64,128]{3,2,1,0:T(8,128)(2,1)} %pad_maximum_fusion), calls=%async_computation | async-start | bytes 3145728 | tf_op jit(solution)/shard_map/all_to_all | solution.py:494
  16.2 26.8 %copy-start.2 = (s32[2]{0:T(128)S(1)}, s32[2]{0:T(128)}, u32[]{:S(2)}) copy-start(s32[2]{0:T(128)} %lengths_ref.1) | copy-start | bytes 28
  16.2 63.3 %collective-permute-start = (bf16[2048,512]{1,0:T(8,128)(2,1)}, bf16[2048,512]{1,0:T(8,128)(2,1)}, u32[]{:S(2)}, u32[]{:S(2)}) collective-permute-start(bf16[2048,512]{1,0:T(8,128)(2,1)} %constant_dynamic-slice_fusion), channel_id=1, source_target_pairs={{0,8},{1,9},{2,10},{3,11},{4,12},{5,13},{6,14},{7,15},{8,0},{9,1},... | collective-permute-start | bytes 6291464 | tf_op jit(solution)/shard_map/ppermute | solution.py:491
  36.4 16.1 %collective-permute-start.3 = (bf16[32,64,128]{2,1,0:T(8,128)(2,1)S(1)}, bf16[32,64,128]{2,1,0:T(8,128)(2,1)S(1)}, u32[]{:S(2)}, u32[]{:S(2)}) collective-permute-start(bf16[32,64,128]{2,1,0:T(8,128)(2,1)S(1)} %get-tuple-element.55), channel_id=1, source_target_pairs={{0,32},{1,33},{2,34},{3,35},{4,36},{5,37},{6,38},{7,39},{8,40},{9,... | collective-permute-start | bytes 1572872 | tf_op jit(solution)/shard_map/ppermute | solution.py:491
  38.0 14.8 %collective-permute-start.5 = (bf16[32,64,128]{2,1,0:T(8,128)(2,1)S(1)}, bf16[32,64,128]{2,1,0:T(8,128)(2,1)S(1)}, u32[]{:S(2)}, u32[]{:S(2)}) collective-permute-start(bf16[32,64,128]{2,1,0:T(8,128)(2,1)S(1)} %get-tuple-element.54), channel_id=1, source_target_pairs={{0,96},{1,97},{2,98},{3,99},{4,100},{5,101},{6,102},{7,103},{8,104... | collective-permute-start | bytes 1572872 | tf_op jit(solution)/shard_map/ppermute | solution.py:491
  39.7 39.8 %collective-permute-start.7 = (bf16[32,64,128]{2,1,0:T(8,128)(2,1)S(1)}, bf16[32,64,128]{2,1,0:T(8,128)(2,1)S(1)}, u32[]{:S(2)}, u32[]{:S(2)}) collective-permute-start(bf16[32,64,128]{2,1,0:T(8,128)(2,1)S(1)} %get-tuple-element.54), channel_id=1, source_target_pairs={{0,32},{1,33},{2,34},{3,35},{4,36},{5,37},{6,38},{7,39},{8,40},{9,... | collective-permute-start | bytes 1572872 | tf_op jit(solution)/shard_map/ppermute | solution.py:491
  40.1 39.4 %collective-permute-start.8 = (bf16[32,64,128]{2,1,0:T(8,128)(2,1)S(1)}, bf16[32,64,128]{2,1,0:T(8,128)(2,1)S(1)}, u32[]{:S(2)}, u32[]{:S(2)}) collective-permute-start(bf16[32,64,128]{2,1,0:T(8,128)(2,1)S(1)} %get-tuple-element.55), channel_id=1, source_target_pairs={{0,96},{1,97},{2,98},{3,99},{4,100},{5,101},{6,102},{7,103},{8,104... | collective-permute-start | bytes 1572872 | tf_op jit(solution)/shard_map/ppermute | solution.py:491
  52.5 40.8 %collective-permute-start.4 = (bf16[32,64,128]{2,1,0:T(8,128)(2,1)S(1)}, bf16[32,64,128]{2,1,0:T(8,128)(2,1)S(1)}, u32[]{:S(2)}, u32[]{:S(2)}) collective-permute-start(bf16[32,64,128]{2,1,0:T(8,128)(2,1)S(1)} %collective-permute-done.3.refs_2_), channel_id=1, source_target_pairs={{0,32},{1,33},{2,34},{3,35},{4,36},{5,37},{6,38},{7,39},{8,40},{9,... | collective-permute-start | bytes 1572872 | tf_op jit(solution)/shard_map/ppermute | solution.py:491
  52.8 40.5 %collective-permute-start.6 = (bf16[32,64,128]{2,1,0:T(8,128)(2,1)S(1)}, bf16[32,64,128]{2,1,0:T(8,128)(2,1)S(1)}, u32[]{:S(2)}, u32[]{:S(2)}) collective-permute-start(bf16[32,64,128]{2,1,0:T(8,128)(2,1)S(1)} %collective-permute-done.5.refs_5_), channel_id=1, source_target_pairs={{0,96},{1,97},{2,98},{3,99},{4,100},{5,101},{6,102},{7,103},{8,104... | collective-permute-start | bytes 1572872 | tf_op jit(solution)/shard_map/ppermute | solution.py:491
  79.5 71.9 %collective-permute-start.1 = (bf16[2048,512]{1,0:T(8,128)(2,1)}, bf16[2048,512]{1,0:T(8,128)(2,1)}, u32[]{:S(2)}, u32[]{:S(2)}) collective-permute-start(bf16[2048,512]{1,0:T(8,128)(2,1)} %collective-permute-done.near_hbm), channel_id=1, source_target_pairs={{0,16},{1,17},{2,18},{3,19},{4,20},{5,21},{6,22},{7,23},{8,24},{9,... | collective-permute-start | bytes 6291464 | tf_op jit(solution)/shard_map/ppermute | solution.py:491
  93.3 13.6 %copy-start.5 = (bf16[64,2,2048]{2,1,0:T(2,128)(2,1)S(1)}, bf16[64,2,2048]{2,1,0:T(2,128)(2,1)}, u32[]{:S(2)}) copy-start(bf16[64,2,2048]{2,1,0:T(2,128)(2,1)} %param.11) | copy-start | bytes 1572868
  101.1 17.8 %copy-start = (f32[2048]{0:T(1024)S(1)}, f32[2048]{0:T(1024)}, u32[]{:S(2)}) copy-start(f32[2048]{0:T(1024)} %param.12) | copy-start | bytes 24580
  101.1 35.6 %copy-start.1 = (f32[1024]{0:T(1024)S(1)}, f32[1024]{0:T(1024)}, u32[]{:S(2)}) copy-start(f32[1024]{0:T(1024)} %param.14) | copy-start | bytes 12292
  101.1 17.7 %all-to-all-start.1 = ((bf16[32,64,128]{2,1,0:T(8,128)(2,1)}), bf16[32,64,128]{2,1,0:T(8,128)(2,1)S(1)}, u32[]{:S(2)}, u32[]{:S(2)}) async-start(bf16[32,64,128]{2,1,0:T(8,128)(2,1)} %attend_last.1), calls=%async_computation.1 | async-start | bytes 1048576 | tf_op jit(solution)/shard_map/all_to_all | solution.py:522
  119.3 14.3 %collective-permute-start.10 = (bf16[128,2048]{1,0:T(8,128)(2,1)S(1)}, bf16[128,2048]{1,0:T(8,128)(2,1)S(1)}, u32[]{:S(2)}, u32[]{:S(2)}) collective-permute-start(bf16[128,2048]{1,0:T(8,128)(2,1)S(1)} %normalized.1.refs_3_), channel_id=1, source_target_pairs={{0,1},{1,2},{2,3},{3,0},{4,5},{5,6},{6,7},{7,4},{8,9},{9,10},{10,1... | collective-permute-start | bytes 1572872 | tf_op jit(solution)/shard_map/ppermute | solution.py:491
  119.6 15.0 %collective-permute-start.9 = (bf16[128,2048]{1,0:T(8,128)(2,1)S(1)}, bf16[128,2048]{1,0:T(8,128)(2,1)S(1)}, u32[]{:S(2)}, u32[]{:S(2)}) collective-permute-start(bf16[128,2048]{1,0:T(8,128)(2,1)S(1)} %normalized.1.refs_3_), channel_id=1, source_target_pairs={{0,4},{1,5},{2,6},{3,7},{4,0},{5,1},{6,2},{7,3},{8,12},{9,13},{10,... | collective-permute-start | bytes 1572872 | tf_op jit(solution)/shard_map/ppermute | solution.py:491
  133.6 12.2 %collective-permute-start.12 = (bf16[128,2048]{1,0:T(8,128)(2,1)S(1)}, bf16[128,2048]{1,0:T(8,128)(2,1)S(1)}, u32[]{:S(2)}, u32[]{:S(2)}) collective-permute-start(bf16[128,2048]{1,0:T(8,128)(2,1)S(1)} %collective-permute-done.10.refs_4_), channel_id=1, source_target_pairs={{0,4},{1,5},{2,6},{3,7},{4,0},{5,1},{6,2},{7,3},{8,12},{9,13},{10,... | collective-permute-start | bytes 1572872 | tf_op jit(solution)/shard_map/ppermute | solution.py:491
  134.7 13.1 %collective-permute-start.14 = (bf16[128,2048]{1,0:T(8,128)(2,1)S(1)}, bf16[128,2048]{1,0:T(8,128)(2,1)S(1)}, u32[]{:S(2)}, u32[]{:S(2)}) collective-permute-start(bf16[128,2048]{1,0:T(8,128)(2,1)S(1)} %collective-permute-done.9.refs_3_), channel_id=1, source_target_pairs={{0,3},{1,0},{2,1},{3,2},{4,7},{5,4},{6,5},{7,6},{8,11},{9,8},{10,9... | collective-permute-start | bytes 1572872 | tf_op jit(solution)/shard_map/ppermute | solution.py:491
  135.9 19.0 %collective-permute-start.13 = (bf16[128,2048]{1,0:T(8,128)(2,1)S(1)}, bf16[128,2048]{1,0:T(8,128)(2,1)S(1)}, u32[]{:S(2)}, u32[]{:S(2)}) collective-permute-start(bf16[128,2048]{1,0:T(8,128)(2,1)S(1)} %collective-permute-done.10.refs_4_), channel_id=1, source_target_pairs={{0,1},{1,2},{2,3},{3,0},{4,5},{5,6},{6,7},{7,4},{8,9},{9,10},{10,1... | collective-permute-start | bytes 1572872 | tf_op jit(solution)/shard_map/ppermute | solution.py:491
  136.7 11.5 %collective-permute-start.2 = (f32[1,1024]{1,0:T(1,128)S(1)}, f32[1,1024]{1,0:T(1,128)S(1)}, u32[]{:S(2)}, u32[]{:S(2)}) collective-permute-start(f32[1,1024]{1,0:T(1,128)S(1)} %bitcast.29), channel_id=1, source_target_pairs={{0,8},{1,9},{2,10},{3,11},{4,12},{5,13},{6,14},{7,15},{8,0},{9,1},... | collective-permute-start | bytes 12296 | tf_op jit(solution)/shard_map/ppermute | solution.py:491
  145.8 14.8 %collective-permute-start.11 = (bf16[128,2048]{1,0:T(8,128)(2,1)S(1)}, bf16[128,2048]{1,0:T(8,128)(2,1)S(1)}, u32[]{:S(2)}, u32[]{:S(2)}) collective-permute-start(bf16[128,2048]{1,0:T(8,128)(2,1)S(1)} %normalized.1.refs_3_), channel_id=1, source_target_pairs={{0,3},{1,0},{2,1},{3,2},{4,7},{5,4},{6,5},{7,6},{8,11},{9,8},{10,9... | collective-permute-start | bytes 1572872 | tf_op jit(solution)/shard_map/ppermute | solution.py:491
  147.8 21.3 %collective-permute-start.15 = (bf16[64,2048]{1,0:T(8,128)(2,1)S(1)}, bf16[64,2048]{1,0:T(8,128)(2,1)S(1)}, u32[]{:S(2)}, u32[]{:S(2)}) collective-permute-start(bf16[64,2048]{1,0:T(8,128)(2,1)S(1)} %shard_map.98), channel_id=1, source_target_pairs={{0,1},{1,2},{2,3},{3,0},{4,5},{5,6},{6,7},{7,4},{8,9},{9,10},{10,1... | collective-permute-start | bytes 786440 | tf_op jit(solution)/shard_map/ppermute | solution.py:491
  148.2 20.9 %collective-permute-start.16 = (bf16[64,2048]{1,0:T(8,128)(2,1)S(1)}, bf16[64,2048]{1,0:T(8,128)(2,1)S(1)}, u32[]{:S(2)}, u32[]{:S(2)}) collective-permute-start(bf16[64,2048]{1,0:T(8,128)(2,1)S(1)} %shard_map.99), channel_id=1, source_target_pairs={{0,3},{1,0},{2,1},{3,2},{4,7},{5,4},{6,5},{7,6},{8,11},{9,8},{10,9... | collective-permute-start | bytes 786440 | tf_op jit(solution)/shard_map/ppermute | solution.py:491
  172.0 5.3 %collective-permute-start.17 = (f32[4,1024]{1,0:T(4,128)S(1)}, f32[4,1024]{1,0:T(4,128)S(1)}, u32[]{:S(2)}, u32[]{:S(2)}) collective-permute-start(f32[4,1024]{1,0:T(4,128)S(1)} %get-tuple-element.39), channel_id=1, source_target_pairs={{0,8},{1,9},{2,10},{3,11},{4,12},{5,13},{6,14},{7,15},{8,0},{9,1},... | collective-permute-start | bytes 49160 | tf_op jit(solution)/shard_map/ppermute | solution.py:491
  192.3 9.6 %collective-permute-start.21 = (bf16[64,2048]{1,0:T(8,128)(2,1)S(1)}, bf16[64,2048]{1,0:T(8,128)(2,1)S(1)}, u32[]{:S(2)}, u32[]{:S(2)}) collective-permute-start(bf16[64,2048]{1,0:T(8,128)(2,1)S(1)} %get-tuple-element.51), channel_id=1, source_target_pairs={{0,3},{1,0},{2,1},{3,2},{4,7},{5,4},{6,5},{7,6},{8,11},{9,8},{10,9... | collective-permute-start | bytes 786440 | tf_op jit(solution)/shard_map/ppermute | solution.py:491
  194.4 8.8 %collective-permute-start.18 = (bf16[64,2048]{1,0:T(8,128)(2,1)S(1)}, bf16[64,2048]{1,0:T(8,128)(2,1)S(1)}, u32[]{:S(2)}, u32[]{:S(2)}) collective-permute-start(bf16[64,2048]{1,0:T(8,128)(2,1)S(1)} %get-tuple-element.48), channel_id=1, source_target_pairs={{0,1},{1,2},{2,3},{3,0},{4,5},{5,6},{6,7},{7,4},{8,9},{9,10},{10,1... | collective-permute-start | bytes 786440 | tf_op jit(solution)/shard_map/ppermute | solution.py:491
  198.6 13.7 %collective-permute-start.23 = (bf16[128,2048]{1,0:T(8,128)(2,1)S(1)}, bf16[128,2048]{1,0:T(8,128)(2,1)S(1)}, u32[]{:S(2)}, u32[]{:S(2)}) collective-permute-start(bf16[128,2048]{1,0:T(8,128)(2,1)S(1)} %get-tuple-element.52), channel_id=1, source_target_pairs={{0,3},{1,0},{2,1},{3,2},{4,7},{5,4},{6,5},{7,6},{8,11},{9,8},{10,9... | collective-permute-start | bytes 1572872 | tf_op jit(solution)/shard_map/ppermute | solution.py:491
  202.0 12.7 %collective-permute-start.22 = (bf16[128,2048]{1,0:T(8,128)(2,1)S(1)}, bf16[128,2048]{1,0:T(8,128)(2,1)S(1)}, u32[]{:S(2)}, u32[]{:S(2)}) collective-permute-start(bf16[128,2048]{1,0:T(8,128)(2,1)S(1)} %shard_map.110), channel_id=1, source_target_pairs={{0,4},{1,5},{2,6},{3,7},{4,0},{5,1},{6,2},{7,3},{8,12},{9,13},{10,... | collective-permute-start | bytes 1572872 | tf_op jit(solution)/shard_map/ppermute | solution.py:491
  203.2 16.1 %collective-permute-start.19 = (bf16[128,2048]{1,0:T(8,128)(2,1)S(1)}, bf16[128,2048]{1,0:T(8,128)(2,1)S(1)}, u32[]{:S(2)}, u32[]{:S(2)}) collective-permute-start(bf16[128,2048]{1,0:T(8,128)(2,1)S(1)} %shard_map.108), channel_id=1, source_target_pairs={{0,1},{1,2},{2,3},{3,0},{4,5},{5,6},{6,7},{7,4},{8,9},{9,10},{10,1... | collective-permute-start | bytes 1572872 | tf_op jit(solution)/shard_map/ppermute | solution.py:491
  207.5 20.5 %collective-permute-start.25 = (bf16[128,2048]{1,0:T(8,128)(2,1)S(1)}, bf16[128,2048]{1,0:T(8,128)(2,1)S(1)}, u32[]{:S(2)}, u32[]{:S(2)}) collective-permute-start(bf16[128,2048]{1,0:T(8,128)(2,1)S(1)} %get-tuple-element.53), channel_id=1, source_target_pairs={{0,1},{1,2},{2,3},{3,0},{4,5},{5,6},{6,7},{7,4},{8,9},{9,10},{10,1... | collective-permute-start | bytes 1572872 | tf_op jit(solution)/shard_map/ppermute | solution.py:491
  214.9 13.2 %collective-permute-start.24 = (bf16[128,2048]{1,0:T(8,128)(2,1)S(1)}, bf16[128,2048]{1,0:T(8,128)(2,1)S(1)}, u32[]{:S(2)}, u32[]{:S(2)}) collective-permute-start(bf16[128,2048]{1,0:T(8,128)(2,1)S(1)} %shard_map.111), channel_id=1, source_target_pairs={{0,3},{1,0},{2,1},{3,2},{4,7},{5,4},{6,5},{7,6},{8,11},{9,8},{10,9... | collective-permute-start | bytes 1572872 | tf_op jit(solution)/shard_map/ppermute | solution.py:491
  219.4 9.3 %collective-permute-start.20 = (bf16[128,2048]{1,0:T(8,128)(2,1)S(1)}, bf16[128,2048]{1,0:T(8,128)(2,1)S(1)}, u32[]{:S(2)}, u32[]{:S(2)}) collective-permute-start(bf16[128,2048]{1,0:T(8,128)(2,1)S(1)} %shard_map.109), channel_id=1, source_target_pairs={{0,4},{1,5},{2,6},{3,7},{4,0},{5,1},{6,2},{7,3},{8,12},{9,13},{10,... | collective-permute-start | bytes 1572872 | tf_op jit(solution)/shard_map/ppermute | solution.py:491
